TPU v7x, 512 devices: a whole 4x8x8 slice. The times are simulated.
512 devices in a mesh: expert: 128 (over z, y, core), dp: 4 (over x).
Axes of the slice: x: 4, y: 8, z: 8, core: 2. Of those that a mesh axis runs over, the one named last changes fastest.
Arguments:
- hidden_in: bfloat16 [4, 16384, 2048], P('dp', 'expert'), may hold values from -6 to 6
- out_grad: bfloat16 [4, 16384, 2048], P('dp', 'expert'), may hold values from -6 to 6
- routes: int32 [4, 16384, 2], P('dp', 'expert'), may hold values from 0 to 127, all different within a row; in each aligned block of 128 rows (0 to 127, 128 to 255, ..., all dimensions but the last counted through in order) at most 3 rows name the same one
- gate_num: int32 [4, 16384, 2], P('dp', 'expert'), may hold values from 64 to 1023
- doc_lengths: int32 [4, 32], P('dp'), may hold values from 1 to 8192, 16384 in all within a row
- w_gate: bfloat16 [128, 768, 2048], P('expert', 'dp'), may hold values from -0.125 to 0.125
- w_up: bfloat16 [128, 768, 2048], P('expert', 'dp'), may hold values from -0.125 to 0.125
- w_down: bfloat16 [128, 768, 2048], P('expert', 'dp'), may hold values from -0.21875 to 0.21875
- a_gate: bfloat16 [128, 2048, 16], P('expert'), may hold values from -0.125 to 0.125
- b_gate: bfloat16 [128, 16, 768], P('expert'), may hold values from -0.59765625 to 0.59765625
- a_up: bfloat16 [128, 2048, 16], P('expert'), may hold values from -0.125 to 0.125
- b_up: bfloat16 [128, 16, 768], P('expert'), may hold values from -0.59765625 to 0.59765625
- a_down: bfloat16 [128, 768, 16], P('expert'), may hold values from -0.21875 to 0.21875
- b_down: bfloat16 [128, 16, 2048], P('expert'), may hold values from -0.59765625 to 0.59765625
Outputs:
- input_grad: bfloat16 [4, 16384, 2048], P('dp', 'expert')
- grad_a_gate: float32 [128, 2048, 16], P('expert', 'dp')
- grad_b_gate: float32 [128, 16, 768], P('expert', None, 'dp')
- grad_a_up: float32 [128, 2048, 16], P('expert', 'dp')
- grad_b_up: float32 [128, 16, 768], P('expert', None, 'dp')
- grad_a_down: float32 [128, 768, 16], P('expert', 'dp')
- grad_b_down: float32 [128, 16, 2048], P('expert', None, 'dp')
Inputs may be any that keep to these rules, and one draw needn't show every extreme that they name: `routes`: each row names 2 different experts; the rows of one device name one expert 3 times at most. `doc_lengths`: each row sums to 16384.
All inputs are finite; a program needn't handle non-finite values.
Results may differ from a plain program's by a relative error of at most 0.0074.
Values may be sent and summed in bfloat16 or wider, within the bound.
No kernel may reach another device: no remote copies, remote signals or barrier semaphores. Data moves between devices by JAX's collectives and lax.ppermute only.
A program may use at most 64 MiB of HBM per device.

v0:
```python
import jax
import jax.numpy as jnp
from jax import lax
from jax.experimental import pallas as pl
from jax.experimental.pallas import tpu as pltpu
from jax.sharding import PartitionSpec as P


SCALE = 2.0
F32 = jnp.float32
BF16 = jnp.bfloat16
LANES = 128

NN = (((1,), (0,)), ((), ()))
NT = (((1,), (1,)), ((), ()))
TN = (((0,), (0,)), ((), ()))


def dot(left, right, dims=NN):
    return lax.dot_general(left, right, dims, preferred_element_type=F32)


def vmem():
    return pl.BlockSpec(memory_space=pltpu.VMEM)


def in_hbm(arrays):
    return [pltpu.with_memory_space_constraint(a, pltpu.HBM) for a in arrays]


def smem():
    return pl.BlockSpec(memory_space=pltpu.SMEM)


def anyspace():
    return pl.BlockSpec(memory_space=pl.ANY)


def call(body, ins, in_specs, outs, out_specs, scratch, flops, nbytes, mib):
    return pl.pallas_call(
        body,
        out_shape=[space(s, d) for s, d, space in outs],
        in_specs=in_specs,
        out_specs=out_specs,
        scratch_shapes=scratch,
        compiler_params=pltpu.CompilerParams(vmem_limit_bytes=mib * 1024 * 1024),
        cost_estimate=pl.CostEstimate(flops=flops, bytes_accessed=nbytes, transcendentals=0),
    )(*ins)


def pack_blocks(wide, stage, out_ref, sems, pitch):
    blocks, depth, _ = stage.shape

    def copy_of(i):
        some = pl.ds(i * 8, 8)
        return pltpu.make_async_copy(stage.at[some], out_ref.at[some], sems.at[i])

    @pl.loop(0, blocks // 8)
    def _(i):
        for e in range(8):
            at = pl.multiple_of(i * 8 * pitch, 8) + e * pitch
            stage[i * 8 + e] = wide[pl.ds(at, depth), :].astype(BF16)
        copy_of(i).start()

    @pl.loop(0, blocks // 8)
    def _(i):
        copy_of(i).wait()


def unpack_blocks(in_ref, wide, pitch):
    blocks, depth, _ = in_ref.shape

    @pl.loop(0, blocks // 8)
    def _(i):
        for e in range(8):
            at = pl.multiple_of(i * 8 * pitch, 8) + e * pitch
            wide[pl.ds(at, depth), :] = in_ref[i * 8 + e].astype(F32)


def choice_masks(routes_ref, experts, tokens):
    expert_id = lax.broadcasted_iota(jnp.int32, (experts, tokens), 0)
    first = routes_ref[0:1, :] == expert_id
    second = routes_ref[1:2, :] == expert_id
    either = first | second
    earlier = lax.broadcasted_iota(jnp.int32, (tokens, tokens), 0) < lax.broadcasted_iota(
        jnp.int32, (tokens, tokens), 1
    )
    rank = dot(jnp.where(either, 1.0, 0.0).astype(BF16), jnp.where(earlier, 1.0, 0.0).astype(BF16))
    return first, second, either, rank


def dispatch_body(slots, group_tokens, doc_count):
    def body(routes_ref, nums_ref, lengths_ref, start_ref, x_hbm, g_hbm, send_ref, wide, stage, x_ref, g_ref, lsems, sems):
        loads = [
            pltpu.make_async_copy(x_hbm, x_ref, lsems.at[0]),
            pltpu.make_async_copy(g_hbm, g_ref, lsems.at[1]),
        ]
        for load in loads:
            load.start()
        experts = stage.shape[0]
        tokens, features = x_ref.shape
        tiles = features // LANES
        depth = 2 * slots * tiles
        pitch = depth + 4
        first, second, either, rank = choice_masks(routes_ref, experts, tokens)
        position = start_ref[0] + lax.broadcasted_iota(jnp.int32, (1, tokens), 1)
        own = jnp.zeros((1, tokens), jnp.int32)
        begin = jnp.int32(0)
        for j in range(doc_count):
            length = lengths_ref[0, j]
            own = jnp.where((position >= begin) & (position < begin + length), length, own)
            begin = begin + length
        weight = jnp.sqrt(jnp.float32(group_tokens) / (doc_count * own).astype(F32))
        factor = nums_ref[...].astype(F32) / 1024.0 * weight
        factors = jnp.where(first, factor[0:1, :], 0.0) + jnp.where(second, factor[1:2, :], 0.0)
        picks, scales = [], []
        for c in range(slots):
            chosen = jnp.where(either & (rank == float(c)), 1.0, 0.0)
            scales.append(jnp.sum(chosen * factors, axis=1, keepdims=True))
            picks.append(chosen.astype(BF16))
        pick = jnp.concatenate(picks, axis=0)
        scale = jnp.concatenate(scales, axis=0)
        for load in loads:
            load.wait()
        chunk = 2 * LANES
        for j in range(features // chunk):
            cols = slice(j * chunk, (j + 1) * chunk)
            both = (dot(pick, x_ref[:, cols]), scale * dot(pick, g_ref[:, cols]))
            for side in range(2):
                for c in range(slots):
                    for h in range(2):
                        wide[pl.ds((side * slots + c) * tiles + 2 * j + h, experts, stride=pitch), :] = both[
                            side
                        ][c * experts : (c + 1) * experts, h * LANES : (h + 1) * LANES]
        pack_blocks(wide, stage, send_ref, sems, pitch)

    return body


def expert_body(slots, places):
    def body(recv_ref, *refs):
        weight_refs, refs = refs[: len(places)], refs[len(places) :]
        left_ref, bdown_ref, right_ref, send_ref, rows_out, acts_out, lows_ref = refs[:7]
        wide, more, x, s, gates, ups, acts, weights, backs, stage, sems, osems, ssems = refs[7:]
        peers = recv_ref.shape[0]
        features = x.shape[1]
        hidden = acts.shape[2]
        tiles = features // LANES
        depth = slots * tiles
        pitch = depth + 4
        narrow = tiles + 4
        copies = [[], [], []]
        for k, (ref, (m, at, size)) in enumerate(zip(weight_refs, places)):
            copies[m].append(
                pltpu.make_async_copy(ref, weights.at[m, pl.ds(at, size)], sems.at[k])
            )
        for m in range(3):
            for copy in copies[m]:
                copy.start()

        for e in range(peers):
            wide[e * pitch : e * pitch + depth, :] = recv_ref[e, :depth, :].astype(F32)
        for j in range(tiles):
            for c in range(slots):
                x[c * peers : (c + 1) * peers, j * LANES : (j + 1) * LANES] = wide[
                    pl.ds(c * tiles + j, peers, stride=pitch), :
                ].astype(BF16)

        chunk = 256
        chunks = [slice(n * chunk, (n + 1) * chunk) for n in range(hidden // chunk)]
        for copy in copies[0]:
            copy.wait()
        lows = dot(x[...], left_ref[...], NT)
        gate_low = lows[:, :16].astype(BF16)
        up_low = lows[:, 16:].astype(BF16)
        lows_ref[0] = gate_low
        lows_ref[1] = up_low

        @pl.loop(0, slots)
        def _(c):
            cols = pl.ds(pl.multiple_of(c * chunk, chunk), chunk)
            gates[:, cols] = dot(x[...], weights[0, cols, :], NT) + SCALE * dot(
                lows_ref[0], right_ref[0, :, cols]
            )
            from_row = pl.multiple_of(depth + c * tiles, tiles)
            for e in range(peers):
                more[e * narrow : e * narrow + tiles, :] = recv_ref[e, pl.ds(from_row, tiles), :].astype(F32)
            for j in range(tiles):
                s[pl.ds(pl.multiple_of(c * peers, peers), peers), j * LANES : (j + 1) * LANES] = more[
                    pl.ds(j, peers, stride=narrow), :
                ].astype(BF16)

        for copy in copies[1]:
            copy.wait()
        out_copies = [
            pltpu.make_async_copy(x, rows_out.at[0], osems.at[0]),
            pltpu.make_async_copy(s, rows_out.at[1], osems.at[1]),
        ]
        for copy in out_copies:
            copy.start()
        for cols in chunks:
            ups[:, cols] = dot(x[...], weights[1, cols, :], NT) + SCALE * dot(
                lows_ref[1], right_ref[1, :, cols]
            )
        grad_low = dot(s[...], bdown_ref[...], NT).astype(BF16)
        lows_ref[2] = grad_low
        for copy in copies[2]:
            copy.wait()
        for cols in chunks:
            gate, up = gates[:, cols], ups[:, cols]
            back = dot(s[...], weights[2, cols, :], NT) + SCALE * dot(
                lows_ref[2], right_ref[2, :, cols]
            )
            sigma = jax.nn.sigmoid(gate)
            active = gate * sigma
            acts[0, :, cols] = (active * up).astype(BF16)
            acts[1, :, cols] = (back * up * sigma * (1.0 + gate * (1.0 - sigma))).astype(BF16)
            acts[2, :, cols] = (back * active).astype(BF16)
        out_copies.append(pltpu.make_async_copy(acts, acts_out, osems.at[2]))
        out_copies[2].start()
        gate_back = dot(acts[1], right_ref[0], NT).astype(BF16)
        up_back = dot(acts[2], right_ref[1], NT).astype(BF16)
        backs[:, :16] = gate_back
        backs[:, 16:] = up_back
        for j in range(features // chunk):
            cols = slice(j * chunk, (j + 1) * chunk)
            part = (
                dot(acts[1], weights[0, :, cols])
                + dot(acts[2], weights[1, :, cols])
                + SCALE * dot(backs[...], left_ref[:, cols])
            )
            for c in range(slots):
                for h in range(chunk // LANES):
                    wide[
                        pl.ds(c * tiles + j * (chunk // LANES) + h, peers, stride=pitch), :
                    ] = part[c * peers : (c + 1) * peers, h * LANES : (h + 1) * LANES]

        lows_ref[3] = gate_back
        lows_ref[4] = up_back
        pack_blocks(wide, stage, send_ref, ssems, pitch)
        for copy in out_copies:
            copy.wait()

    return body


def adapter_body(slots, share, width):
    def body(me_ref, routes_ref, rows_ref, acts_ref, lows_ref, right_ref, *refs):
        shares = refs[:4]
        back_ref = refs[4]
        big, small = refs[5:]
        tokens = routes_ref.shape[1]
        experts = tokens
        down_low = dot(acts_ref[0], right_ref[2], NT).astype(BF16)
        big[0] = SCALE * dot(lows_ref[3], rows_ref[0], TN)
        big[1] = SCALE * dot(lows_ref[4], rows_ref[0], TN)
        big[2] = SCALE * dot(down_low, rows_ref[1], TN)
        small[0] = SCALE * dot(lows_ref[0], acts_ref[1], TN)
        small[1] = SCALE * dot(lows_ref[1], acts_ref[2], TN)
        small[2] = SCALE * dot(lows_ref[2], acts_ref[0], TN)
        for k in range(4):
            at = pl.multiple_of(((me_ref[0] + k) % 4) * width, width)
            for m in range(3):
                shares[k][m, :, 0:width] = big[m, :, pl.ds(at, width)]
                shares[k][m, :, width : width + share] = small[m, :, k * share : (k + 1) * share]
                shares[k][m, :, width + share :] = jnp.zeros((16, 256 - share), F32)
        _, _, either, rank = choice_masks(routes_ref, experts, tokens)
        for c in range(slots):
            back_ref[:, c * experts : (c + 1) * experts] = jnp.where(
                either & (rank == float(c)), 1.0, 0.0
            ).T.astype(BF16)

    return body


def total_body(share, width):
    def body(a_ref, b_ref, c_ref, d_ref, *outs):
        for m in range(3):
            total = a_ref[m] + b_ref[m] + c_ref[m] + d_ref[m]
            outs[m][...] = total[:, :width]
            outs[3 + m][...] = total[:, width : width + share]

    return body


def combine_body(slots):
    def body(back_ref, pick_ref, out_ref, wide, rows):
        experts = back_ref.shape[0]
        _, features = out_ref.shape
        tiles = features // LANES
        depth = slots * tiles

        unpack_blocks(back_ref, wide, depth + 4)
        for j in range(tiles):
            for c in range(slots):
                rows[c * experts : (c + 1) * experts, j * LANES : (j + 1) * LANES] = wide[
                    pl.ds(c * tiles + j, experts, stride=depth + 4), :
                ].astype(BF16)
        for j in range(0, features, 256):
            out_ref[:, j : j + 256] = dot(pick_ref[...], rows[:, j : j + 256]).astype(BF16)

    return body


def layer(
    hidden_in,
    out_grad,
    routes,
    gate_num,
    doc_lengths,
    w_gate,
    w_up,
    w_down,
    a_gate,
    b_gate,
    a_up,
    b_up,
    a_down,
    b_down,
):
    tokens, features = hidden_in.shape[1:]
    groups = lax.axis_size("expert")
    shards = lax.axis_size("dp")
    share = w_gate.shape[1]
    hidden = share * shards
    rank_dim = a_gate.shape[2]
    width = features // shards
    slots = min(tokens, max(2, 3 * tokens * routes.shape[2] // (2 * groups)))
    tiles = features // LANES
    depth = slots * tiles
    rows = slots * groups
    me = lax.axis_index("dp")
    routes_t = routes[0].T
    start = (lax.axis_index("expert") * tokens).astype(jnp.int32).reshape(1)
    x, g = hidden_in[0], out_grad[0]

    up_ring = [(i, (i + 1) % shards) for i in range(shards)]
    down_ring = [(i, (i - 1) % shards) for i in range(shards)]
    early = lax.ppermute(w_gate[0], "dp", up_ring)
    (send,) = call(
        dispatch_body(slots, tokens * groups, doc_lengths.shape[1]),
        (*in_hbm((routes_t, gate_num[0].T, doc_lengths)), start, *in_hbm((x, g))),
        [vmem(), vmem(), smem(), smem(), anyspace(), anyspace()],
        [((groups, 2 * depth, LANES), BF16, pltpu.HBM)],
        [anyspace()],
        [
            pltpu.VMEM((groups * (2 * depth + 4), LANES), F32),
            pltpu.VMEM((groups, 2 * depth, LANES), BF16),
            pltpu.VMEM((tokens, features), BF16),
            pltpu.VMEM((tokens, features), BF16),
            pltpu.SemaphoreType.DMA((2,)),
            pltpu.SemaphoreType.DMA((groups // 8,)),
        ],
        4 * rows * tokens * features,
        4 * rows * features,
        16,
    )
    send, gate_late, w_up_late, w_down_late = lax.optimization_barrier(
        (send, w_gate[0], w_up[0], w_down[0])
    )
    own = (w_gate[0], w_up[0], w_down[0])
    late = (gate_late, w_up_late, w_down_late)
    recv = lax.all_to_all(send, "expert", split_axis=0, concat_axis=0, tiled=True)

    half = share // 2
    behind = [early] + [lax.ppermute(w, "dp", up_ring) for w in late[1:]]
    ahead = [lax.ppermute(w, "dp", down_ring) for w in late]
    far = [[lax.ppermute(behind[0], "dp", up_ring)]] + [
        [lax.ppermute(behind[m][:half], "dp", up_ring), lax.ppermute(ahead[m][half:], "dp", down_ring)]
        for m in (1, 2)
    ]
    weights, places = [], []
    for m in range(3):
        weights += [own[m], ahead[m], behind[m], *far[m]]
        places += [(m, 0, share), (m, share, share), (m, 3 * share, share)]
        size = share // len(far[m])
        places += [(m, 2 * share + k * size, size) for k in range(len(far[m]))]

    left = jnp.concatenate([a_gate[0].T, a_up[0].T], axis=0)
    right = jnp.stack([b_gate[0], b_up[0], a_down[0].T])
    right = lax.dynamic_slice_in_dim(
        jnp.concatenate([right, right], axis=2), me * share, hidden, axis=2
    )
    send_back, row_blocks, acts, lows = call(
        expert_body(slots, places),
        (recv, *in_hbm((*weights, left, b_down[0], right))),
        [vmem()] + [anyspace()] * len(weights) + [vmem()] * 3,
        [
            ((groups, depth, LANES), BF16, pltpu.HBM),
            ((2, rows, features), BF16, pltpu.HBM),
            ((3, rows, hidden), BF16, pltpu.HBM),
            ((5, rows, rank_dim), BF16, pltpu.HBM),
        ],
        [anyspace(), anyspace(), anyspace(), vmem()],
        [
            pltpu.VMEM((groups * (depth + 4), LANES), F32),
            pltpu.VMEM((groups * (tiles + 4), LANES), F32),
            pltpu.VMEM((rows, features), BF16),
            pltpu.VMEM((rows, features), BF16),
            pltpu.VMEM((rows, hidden), F32),
            pltpu.VMEM((rows, hidden), F32),
            pltpu.VMEM((3, rows, hidden), BF16),
            pltpu.VMEM((3, hidden, features), BF16),
            pltpu.VMEM((rows, 2 * rank_dim), BF16),
            pltpu.VMEM((groups, depth, LANES), BF16),
            pltpu.SemaphoreType.DMA((len(places),)),
            pltpu.SemaphoreType.DMA((3,)),
            pltpu.SemaphoreType.DMA((groups // 8,)),
        ],
        10 * rows * hidden * features,
        6 * hidden * features + 6 * rows * features,
        40,
    )
    back = lax.all_to_all(send_back, "expert", split_axis=0, concat_axis=0, tiled=True)

    *shares, pick = call(
        adapter_body(slots, share, width),
        (me.astype(jnp.int32).reshape(1), *in_hbm((routes_t, row_blocks, acts, lows, right))),
        [smem()] + [vmem()] * 5,
        [((3, rank_dim, width + 256), F32, pltpu.HBM)] * 4 + [((tokens, rows), BF16, pltpu.VMEM)],
        [vmem()] * 5,
        [pltpu.VMEM((3, rank_dim, features), F32), pltpu.VMEM((3, rank_dim, hidden), F32)],
        12 * rows * features * rank_dim,
        4 * rows * features,
        12,
    )
    parts = [shares[0]] + [
        lax.ppermute(shares[k], "dp", [(i, (i + k) % shards) for i in range(shards)])
        for k in range(1, shards)
    ]
    big_gate, big_up, big_down, small_gate, small_up, small_down = call(
        total_body(share, width),
        parts,
        [vmem()] * 4,
        [((rank_dim, width), F32, pltpu.HBM)] * 3 + [((rank_dim, share), F32, pltpu.HBM)] * 3,
        [vmem()] * 6,
        [],
        9 * rank_dim * (width + share),
        60 * rank_dim * (width + share),
        4,
    )
    (input_grad,) = call(
        combine_body(slots),
        (back, pltpu.with_memory_space_constraint(pick, pltpu.VMEM)),
        [vmem()] * 2,
        [((tokens, features), BF16, pltpu.HBM)],
        [vmem()],
        [pltpu.VMEM((groups * (depth + 4), LANES), F32), pltpu.VMEM((rows, features), BF16)],
        2 * rows * tokens * features,
        2 * rows * features,
        12,
    )
    return (
        input_grad[None],
        big_gate.T[None],
        small_gate[None],
        big_up.T[None],
        small_up[None],
        small_down.T[None],
        big_down[None],
    )


def solution(mesh):
    return jax.shard_map(
        layer,
        mesh=mesh,
        in_specs=(
            P("dp", "expert", None),
            P("dp", "expert", None),
            P("dp", "expert", None),
            P("dp", "expert", None),
            P("dp", None),
            P("expert", "dp", None),
            P("expert", "dp", None),
            P("expert", "dp", None),
            P("expert", None, None),
            P("expert", None, None),
            P("expert", None, None),
            P("expert", None, None),
            P("expert", None, None),
            P("expert", None, None),
        ),
        out_specs=(
            P("dp", "expert", None),
            P("expert", "dp", None),
            P("expert", None, "dp"),
            P("expert", "dp", None),
            P("expert", None, "dp"),
            P("expert", "dp", None),
            P("expert", None, "dp"),
        ),
        check_vma=False,
    )
```

profile of v0, /device:TPU:8, one launch (start us, length us, event | category | flops | bytes accessed | tf_op | source)
XLA Modules:
  0.0 186.9 jit_solution(11284992963813152880)
XLA Ops:
  0.6 4.8 %shard_map.189 = bf16[128,96,128]{2,1,0:T(8,128)(2,1)} custom-call(s32[2,128]{1,0:T(2,128)} %bitcast.44, s32[2,128]{1,0:T(2,128)} %bitcast.46, s32[1,32]{1,0:T(1,128)} %lengths_ref.1, s32[1]{0:T(128)} %bitcast.4.start_ref, bf16[128,2048]{1,0:T(8,128)(2,1)} %bitcast.38, bf16[128,2048]{1,0:T(8,128)(2,1)} %bitcast.39), custom_call_target="tpu_custom_call" | custom-call | flops 402653184 | bytes 3145728 | tf_op jit(solution)/shard_map/pallas_call | solution.py:40
  5.5 17.4 %all-to-all-start = ((bf16[128,96,128]{2,1,0:T(8,128)(2,1)}), bf16[128,96,128]{2,1,0:T(8,128)(2,1)S(1)}, u32[]{:S(2)}, u32[]{:S(2)}) async-start(bf16[128,96,128]{2,1,0:T(8,128)(2,1)} %shard_map.189), calls=%async_computation | async-start | bytes 6291456 | tf_op jit(solution)/shard_map/all_to_all | solution.py:363
  22.8 3.4 %collective-permute-start.1 = (bf16[192,2048]{1,0:T(8,128)(2,1)}, bf16[192,2048]{1,0:T(8,128)(2,1)}, u32[]{:S(2)}, u32[]{:S(2)}) collective-permute-start(bf16[192,2048]{1,0:T(8,128)(2,1)} %bitcast.47), channel_id=1, source_target_pairs={{0,1},{1,2},{2,3},{3,0},{4,5},{5,6},{6,7},{7,4},{8,9},{9,10},{10,1... | collective-permute-start | bytes 2359304 | tf_op jit(solution)/shard_map/ppermute | solution.py:339
  26.3 3.4 %collective-permute-start.4 = (bf16[192,2048]{1,0:T(8,128)(2,1)}, bf16[192,2048]{1,0:T(8,128)(2,1)S(1)}, u32[]{:S(2)}, u32[]{:S(2)}) collective-permute-start(bf16[192,2048]{1,0:T(8,128)(2,1)} %bitcast.50), channel_id=1, source_target_pairs={{0,1},{1,2},{2,3},{3,0},{4,5},{5,6},{6,7},{7,4},{8,9},{9,10},{10,1... | collective-permute-start | bytes 2359304 | tf_op jit(solution)/shard_map/ppermute | solution.py:366
  29.7 3.7 %collective-permute-start.3 = (bf16[192,2048]{1,0:T(8,128)(2,1)}, bf16[192,2048]{1,0:T(8,128)(2,1)S(1)}, u32[]{:S(2)}, u32[]{:S(2)}) collective-permute-start(bf16[192,2048]{1,0:T(8,128)(2,1)} %bitcast.51), channel_id=1, source_target_pairs={{0,3},{1,0},{2,1},{3,2},{4,7},{5,4},{6,5},{7,6},{8,11},{9,8},{10,9... | collective-permute-start | bytes 2359304 | tf_op jit(solution)/shard_map/ppermute | solution.py:367
  33.3 2.2 %collective-permute-start.8 = (bf16[192,2048]{1,0:T(8,128)(2,1)}, bf16[192,2048]{1,0:T(8,128)(2,1)S(1)}, u32[]{:S(2)}, u32[]{:S(2)}) collective-permute-start(bf16[192,2048]{1,0:T(8,128)(2,1)} %bitcast.53), channel_id=1, source_target_pairs={{0,1},{1,2},{2,3},{3,0},{4,5},{5,6},{6,7},{7,4},{8,9},{9,10},{10,1... | collective-permute-start | bytes 2359304 | tf_op jit(solution)/shard_map/ppermute | solution.py:366
  35.5 4.9 %collective-permute-start.7 = (bf16[192,2048]{1,0:T(8,128)(2,1)}, bf16[192,2048]{1,0:T(8,128)(2,1)S(1)}, u32[]{:S(2)}, u32[]{:S(2)}) collective-permute-start(bf16[192,2048]{1,0:T(8,128)(2,1)} %bitcast.54), channel_id=1, source_target_pairs={{0,3},{1,0},{2,1},{3,2},{4,7},{5,4},{6,5},{7,6},{8,11},{9,8},{10,9... | collective-permute-start | bytes 2359304 | tf_op jit(solution)/shard_map/ppermute | solution.py:367
  40.4 6.3 %collective-permute-done.1.refs_2_ = bf16[192,2048]{1,0:T(8,128)(2,1)} collective-permute-done((bf16[192,2048]{1,0:T(8,128)(2,1)}, bf16[192,2048]{1,0:T(8,128)(2,1)}, u32[]{:S(2)}, u32[]{:S(2)}) %collective-permute-start.1) | collective-permute-done | bytes 786464 | tf_op jit(solution)/shard_map/ppermute | solution.py:339
  46.7 3.4 %collective-permute-start = (bf16[192,2048]{1,0:T(8,128)(2,1)}, bf16[192,2048]{1,0:T(8,128)(2,1)}, u32[]{:S(2)}, u32[]{:S(2)}) collective-permute-start(bf16[192,2048]{1,0:T(8,128)(2,1)} %bitcast.48), channel_id=1, source_target_pairs={{0,3},{1,0},{2,1},{3,2},{4,7},{5,4},{6,5},{7,6},{8,11},{9,8},{10,9... | collective-permute-start | bytes 2359304 | tf_op jit(solution)/shard_map/ppermute | solution.py:367
  50.1 13.3 %collective-permute-done.4.refs_6_ = bf16[192,2048]{1,0:T(8,128)(2,1)S(1)} collective-permute-done((bf16[192,2048]{1,0:T(8,128)(2,1)}, bf16[192,2048]{1,0:T(8,128)(2,1)S(1)}, u32[]{:S(2)}, u32[]{:S(2)}) %collective-permute-start.4) | collective-permute-done | bytes 786464 | tf_op jit(solution)/shard_map/ppermute | solution.py:366
  63.4 0.0 copy-start.1
  63.4 2.2 %collective-permute-start.2 = (bf16[192,2048]{1,0:T(8,128)(2,1)}, bf16[192,2048]{1,0:T(8,128)(2,1)}, u32[]{:S(2)}, u32[]{:S(2)}) collective-permute-start(bf16[192,2048]{1,0:T(8,128)(2,1)} %collective-permute-done.1.refs_2_), channel_id=1, source_target_pairs={{0,1},{1,2},{2,3},{3,0},{4,5},{5,6},{6,7},{7,4},{8,9},{9,10},{10,1... | collective-permute-start | bytes 2359304 | tf_op jit(solution)/shard_map/ppermute | solution.py:368
  65.6 0.0 collective-permute-done.3.refs_5_
  65.7 0.0 copy-start.2
  65.7 3.4 %collective-permute-start.5 = (bf16[96,2048]{1,0:T(8,128)(2,1)S(1)}, bf16[96,2048]{1,0:T(8,128)(2,1)}, u32[]{:S(2)}, u32[]{:S(2)}) collective-permute-start(bf16[96,2048]{1,0:T(8,128)(2,1)S(1)} %slice.16), channel_id=1, source_target_pairs={{0,1},{1,2},{2,3},{3,0},{4,5},{5,6},{6,7},{7,4},{8,9},{9,10},{10,1... | collective-permute-start | bytes 1179656 | tf_op jit(solution)/shard_map/ppermute | solution.py:369
  69.1 0.0 copy-done.1
  69.1 0.8 slice.17
  69.9 0.0 copy-done.2
  69.9 10.4 %collective-permute-done.8.refs_11_ = bf16[192,2048]{1,0:T(8,128)(2,1)S(1)} collective-permute-done((bf16[192,2048]{1,0:T(8,128)(2,1)}, bf16[192,2048]{1,0:T(8,128)(2,1)S(1)}, u32[]{:S(2)}, u32[]{:S(2)}) %collective-permute-start.8) | collective-permute-done | bytes 786464 | tf_op jit(solution)/shard_map/ppermute | solution.py:366
  80.3 0.0 copy-start.3
  80.3 3.4 %collective-permute-start.6 = (bf16[96,2048]{1,0:T(8,128)(2,1)}, bf16[96,2048]{1,0:T(8,128)(2,1)}, u32[]{:S(2)}, u32[]{:S(2)}) collective-permute-start(bf16[96,2048]{1,0:T(8,128)(2,1)} %slice.17), channel_id=1, source_target_pairs={{0,3},{1,0},{2,1},{3,2},{4,7},{5,4},{6,5},{7,6},{8,11},{9,8},{10,9... | collective-permute-start | bytes 1179656 | tf_op jit(solution)/shard_map/ppermute | solution.py:369
  83.7 0.0 copy-done.3
  83.7 0.8 slice.18
  84.5 0.0 collective-permute-done.7.refs_10_
  84.5 0.0 copy-start.4
  84.5 2.4 %collective-permute-start.9 = (bf16[96,2048]{1,0:T(8,128)(2,1)}, bf16[96,2048]{1,0:T(8,128)(2,1)}, u32[]{:S(2)}, u32[]{:S(2)}) collective-permute-start(bf16[96,2048]{1,0:T(8,128)(2,1)} %slice.18), channel_id=1, source_target_pairs={{0,1},{1,2},{2,3},{3,0},{4,5},{5,6},{6,7},{7,4},{8,9},{9,10},{10,1... | collective-permute-start | bytes 1179656 | tf_op jit(solution)/shard_map/ppermute | solution.py:369
  86.9 0.0 copy-done.4
  86.9 0.8 slice.19
  87.7 0.0 collective-permute-done.refs_1_
  87.7 4.8 %collective-permute-start.10 = (bf16[96,2048]{1,0:T(8,128)(2,1)}, bf16[96,2048]{1,0:T(8,128)(2,1)}, u32[]{:S(2)}, u32[]{:S(2)}) collective-permute-start(bf16[96,2048]{1,0:T(8,128)(2,1)} %slice.19), channel_id=1, source_target_pairs={{0,3},{1,0},{2,1},{3,2},{4,7},{5,4},{6,5},{7,6},{8,11},{9,8},{10,9... | collective-permute-start | bytes 1179656 | tf_op jit(solution)/shard_map/ppermute | solution.py:369
  92.5 1.6 fusion.2.refs_16_.right_ref
  94.1 1.5 pad_maximum_fusion.refs_14_
  95.6 10.0 %collective-permute-done.5.refs_7_ = bf16[96,2048]{1,0:T(8,128)(2,1)} collective-permute-done((bf16[96,2048]{1,0:T(8,128)(2,1)S(1)}, bf16[96,2048]{1,0:T(8,128)(2,1)}, u32[]{:S(2)}, u32[]{:S(2)}) %collective-permute-start.5) | collective-permute-done | bytes 393248 | tf_op jit(solution)/shard_map/ppermute | solution.py:369
  105.7 0.0 collective-permute-done.6.refs_8_
  105.7 7.6 %collective-permute-done.9.refs_12_ = bf16[96,2048]{1,0:T(8,128)(2,1)} collective-permute-done((bf16[96,2048]{1,0:T(8,128)(2,1)}, bf16[96,2048]{1,0:T(8,128)(2,1)}, u32[]{:S(2)}, u32[]{:S(2)}) %collective-permute-start.9) | collective-permute-done | bytes 393248 | tf_op jit(solution)/shard_map/ppermute | solution.py:369
  113.2 0.0 collective-permute-done.10.refs_13_
  113.2 0.0 collective-permute-done.2.refs_3_
  113.2 0.0 all-to-all-done.recv_ref
  113.3 15.7 %shard_map.190 = (bf16[128,48,128]{2,1,0:T(8,128)(2,1)}, bf16[2,384,2048]{2,1,0:T(8,128)(2,1)}, bf16[3,384,768]{2,1,0:T(8,128)(2,1)}, bf16[5,384,16]{2,1,0:T(8,128)(2,1)}) custom-call(bf16[128,96,128]{2,1,0:T(8,128)(2,1)S(1)} %all-to-all-done.recv_ref, bf16[192,2048]{1,0:T(8,128)(2,1)} %bitcast.49, bf16[192,2048]{1,0:T(8,128)(2,1)} %collective-permute-done.refs_1_, ...), custom_call_target="tpu_custom_call" | custom-call | flops 6039797760 | bytes 14155776 | tf_op jit(solution)/shard_map/pallas_call | solution.py:40
  128.9 13.7 %all-to-all-start.1 = ((bf16[128,48,128]{2,1,0:T(8,128)(2,1)}), bf16[128,48,128]{2,1,0:T(8,128)(2,1)S(1)}, u32[]{:S(2)}, u32[]{:S(2)}) async-start(bf16[128,48,128]{2,1,0:T(8,128)(2,1)} %get-tuple-element.30), calls=%async_computation.1 | async-start | bytes 3145728 | tf_op jit(solution)/shard_map/all_to_all | solution.py:414
  142.7 4.6 %shard_map.191 = (f32[3,16,768]{2,1,0:T(8,128)}, f32[3,16,768]{2,1,0:T(8,128)}, f32[3,16,768]{2,1,0:T(8,128)}, f32[3,16,768]{2,1,0:T(8,128)}, bf16[128,384]{1,0:T(8,128)(2,1)S(1)}) custom-call(s32[1]{0:T(128)} %bitcast.18.me_ref, s32[2,128]{1,0:T(2,128)} %bitcast.45, bf16[2,384,2048]{2,1,0:T(8,128)(2,1)} %get-tuple-element.31.rows_ref, ...), custom_call_target="tpu_custom_call" | custom-call | flops 150994944 | bytes 3145728 | tf_op jit(solution)/shard_map/pallas_call | solution.py:40
  147.3 2.2 %collective-permute-start.11 = (f32[3,16,768]{2,1,0:T(8,128)}, f32[3,16,768]{2,1,0:T(8,128)S(1)}, u32[]{:S(2)}, u32[]{:S(2)}) collective-permute-start(f32[3,16,768]{2,1,0:T(8,128)} %get-tuple-element.36), channel_id=1, source_target_pairs={{0,1},{1,2},{2,3},{3,0},{4,5},{5,6},{6,7},{7,4},{8,9},{9,10},{10,1... | collective-permute-start | bytes 442376 | tf_op jit(solution)/shard_map/ppermute | solution.py:428
  149.4 4.6 %collective-permute-start.12 = (f32[3,16,768]{2,1,0:T(8,128)}, f32[3,16,768]{2,1,0:T(8,128)S(1)}, u32[]{:S(2)}, u32[]{:S(2)}) collective-permute-start(f32[3,16,768]{2,1,0:T(8,128)} %get-tuple-element.37), channel_id=1, source_target_pairs={{0,2},{1,3},{2,0},{3,1},{4,6},{5,7},{6,4},{7,5},{8,10},{9,11},{10,... | collective-permute-start | bytes 442376 | tf_op jit(solution)/shard_map/ppermute | solution.py:428
  154.1 3.3 %collective-permute-start.13 = (f32[3,16,768]{2,1,0:T(8,128)}, f32[3,16,768]{2,1,0:T(8,128)S(1)}, u32[]{:S(2)}, u32[]{:S(2)}) collective-permute-start(f32[3,16,768]{2,1,0:T(8,128)} %get-tuple-element.38), channel_id=1, source_target_pairs={{0,3},{1,0},{2,1},{3,2},{4,7},{5,4},{6,5},{7,6},{8,11},{9,8},{10,9... | collective-permute-start | bytes 442376 | tf_op jit(solution)/shard_map/ppermute | solution.py:428
  157.4 2.2 %collective-permute-done.11.b_ref = f32[3,16,768]{2,1,0:T(8,128)S(1)} collective-permute-done((f32[3,16,768]{2,1,0:T(8,128)}, f32[3,16,768]{2,1,0:T(8,128)S(1)}, u32[]{:S(2)}, u32[]{:S(2)}) %collective-permute-start.11) | collective-permute-done | bytes 147488 | tf_op jit(solution)/shard_map/ppermute | solution.py:428
  159.6 0.0 collective-permute-done.12.c_ref
  159.6 2.5 %collective-permute-done.13.d_ref = f32[3,16,768]{2,1,0:T(8,128)S(1)} collective-permute-done((f32[3,16,768]{2,1,0:T(8,128)}, f32[3,16,768]{2,1,0:T(8,128)S(1)}, u32[]{:S(2)}, u32[]{:S(2)}) %collective-permute-start.13) | collective-permute-done | bytes 147488 | tf_op jit(solution)/shard_map/ppermute | solution.py:428
  162.1 0.0 copy-start
  162.1 0.9 copy-done
  163.0 0.7 shard_map.193
  163.7 21.6 %all-to-all-done.1.back_ref = bf16[128,48,128]{2,1,0:T(8,128)(2,1)S(1)} async-done(((bf16[128,48,128]{2,1,0:T(8,128)(2,1)}), bf16[128,48,128]{2,1,0:T(8,128)(2,1)S(1)}, u32[]{:S(2)}, u32[]{:S(2)}) %all-to-all-start.1) | async-done | bytes 1572896 | tf_op jit(solution)/shard_map/all_to_all | solution.py:414
  185.3 1.6 shard_map.192
  (1 shorter events, 0.0 us)
Async XLA Ops:
  5.5 107.8 %all-to-all-start = ((bf16[128,96,128]{2,1,0:T(8,128)(2,1)}), bf16[128,96,128]{2,1,0:T(8,128)(2,1)S(1)}, u32[]{:S(2)}, u32[]{:S(2)}) async-start(bf16[128,96,128]{2,1,0:T(8,128)(2,1)} %shard_map.189), calls=%async_computation | async-start | bytes 6291456 | tf_op jit(solution)/shard_map/all_to_all | solution.py:363
  22.8 23.8 %collective-permute-start.1 = (bf16[192,2048]{1,0:T(8,128)(2,1)}, bf16[192,2048]{1,0:T(8,128)(2,1)}, u32[]{:S(2)}, u32[]{:S(2)}) collective-permute-start(bf16[192,2048]{1,0:T(8,128)(2,1)} %bitcast.47), channel_id=1, source_target_pairs={{0,1},{1,2},{2,3},{3,0},{4,5},{5,6},{6,7},{7,4},{8,9},{9,10},{10,1... | collective-permute-start | bytes 2359304 | tf_op jit(solution)/shard_map/ppermute | solution.py:339
  26.3 37.2 %collective-permute-start.4 = (bf16[192,2048]{1,0:T(8,128)(2,1)}, bf16[192,2048]{1,0:T(8,128)(2,1)S(1)}, u32[]{:S(2)}, u32[]{:S(2)}) collective-permute-start(bf16[192,2048]{1,0:T(8,128)(2,1)} %bitcast.50), channel_id=1, source_target_pairs={{0,1},{1,2},{2,3},{3,0},{4,5},{5,6},{6,7},{7,4},{8,9},{9,10},{10,1... | collective-permute-start | bytes 2359304 | tf_op jit(solution)/shard_map/ppermute | solution.py:366
  29.7 36.0 %collective-permute-start.3 = (bf16[192,2048]{1,0:T(8,128)(2,1)}, bf16[192,2048]{1,0:T(8,128)(2,1)S(1)}, u32[]{:S(2)}, u32[]{:S(2)}) collective-permute-start(bf16[192,2048]{1,0:T(8,128)(2,1)} %bitcast.51), channel_id=1, source_target_pairs={{0,3},{1,0},{2,1},{3,2},{4,7},{5,4},{6,5},{7,6},{8,11},{9,8},{10,9... | collective-permute-start | bytes 2359304 | tf_op jit(solution)/shard_map/ppermute | solution.py:367
  33.3 47.0 %collective-permute-start.8 = (bf16[192,2048]{1,0:T(8,128)(2,1)}, bf16[192,2048]{1,0:T(8,128)(2,1)S(1)}, u32[]{:S(2)}, u32[]{:S(2)}) collective-permute-start(bf16[192,2048]{1,0:T(8,128)(2,1)} %bitcast.53), channel_id=1, source_target_pairs={{0,1},{1,2},{2,3},{3,0},{4,5},{5,6},{6,7},{7,4},{8,9},{9,10},{10,1... | collective-permute-start | bytes 2359304 | tf_op jit(solution)/shard_map/ppermute | solution.py:366
  35.5 49.0 %collective-permute-start.7 = (bf16[192,2048]{1,0:T(8,128)(2,1)}, bf16[192,2048]{1,0:T(8,128)(2,1)S(1)}, u32[]{:S(2)}, u32[]{:S(2)}) collective-permute-start(bf16[192,2048]{1,0:T(8,128)(2,1)} %bitcast.54), channel_id=1, source_target_pairs={{0,3},{1,0},{2,1},{3,2},{4,7},{5,4},{6,5},{7,6},{8,11},{9,8},{10,9... | collective-permute-start | bytes 2359304 | tf_op jit(solution)/shard_map/ppermute | solution.py:367
  46.7 41.0 %collective-permute-start = (bf16[192,2048]{1,0:T(8,128)(2,1)}, bf16[192,2048]{1,0:T(8,128)(2,1)}, u32[]{:S(2)}, u32[]{:S(2)}) collective-permute-start(bf16[192,2048]{1,0:T(8,128)(2,1)} %bitcast.48), channel_id=1, source_target_pairs={{0,3},{1,0},{2,1},{3,2},{4,7},{5,4},{6,5},{7,6},{8,11},{9,8},{10,9... | collective-permute-start | bytes 2359304 | tf_op jit(solution)/shard_map/ppermute | solution.py:367
  63.4 5.7 %copy-start.1 = (bf16[192,2048]{1,0:T(8,128)(2,1)}, bf16[192,2048]{1,0:T(8,128)(2,1)S(1)}, u32[]{:S(2)}) copy-start(bf16[192,2048]{1,0:T(8,128)(2,1)S(1)} %collective-permute-done.4.refs_6_) | copy-start | bytes 2359300
  63.4 49.8 %collective-permute-start.2 = (bf16[192,2048]{1,0:T(8,128)(2,1)}, bf16[192,2048]{1,0:T(8,128)(2,1)}, u32[]{:S(2)}, u32[]{:S(2)}) collective-permute-start(bf16[192,2048]{1,0:T(8,128)(2,1)} %collective-permute-done.1.refs_2_), channel_id=1, source_target_pairs={{0,1},{1,2},{2,3},{3,0},{4,5},{5,6},{6,7},{7,4},{8,9},{9,10},{10,1... | collective-permute-start | bytes 2359304 | tf_op jit(solution)/shard_map/ppermute | solution.py:368
  65.7 4.2 %copy-start.2 = (bf16[192,2048]{1,0:T(8,128)(2,1)}, bf16[192,2048]{1,0:T(8,128)(2,1)S(1)}, u32[]{:S(2)}) copy-start(bf16[192,2048]{1,0:T(8,128)(2,1)S(1)} %collective-permute-done.3.refs_5_) | copy-start | bytes 2359300
  65.7 40.0 %collective-permute-start.5 = (bf16[96,2048]{1,0:T(8,128)(2,1)S(1)}, bf16[96,2048]{1,0:T(8,128)(2,1)}, u32[]{:S(2)}, u32[]{:S(2)}) collective-permute-start(bf16[96,2048]{1,0:T(8,128)(2,1)S(1)} %slice.16), channel_id=1, source_target_pairs={{0,1},{1,2},{2,3},{3,0},{4,5},{5,6},{6,7},{7,4},{8,9},{9,10},{10,1... | collective-permute-start | bytes 1179656 | tf_op jit(solution)/shard_map/ppermute | solution.py:369
  80.3 3.5 %copy-start.3 = (bf16[192,2048]{1,0:T(8,128)(2,1)}, bf16[192,2048]{1,0:T(8,128)(2,1)S(1)}, u32[]{:S(2)}) copy-start(bf16[192,2048]{1,0:T(8,128)(2,1)S(1)} %collective-permute-done.8.refs_11_) | copy-start | bytes 2359300
  80.3 25.4 %collective-permute-start.6 = (bf16[96,2048]{1,0:T(8,128)(2,1)}, bf16[96,2048]{1,0:T(8,128)(2,1)}, u32[]{:S(2)}, u32[]{:S(2)}) collective-permute-start(bf16[96,2048]{1,0:T(8,128)(2,1)} %slice.17), channel_id=1, source_target_pairs={{0,3},{1,0},{2,1},{3,2},{4,7},{5,4},{6,5},{7,6},{8,11},{9,8},{10,9... | collective-permute-start | bytes 1179656 | tf_op jit(solution)/shard_map/ppermute | solution.py:369
  84.5 2.4 %copy-start.4 = (bf16[192,2048]{1,0:T(8,128)(2,1)}, bf16[192,2048]{1,0:T(8,128)(2,1)S(1)}, u32[]{:S(2)}) copy-start(bf16[192,2048]{1,0:T(8,128)(2,1)S(1)} %collective-permute-done.7.refs_10_) | copy-start | bytes 2359300
  84.5 28.7 %collective-permute-start.9 = (bf16[96,2048]{1,0:T(8,128)(2,1)}, bf16[96,2048]{1,0:T(8,128)(2,1)}, u32[]{:S(2)}, u32[]{:S(2)}) collective-permute-start(bf16[96,2048]{1,0:T(8,128)(2,1)} %slice.18), channel_id=1, source_target_pairs={{0,1},{1,2},{2,3},{3,0},{4,5},{5,6},{6,7},{7,4},{8,9},{9,10},{10,1... | collective-permute-start | bytes 1179656 | tf_op jit(solution)/shard_map/ppermute | solution.py:369
  87.7 25.6 %collective-permute-start.10 = (bf16[96,2048]{1,0:T(8,128)(2,1)}, bf16[96,2048]{1,0:T(8,128)(2,1)}, u32[]{:S(2)}, u32[]{:S(2)}) collective-permute-start(bf16[96,2048]{1,0:T(8,128)(2,1)} %slice.19), channel_id=1, source_target_pairs={{0,3},{1,0},{2,1},{3,2},{4,7},{5,4},{6,5},{7,6},{8,11},{9,8},{10,9... | collective-permute-start | bytes 1179656 | tf_op jit(solution)/shard_map/ppermute | solution.py:369
  128.9 56.3 %all-to-all-start.1 = ((bf16[128,48,128]{2,1,0:T(8,128)(2,1)}), bf16[128,48,128]{2,1,0:T(8,128)(2,1)S(1)}, u32[]{:S(2)}, u32[]{:S(2)}) async-start(bf16[128,48,128]{2,1,0:T(8,128)(2,1)} %get-tuple-element.30), calls=%async_computation.1 | async-start | bytes 3145728 | tf_op jit(solution)/shard_map/all_to_all | solution.py:414
  147.3 12.3 %collective-permute-start.11 = (f32[3,16,768]{2,1,0:T(8,128)}, f32[3,16,768]{2,1,0:T(8,128)S(1)}, u32[]{:S(2)}, u32[]{:S(2)}) collective-permute-start(f32[3,16,768]{2,1,0:T(8,128)} %get-tuple-element.36), channel_id=1, source_target_pairs={{0,1},{1,2},{2,3},{3,0},{4,5},{5,6},{6,7},{7,4},{8,9},{9,10},{10,1... | collective-permute-start | bytes 442376 | tf_op jit(solution)/shard_map/ppermute | solution.py:428
  149.4 10.2 %collective-permute-start.12 = (f32[3,16,768]{2,1,0:T(8,128)}, f32[3,16,768]{2,1,0:T(8,128)S(1)}, u32[]{:S(2)}, u32[]{:S(2)}) collective-permute-start(f32[3,16,768]{2,1,0:T(8,128)} %get-tuple-element.37), channel_id=1, source_target_pairs={{0,2},{1,3},{2,0},{3,1},{4,6},{5,7},{6,4},{7,5},{8,10},{9,11},{10,... | collective-permute-start | bytes 442376 | tf_op jit(solution)/shard_map/ppermute | solution.py:428
  154.1 8.0 %collective-permute-start.13 = (f32[3,16,768]{2,1,0:T(8,128)}, f32[3,16,768]{2,1,0:T(8,128)S(1)}, u32[]{:S(2)}, u32[]{:S(2)}) collective-permute-start(f32[3,16,768]{2,1,0:T(8,128)} %get-tuple-element.38), channel_id=1, source_target_pairs={{0,3},{1,0},{2,1},{3,2},{4,7},{5,4},{6,5},{7,6},{8,11},{9,8},{10,9... | collective-permute-start | bytes 442376 | tf_op jit(solution)/shard_map/ppermute | solution.py:428
  162.1 0.9 copy-start
where the time goes:
time: 188 us; the launch traced here: 187 us
  starting transfers between devices  78.5 us (42%)
  waiting for transfers between devices  73.9 us (39%)
  Pallas kernels  27.4 us (15%)
  local copies, waits for them, and re-layouts  3.27 us (2%)
  other arithmetic  3.09 us (2%)
    pallas_call x5, Pallas kernels, call(): pl.pallas_call(body, out_shape=[space(s, d) for s, d, space in outs], in_...  27.4 us
    ppermute x2, waiting for transfers between devices, layer(): behind = [early] + [lax.ppermute(w, 'dp', up_ring) for w in late[1:]]  23.7 us
    all_to_all x1, waiting for transfers between devices, layer(): lax.all_to_all(send_back, 'expert', split_axis=0, concat_axis=0, tiled=True)  21.6 us
    ppermute x2, waiting for transfers between devices, layer(): lax.ppermute(behind[m][:half], 'dp', up_ring)  17.6 us
    all_to_all x1, starting transfers between devices, layer(): lax.all_to_all(send, 'expert', split_axis=0, concat_axis=0, tiled=True)  17.4 us
    all_to_all x1, starting transfers between devices, layer(): lax.all_to_all(send_back, 'expert', split_axis=0, concat_axis=0, tiled=True)  13.7 us
    ppermute x3, starting transfers between devices, layer(): ahead = [lax.ppermute(w, 'dp', down_ring) for w in late]  12 us
    ppermute x3, starting transfers between devices, layer(): lax.ppermute(shares[k], 'dp', [(i, (i + k) % shards) for i in range(shard...  10.1 us
  transfers between devices with their start and end apart: 16, of which 8 were waited for; matrix products, arithmetic and copies ran while one was open for 3% of the time, Pallas kernels for 3%

commit v1 on v0

--- a/solution.py
+++ b/solution.py
@@ -26,6 +26,10 @@
 
 def in_hbm(arrays):
     return [pltpu.with_memory_space_constraint(a, pltpu.HBM) for a in arrays]
+
+
+def in_vmem(arrays):
+    return [pltpu.with_memory_space_constraint(a, pltpu.VMEM) for a in arrays]
 
 
 def smem():
@@ -90,7 +94,7 @@
 
 
 def dispatch_body(slots, group_tokens, doc_count):
-    def body(routes_ref, nums_ref, lengths_ref, start_ref, x_hbm, g_hbm, send_ref, wide, stage, x_ref, g_ref, lsems, sems):
+    def body(routes_ref, nums_ref, lengths_ref, start_ref, x_hbm, g_hbm, send_ref, wide, more, stage, x_ref, g_ref, lsems, sems):
         loads = [
             pltpu.make_async_copy(x_hbm, x_ref, lsems.at[0]),
             pltpu.make_async_copy(g_hbm, g_ref, lsems.at[1]),
@@ -100,7 +104,7 @@
         experts = stage.shape[0]
         tokens, features = x_ref.shape
         tiles = features // LANES
-        depth = 2 * slots * tiles
+        depth = slots * tiles
         pitch = depth + 4
         first, second, either, rank = choice_masks(routes_ref, experts, tokens)
         position = start_ref[0] + lax.broadcasted_iota(jnp.int32, (1, tokens), 1)
@@ -120,44 +124,49 @@
             picks.append(chosen.astype(BF16))
         pick = jnp.concatenate(picks, axis=0)
         scale = jnp.concatenate(scales, axis=0)
-        for load in loads:
-            load.wait()
         chunk = 2 * LANES
-        for j in range(features // chunk):
-            cols = slice(j * chunk, (j + 1) * chunk)
-            both = (dot(pick, x_ref[:, cols]), scale * dot(pick, g_ref[:, cols]))
-            for side in range(2):
+        copies = []
+        for side, (source, scratch) in enumerate(((x_ref, wide), (g_ref, more))):
+            loads[side].wait()
+            for j in range(features // chunk):
+                part = dot(pick, source[:, j * chunk : (j + 1) * chunk])
+                if side == 1:
+                    part = scale * part
                 for c in range(slots):
                     for h in range(2):
-                        wide[pl.ds((side * slots + c) * tiles + 2 * j + h, experts, stride=pitch), :] = both[
-                            side
-                        ][c * experts : (c + 1) * experts, h * LANES : (h + 1) * LANES]
-        pack_blocks(wide, stage, send_ref, sems, pitch)
+                        scratch[pl.ds(c * tiles + 2 * j + h, experts, stride=pitch), :] = part[
+                            c * experts : (c + 1) * experts, h * LANES : (h + 1) * LANES
+                        ]
+            at = pl.ds(side * depth, depth)
+            for i in range(experts // 8):
+                for e in range(i * 8, i * 8 + 8):
+                    stage[e, at, :] = scratch[e * pitch : e * pitch + depth, :].astype(BF16)
+                some = pl.ds(i * 8, 8)
+                copies.append(
+                    pltpu.make_async_copy(
+                        stage.at[some, at], send_ref.at[some, at], sems.at[side, i]
+                    )
+                )
+                copies[-1].start()
+        for copy in copies:
+            copy.wait()
 
     return body
 
 
-def expert_body(slots, places):
+def product_body(slots, places):
     def body(recv_ref, *refs):
         weight_refs, refs = refs[: len(places)], refs[len(places) :]
-        left_ref, bdown_ref, right_ref, send_ref, rows_out, acts_out, lows_ref = refs[:7]
-        wide, more, x, s, gates, ups, acts, weights, backs, stage, sems, osems, ssems = refs[7:]
+        left_ref, bdown_ref, right_ref, rows_out, s, gates, ups, lows_ref, weights = refs[:9]
+        x, wide, more, sems, osems = refs[9:]
         peers = recv_ref.shape[0]
         features = x.shape[1]
-        hidden = acts.shape[2]
+        hidden = gates.shape[1]
         tiles = features // LANES
         depth = slots * tiles
         pitch = depth + 4
         narrow = tiles + 4
-        copies = [[], [], []]
-        for k, (ref, (m, at, size)) in enumerate(zip(weight_refs, places)):
-            copies[m].append(
-                pltpu.make_async_copy(ref, weights.at[m, pl.ds(at, size)], sems.at[k])
-            )
-        for m in range(3):
-            for copy in copies[m]:
-                copy.start()
-
+        copies = start_copies(weight_refs, places, weights, sems)
         for e in range(peers):
             wide[e * pitch : e * pitch + depth, :] = recv_ref[e, :depth, :].astype(F32)
         for j in range(tiles):
@@ -165,16 +174,12 @@
                 x[c * peers : (c + 1) * peers, j * LANES : (j + 1) * LANES] = wide[
                     pl.ds(c * tiles + j, peers, stride=pitch), :
                 ].astype(BF16)
-
-        chunk = 256
-        chunks = [slice(n * chunk, (n + 1) * chunk) for n in range(hidden // chunk)]
+        chunk = hidden // slots
         for copy in copies[0]:
             copy.wait()
         lows = dot(x[...], left_ref[...], NT)
-        gate_low = lows[:, :16].astype(BF16)
-        up_low = lows[:, 16:].astype(BF16)
-        lows_ref[0] = gate_low
-        lows_ref[1] = up_low
+        lows_ref[0] = lows[:, :16].astype(BF16)
+        lows_ref[1] = lows[:, 16:].astype(BF16)
 
         @pl.loop(0, slots)
         def _(c):
@@ -198,28 +203,59 @@
         ]
         for copy in out_copies:
             copy.start()
-        for cols in chunks:
+        for n in range(slots):
+            cols = slice(n * chunk, (n + 1) * chunk)
             ups[:, cols] = dot(x[...], weights[1, cols, :], NT) + SCALE * dot(
                 lows_ref[1], right_ref[1, :, cols]
             )
-        grad_low = dot(s[...], bdown_ref[...], NT).astype(BF16)
-        lows_ref[2] = grad_low
-        for copy in copies[2]:
+        lows_ref[2] = dot(s[...], bdown_ref[...], NT).astype(BF16)
+        for copy in out_copies:
             copy.wait()
-        for cols in chunks:
+
+    return body
+
+
+def start_copies(refs, places, weights, sems):
+    copies = [[] for _ in range(weights.shape[0])]
+    for k, (ref, (m, at, size)) in enumerate(zip(refs, places)):
+        copies[m].append(pltpu.make_async_copy(ref, weights.at[m, pl.ds(at, size)], sems.at[k]))
+        copies[m][-1].start()
+    return copies
+
+
+def expert_body(slots, places):
+    def body(s, gates, ups, lows_ref, weights, *refs):
+        weight_refs, refs = refs[: len(places)], refs[len(places) :]
+        left_ref, right_ref, send_ref, acts_out, lows_out = refs[:5]
+        wide, down, acts, all_lows, backs, stage, sems, ssems, osems = refs[5:]
+        rows, features = s.shape
+        hidden = gates.shape[1]
+        peers = rows // slots
+        tiles = features // LANES
+        pitch = slots * tiles + 4
+        chunk = 2 * LANES
+        for copy in start_copies(weight_refs, places, down, sems)[0]:
+            copy.wait()
+        for n in range(hidden // chunk):
+            cols = slice(n * chunk, (n + 1) * chunk)
             gate, up = gates[:, cols], ups[:, cols]
-            back = dot(s[...], weights[2, cols, :], NT) + SCALE * dot(
-                lows_ref[2], right_ref[2, :, cols]
-            )
+            back = dot(s[...], down[0, cols, :], NT) + SCALE * dot(lows_ref[2], right_ref[2, :, cols])
             sigma = jax.nn.sigmoid(gate)
             active = gate * sigma
             acts[0, :, cols] = (active * up).astype(BF16)
             acts[1, :, cols] = (back * up * sigma * (1.0 + gate * (1.0 - sigma))).astype(BF16)
             acts[2, :, cols] = (back * active).astype(BF16)
-        out_copies.append(pltpu.make_async_copy(acts, acts_out, osems.at[2]))
-        out_copies[2].start()
         gate_back = dot(acts[1], right_ref[0], NT).astype(BF16)
         up_back = dot(acts[2], right_ref[1], NT).astype(BF16)
+        all_lows[0:3] = lows_ref[...]
+        all_lows[3] = gate_back
+        all_lows[4] = up_back
+        out_copies = [
+            pltpu.make_async_copy(acts, acts_out, osems.at[0]),
+            pltpu.make_async_copy(all_lows, lows_out, osems.at[1]),
+        ]
+        for copy in out_copies:
+            copy.start()
         backs[:, :16] = gate_back
         backs[:, 16:] = up_back
         for j in range(features // chunk):
@@ -234,9 +270,6 @@
                     wide[
                         pl.ds(c * tiles + j * (chunk // LANES) + h, peers, stride=pitch), :
                     ] = part[c * peers : (c + 1) * peers, h * LANES : (h + 1) * LANES]
-
-        lows_ref[3] = gate_back
-        lows_ref[4] = up_back
         pack_blocks(wide, stage, send_ref, ssems, pitch)
         for copy in out_copies:
             copy.wait()
@@ -336,7 +369,6 @@
 
     up_ring = [(i, (i + 1) % shards) for i in range(shards)]
     down_ring = [(i, (i - 1) % shards) for i in range(shards)]
-    early = lax.ppermute(w_gate[0], "dp", up_ring)
     (send,) = call(
         dispatch_body(slots, tokens * groups, doc_lengths.shape[1]),
         (*in_hbm((routes_t, gate_num[0].T, doc_lengths)), start, *in_hbm((x, g))),
@@ -344,78 +376,92 @@
         [((groups, 2 * depth, LANES), BF16, pltpu.HBM)],
         [anyspace()],
         [
-            pltpu.VMEM((groups * (2 * depth + 4), LANES), F32),
+            pltpu.VMEM((groups * (depth + 4), LANES), F32),
+            pltpu.VMEM((groups * (depth + 4), LANES), F32),
             pltpu.VMEM((groups, 2 * depth, LANES), BF16),
             pltpu.VMEM((tokens, features), BF16),
             pltpu.VMEM((tokens, features), BF16),
             pltpu.SemaphoreType.DMA((2,)),
-            pltpu.SemaphoreType.DMA((groups // 8,)),
+            pltpu.SemaphoreType.DMA((2, groups // 8)),
         ],
         4 * rows * tokens * features,
         4 * rows * features,
         16,
     )
-    send, gate_late, w_up_late, w_down_late = lax.optimization_barrier(
-        (send, w_gate[0], w_up[0], w_down[0])
-    )
     own = (w_gate[0], w_up[0], w_down[0])
-    late = (gate_late, w_up_late, w_down_late)
     recv = lax.all_to_all(send, "expert", split_axis=0, concat_axis=0, tiled=True)
 
     half = share // 2
-    behind = [early] + [lax.ppermute(w, "dp", up_ring) for w in late[1:]]
-    ahead = [lax.ppermute(w, "dp", down_ring) for w in late]
-    far = [[lax.ppermute(behind[0], "dp", up_ring)]] + [
-        [lax.ppermute(behind[m][:half], "dp", up_ring), lax.ppermute(ahead[m][half:], "dp", down_ring)]
-        for m in (1, 2)
-    ]
-    weights, places = [], []
-    for m in range(3):
-        weights += [own[m], ahead[m], behind[m], *far[m]]
-        places += [(m, 0, share), (m, share, share), (m, 3 * share, share)]
-        size = share // len(far[m])
-        places += [(m, 2 * share + k * size, size) for k in range(len(far[m]))]
+    parts = []
+    for w in own:
+        behind = lax.ppermute(w, "dp", up_ring)
+        ahead = lax.ppermute(w, "dp", down_ring)
+        far = [lax.ppermute(behind[:half], "dp", up_ring), lax.ppermute(ahead[half:], "dp", down_ring)]
+        parts.append((w, ahead, behind, *far))
+    spots = ((0, share), (share, share), (3 * share, share), (2 * share, half), (2 * share + half, half))
 
     left = jnp.concatenate([a_gate[0].T, a_up[0].T], axis=0)
     right = jnp.stack([b_gate[0], b_up[0], a_down[0].T])
     right = lax.dynamic_slice_in_dim(
         jnp.concatenate([right, right], axis=2), me * share, hidden, axis=2
     )
-    send_back, row_blocks, acts, lows = call(
-        expert_body(slots, places),
-        (recv, *in_hbm((*weights, left, b_down[0], right))),
-        [vmem()] + [anyspace()] * len(weights) + [vmem()] * 3,
+    row_blocks, s_rows, gates, ups, lows, both = call(
+        product_body(slots, [(m, *spot) for m in range(2) for spot in spots]),
+        (recv, *in_hbm((*parts[0], *parts[1], left, b_down[0], right))),
+        [vmem()] + [anyspace()] * 10 + [vmem()] * 3,
+        [
+            ((2, rows, features), BF16, pltpu.HBM),
+            ((rows, features), BF16, pltpu.VMEM),
+            ((rows, hidden), F32, pltpu.VMEM),
+            ((rows, hidden), F32, pltpu.VMEM),
+            ((3, rows, rank_dim), BF16, pltpu.VMEM),
+            ((2, hidden, features), BF16, pltpu.VMEM),
+        ],
+        [anyspace()] + [vmem()] * 5,
+        [
+            pltpu.VMEM((rows, features), BF16),
+            pltpu.VMEM((groups * (depth + 4), LANES), F32),
+            pltpu.VMEM((groups * (tiles + 4), LANES), F32),
+            pltpu.SemaphoreType.DMA((10,)),
+            pltpu.SemaphoreType.DMA((2,)),
+        ],
+        4 * rows * hidden * features,
+        4 * hidden * features + 4 * rows * features,
+        12,
+    )
+    send_back, acts, all_lows = call(
+        expert_body(slots, [(0, *spot) for spot in spots]),
+        (*in_vmem((s_rows, gates, ups, lows, both)), *in_hbm((*parts[2], left, right))),
+        [vmem()] * 5 + [anyspace()] * 5 + [vmem()] * 2,
         [
             ((groups, depth, LANES), BF16, pltpu.HBM),
-            ((2, rows, features), BF16, pltpu.HBM),
             ((3, rows, hidden), BF16, pltpu.HBM),
             ((5, rows, rank_dim), BF16, pltpu.HBM),
         ],
-        [anyspace(), anyspace(), anyspace(), vmem()],
+        [anyspace()] * 3,
         [
             pltpu.VMEM((groups * (depth + 4), LANES), F32),
-            pltpu.VMEM((groups * (tiles + 4), LANES), F32),
-            pltpu.VMEM((rows, features), BF16),
-            pltpu.VMEM((rows, features), BF16),
-            pltpu.VMEM((rows, hidden), F32),
-            pltpu.VMEM((rows, hidden), F32),
+            pltpu.VMEM((1, hidden, features), BF16),
             pltpu.VMEM((3, rows, hidden), BF16),
-            pltpu.VMEM((3, hidden, features), BF16),
+            pltpu.VMEM((5, rows, rank_dim), BF16),
             pltpu.VMEM((rows, 2 * rank_dim), BF16),
             pltpu.VMEM((groups, depth, LANES), BF16),
-            pltpu.SemaphoreType.DMA((len(places),)),
-            pltpu.SemaphoreType.DMA((3,)),
+            pltpu.SemaphoreType.DMA((5,)),
             pltpu.SemaphoreType.DMA((groups // 8,)),
+            pltpu.SemaphoreType.DMA((2,)),
         ],
-        10 * rows * hidden * features,
-        6 * hidden * features + 6 * rows * features,
-        40,
+        6 * rows * hidden * features,
+        2 * hidden * features + 2 * rows * features,
+        18,
     )
     back = lax.all_to_all(send_back, "expert", split_axis=0, concat_axis=0, tiled=True)
 
     *shares, pick = call(
         adapter_body(slots, share, width),
-        (me.astype(jnp.int32).reshape(1), *in_hbm((routes_t, row_blocks, acts, lows, right))),
+        (
+            me.astype(jnp.int32).reshape(1),
+            *in_hbm((routes_t, row_blocks, acts, all_lows, right)),
+        ),
         [smem()] + [vmem()] * 5,
         [((3, rank_dim, width + 256), F32, pltpu.HBM)] * 4 + [((tokens, rows), BF16, pltpu.VMEM)],
         [vmem()] * 5,
@@ -424,13 +470,13 @@
         4 * rows * features,
         12,
     )
-    parts = [shares[0]] + [
+    pieces = [shares[0]] + [
         lax.ppermute(shares[k], "dp", [(i, (i + k) % shards) for i in range(shards)])
         for k in range(1, shards)
     ]
     big_gate, big_up, big_down, small_gate, small_up, small_down = call(
         total_body(share, width),
-        parts,
+        pieces,
         [vmem()] * 4,
         [((rank_dim, width), F32, pltpu.HBM)] * 3 + [((rank_dim, share), F32, pltpu.HBM)] * 3,
         [vmem()] * 6,

time: 188 us -> 176 us (0.936)
  the two profiles are of different devices: /device:TPU:8 before, /device:TPU:14 now
where the time goes in v1:
time: 176 us; the launch traced here: 175 us
  starting transfers between devices  78.7 us (45%)
  waiting for transfers between devices  59.2 us (34%)
  Pallas kernels  29.1 us (17%)
  local copies, waits for them, and re-layouts  4.87 us (3%)
  other arithmetic  2.24 us (1%)
    pallas_call x6, Pallas kernels, call(): pl.pallas_call(body, out_shape=[space(s, d) for s, d, space in outs], in_...  29.1 us
    ppermute x3, waiting for transfers between devices, layer(): behind = lax.ppermute(w, 'dp', up_ring)  23.2 us
    all_to_all x1, waiting for transfers between devices, layer(): lax.all_to_all(send_back, 'expert', split_axis=0, concat_axis=0, tiled=True)  21.6 us
    all_to_all x1, starting transfers between devices, layer(): lax.all_to_all(send, 'expert', split_axis=0, concat_axis=0, tiled=True)  17.4 us
    all_to_all x1, starting transfers between devices, layer(): lax.all_to_all(send_back, 'expert', split_axis=0, concat_axis=0, tiled=True)  13.7 us
    ppermute x3, starting transfers between devices, layer(): lax.ppermute(behind[:half], 'dp', up_ring)  11.9 us
    ppermute x3, starting transfers between devices, layer(): behind = lax.ppermute(w, 'dp', up_ring)  10.8 us
    ppermute x3, starting transfers between devices, layer(): ahead = lax.ppermute(w, 'dp', down_ring)  8.42 us
  transfers between devices with their start and end apart: 17, of which 12 were waited for; matrix products, arithmetic and copies ran while one was open for 4% of the time, Pallas kernels for 7%

profile of v1, /device:TPU:14, one launch (start us, length us, event | category | flops | bytes accessed | tf_op | source)
XLA Modules:
  0.0 175.1 jit_solution(10580095730527984420)
XLA Ops:
  0.6 4.7 %shard_map.189 = bf16[128,96,128]{2,1,0:T(8,128)(2,1)} custom-call(s32[2,128]{1,0:T(2,128)} %bitcast.54, s32[2,128]{1,0:T(2,128)} %bitcast.56, s32[1,32]{1,0:T(1,128)} %lengths_ref.1, s32[1]{0:T(128)} %bitcast.4.start_ref, bf16[128,2048]{1,0:T(8,128)(2,1)} %bitcast.47, bf16[128,2048]{1,0:T(8,128)(2,1)} %bitcast.48), custom_call_target="tpu_custom_call" | custom-call | flops 402653184 | bytes 3145728 | tf_op jit(solution)/shard_map/pallas_call | solution.py:44
  5.4 17.4 %all-to-all-start = ((bf16[128,96,128]{2,1,0:T(8,128)(2,1)}), bf16[128,96,128]{2,1,0:T(8,128)(2,1)S(1)}, u32[]{:S(2)}, u32[]{:S(2)}) async-start(bf16[128,96,128]{2,1,0:T(8,128)(2,1)} %shard_map.189), calls=%async_computation | async-start | bytes 6291456 | tf_op jit(solution)/shard_map/all_to_all | solution.py:392
  22.7 2.4 %collective-permute-start.1 = (bf16[192,2048]{1,0:T(8,128)(2,1)}, bf16[192,2048]{1,0:T(8,128)(2,1)S(1)}, u32[]{:S(2)}, u32[]{:S(2)}) collective-permute-start(bf16[192,2048]{1,0:T(8,128)(2,1)} %bitcast.41), channel_id=1, source_target_pairs={{0,1},{1,2},{2,3},{3,0},{4,5},{5,6},{6,7},{7,4},{8,9},{9,10},{10,1... | collective-permute-start | bytes 2359304 | tf_op jit(solution)/shard_map/ppermute | solution.py:397
  25.2 3.5 %collective-permute-start = (bf16[192,2048]{1,0:T(8,128)(2,1)}, bf16[192,2048]{1,0:T(8,128)(2,1)S(1)}, u32[]{:S(2)}, u32[]{:S(2)}) collective-permute-start(bf16[192,2048]{1,0:T(8,128)(2,1)} %bitcast.42), channel_id=1, source_target_pairs={{0,3},{1,0},{2,1},{3,2},{4,7},{5,4},{6,5},{7,6},{8,11},{9,8},{10,9... | collective-permute-start | bytes 2359304 | tf_op jit(solution)/shard_map/ppermute | solution.py:398
  28.6 3.6 %collective-permute-start.5 = (bf16[192,2048]{1,0:T(8,128)(2,1)}, bf16[192,2048]{1,0:T(8,128)(2,1)S(1)}, u32[]{:S(2)}, u32[]{:S(2)}) collective-permute-start(bf16[192,2048]{1,0:T(8,128)(2,1)} %bitcast.44), channel_id=1, source_target_pairs={{0,1},{1,2},{2,3},{3,0},{4,5},{5,6},{6,7},{7,4},{8,9},{9,10},{10,1... | collective-permute-start | bytes 2359304 | tf_op jit(solution)/shard_map/ppermute | solution.py:397
  32.2 2.2 %collective-permute-start.4 = (bf16[192,2048]{1,0:T(8,128)(2,1)}, bf16[192,2048]{1,0:T(8,128)(2,1)S(1)}, u32[]{:S(2)}, u32[]{:S(2)}) collective-permute-start(bf16[192,2048]{1,0:T(8,128)(2,1)} %bitcast.45), channel_id=1, source_target_pairs={{0,3},{1,0},{2,1},{3,2},{4,7},{5,4},{6,5},{7,6},{8,11},{9,8},{10,9... | collective-permute-start | bytes 2359304 | tf_op jit(solution)/shard_map/ppermute | solution.py:398
  34.5 4.8 %collective-permute-start.9 = (bf16[192,2048]{1,0:T(8,128)(2,1)}, bf16[192,2048]{1,0:T(8,128)(2,1)S(1)}, u32[]{:S(2)}, u32[]{:S(2)}) collective-permute-start(bf16[192,2048]{1,0:T(8,128)(2,1)} %bitcast.38), channel_id=1, source_target_pairs={{0,1},{1,2},{2,3},{3,0},{4,5},{5,6},{6,7},{7,4},{8,9},{9,10},{10,1... | collective-permute-start | bytes 2359304 | tf_op jit(solution)/shard_map/ppermute | solution.py:397
  39.3 6.0 %collective-permute-done.1.refs_2_ = bf16[192,2048]{1,0:T(8,128)(2,1)S(1)} collective-permute-done((bf16[192,2048]{1,0:T(8,128)(2,1)}, bf16[192,2048]{1,0:T(8,128)(2,1)S(1)}, u32[]{:S(2)}, u32[]{:S(2)}) %collective-permute-start.1) | collective-permute-done | bytes 786464 | tf_op jit(solution)/shard_map/ppermute | solution.py:397
  45.3 0.0 copy-start.3
  45.3 2.7 %collective-permute-start.8 = (bf16[192,2048]{1,0:T(8,128)(2,1)}, bf16[192,2048]{1,0:T(8,128)(2,1)S(1)}, u32[]{:S(2)}, u32[]{:S(2)}) collective-permute-start(bf16[192,2048]{1,0:T(8,128)(2,1)} %bitcast.39), channel_id=1, source_target_pairs={{0,3},{1,0},{2,1},{3,2},{4,7},{5,4},{6,5},{7,6},{8,11},{9,8},{10,9... | collective-permute-start | bytes 2359304 | tf_op jit(solution)/shard_map/ppermute | solution.py:398
  48.0 0.8 collective-permute-done.refs_1_
  48.9 0.0 copy-start.4
  48.9 3.5 %collective-permute-start.2 = (bf16[96,2048]{1,0:T(8,128)(2,1)S(1)}, bf16[96,2048]{1,0:T(8,128)(2,1)S(1)}, u32[]{:S(2)}, u32[]{:S(2)}) collective-permute-start(bf16[96,2048]{1,0:T(8,128)(2,1)S(1)} %slice.24), channel_id=1, source_target_pairs={{0,1},{1,2},{2,3},{3,0},{4,5},{5,6},{6,7},{7,4},{8,9},{9,10},{10,1... | collective-permute-start | bytes 1179656 | tf_op jit(solution)/shard_map/ppermute | solution.py:399
  52.4 0.8 slice.25
  53.2 0.0 copy-start.8
  53.2 0.0 copy-start.9
  53.2 9.0 %collective-permute-done.5.refs_7_ = bf16[192,2048]{1,0:T(8,128)(2,1)S(1)} collective-permute-done((bf16[192,2048]{1,0:T(8,128)(2,1)}, bf16[192,2048]{1,0:T(8,128)(2,1)S(1)}, u32[]{:S(2)}, u32[]{:S(2)}) %collective-permute-start.5) | collective-permute-done | bytes 786464 | tf_op jit(solution)/shard_map/ppermute | solution.py:397
  62.1 0.0 copy-start.5
  62.1 2.7 %collective-permute-start.3 = (bf16[96,2048]{1,0:T(8,128)(2,1)}, bf16[96,2048]{1,0:T(8,128)(2,1)}, u32[]{:S(2)}, u32[]{:S(2)}) collective-permute-start(bf16[96,2048]{1,0:T(8,128)(2,1)} %slice.25), channel_id=1, source_target_pairs={{0,3},{1,0},{2,1},{3,2},{4,7},{5,4},{6,5},{7,6},{8,11},{9,8},{10,9... | collective-permute-start | bytes 1179656 | tf_op jit(solution)/shard_map/ppermute | solution.py:399
  64.9 0.8 slice.26
  65.6 0.1 collective-permute-done.4.refs_6_
  65.7 0.0 copy-start.6
  65.7 4.2 %collective-permute-start.6 = (bf16[96,2048]{1,0:T(8,128)(2,1)}, bf16[96,2048]{1,0:T(8,128)(2,1)}, u32[]{:S(2)}, u32[]{:S(2)}) collective-permute-start(bf16[96,2048]{1,0:T(8,128)(2,1)} %slice.26), channel_id=1, source_target_pairs={{0,1},{1,2},{2,3},{3,0},{4,5},{5,6},{6,7},{7,4},{8,9},{9,10},{10,1... | collective-permute-start | bytes 1179656 | tf_op jit(solution)/shard_map/ppermute | solution.py:399
  69.9 0.8 slice.27
  70.7 8.2 %collective-permute-done.9.refs_2_ = bf16[192,2048]{1,0:T(8,128)(2,1)S(1)} collective-permute-done((bf16[192,2048]{1,0:T(8,128)(2,1)}, bf16[192,2048]{1,0:T(8,128)(2,1)S(1)}, u32[]{:S(2)}, u32[]{:S(2)}) %collective-permute-start.9) | collective-permute-done | bytes 786464 | tf_op jit(solution)/shard_map/ppermute | solution.py:397
  79.0 2.7 %collective-permute-start.7 = (bf16[96,2048]{1,0:T(8,128)(2,1)}, bf16[96,2048]{1,0:T(8,128)(2,1)}, u32[]{:S(2)}, u32[]{:S(2)}) collective-permute-start(bf16[96,2048]{1,0:T(8,128)(2,1)} %slice.27), channel_id=1, source_target_pairs={{0,3},{1,0},{2,1},{3,2},{4,7},{5,4},{6,5},{7,6},{8,11},{9,8},{10,9... | collective-permute-start | bytes 1179656 | tf_op jit(solution)/shard_map/ppermute | solution.py:399
  81.7 0.0 copy-done.1
  81.7 0.8 slice.28
  82.5 0.0 copy-done.3
  82.5 0.1 collective-permute-done.8.refs_1_
  82.6 4.2 %collective-permute-start.10 = (bf16[96,2048]{1,0:T(8,128)(2,1)}, bf16[96,2048]{1,0:T(8,128)(2,1)}, u32[]{:S(2)}, u32[]{:S(2)}) collective-permute-start(bf16[96,2048]{1,0:T(8,128)(2,1)} %slice.28), channel_id=1, source_target_pairs={{0,1},{1,2},{2,3},{3,0},{4,5},{5,6},{6,7},{7,4},{8,9},{9,10},{10,1... | collective-permute-start | bytes 1179656 | tf_op jit(solution)/shard_map/ppermute | solution.py:399
  86.8 0.0 copy-done.2
  86.8 0.8 slice.29
  87.6 0.0 copy-done.4
  87.6 0.0 collective-permute-done.2.refs_3_
  87.6 0.0 copy-done.5
  87.6 0.0 copy-start.7
  87.7 2.7 %collective-permute-start.11 = (bf16[96,2048]{1,0:T(8,128)(2,1)}, bf16[96,2048]{1,0:T(8,128)(2,1)}, u32[]{:S(2)}, u32[]{:S(2)}) collective-permute-start(bf16[96,2048]{1,0:T(8,128)(2,1)} %slice.29), channel_id=1, source_target_pairs={{0,3},{1,0},{2,1},{3,2},{4,7},{5,4},{6,5},{7,6},{8,11},{9,8},{10,9... | collective-permute-start | bytes 1179656 | tf_op jit(solution)/shard_map/ppermute | solution.py:399
  90.3 0.0 copy-done.6
  90.3 0.0 copy-done.8
  90.3 0.0 copy-done.9
  90.4 0.7 pad_maximum_fusion.refs_10_.refs_5_
  91.0 1.6 fusion.2.refs_12_.refs_6_.right_ref
  92.6 0.0 collective-permute-done.3.refs_4_
  92.6 3.3 %collective-permute-done.6.refs_8_ = bf16[96,2048]{1,0:T(8,128)(2,1)} collective-permute-done((bf16[96,2048]{1,0:T(8,128)(2,1)}, bf16[96,2048]{1,0:T(8,128)(2,1)}, u32[]{:S(2)}, u32[]{:S(2)}) %collective-permute-start.6) | collective-permute-done | bytes 393248 | tf_op jit(solution)/shard_map/ppermute | solution.py:399
  95.9 3.6 %collective-permute-done.7.refs_9_ = bf16[96,2048]{1,0:T(8,128)(2,1)} collective-permute-done((bf16[96,2048]{1,0:T(8,128)(2,1)}, bf16[96,2048]{1,0:T(8,128)(2,1)}, u32[]{:S(2)}, u32[]{:S(2)}) %collective-permute-start.7) | collective-permute-done | bytes 393248 | tf_op jit(solution)/shard_map/ppermute | solution.py:399
  99.5 0.0 all-to-all-done.recv_ref
  99.5 0.0 copy-done.7
  99.6 7.9 %shard_map.190 = (bf16[2,384,2048]{2,1,0:T(8,128)(2,1)}, bf16[384,2048]{1,0:T(8,128)(2,1)S(1)}, f32[384,768]{1,0:T(8,128)S(1)}, f32[384,768]{1,0:T(8,128)S(1)}, ...) custom-call(bf16[128,96,128]{2,1,0:T(8,128)(2,1)S(1)} %all-to-all-done.recv_ref, ...), custom_call_target="tpu_custom_call" | custom-call | flops 2415919104 | bytes 9437184 | tf_op jit(solution)/shard_map/pallas_call | solution.py:44
  107.4 0.0 collective-permute-done.10.refs_3_
  107.5 0.0 collective-permute-done.11.refs_4_
  107.5 9.7 %shard_map.191 = (bf16[128,48,128]{2,1,0:T(8,128)(2,1)}, bf16[3,384,768]{2,1,0:T(8,128)(2,1)}, bf16[5,384,16]{2,1,0:T(8,128)(2,1)}) custom-call(bf16[384,2048]{1,0:T(8,128)(2,1)S(1)} %get-tuple-element.27.s, f32[384,768]{1,0:T(8,128)S(1)} %get-tuple-element.28.gates, f32[384,768]{1,0:T(8,128)S(1)} %get-tuple-element.29.ups, ...), custom_call_target="tpu_custom_call" | custom-call | flops 3623878656 | bytes 4718592 | tf_op jit(solution)/shard_map/pallas_call | solution.py:44
  117.1 13.7 %all-to-all-start.1 = ((bf16[128,48,128]{2,1,0:T(8,128)(2,1)}), bf16[128,48,128]{2,1,0:T(8,128)(2,1)S(1)}, u32[]{:S(2)}, u32[]{:S(2)}) async-start(bf16[128,48,128]{2,1,0:T(8,128)(2,1)} %get-tuple-element.32), calls=%async_computation.1 | async-start | bytes 3145728 | tf_op jit(solution)/shard_map/all_to_all | solution.py:457
  130.9 4.5 %shard_map.192 = (f32[3,16,768]{2,1,0:T(8,128)}, f32[3,16,768]{2,1,0:T(8,128)}, f32[3,16,768]{2,1,0:T(8,128)}, f32[3,16,768]{2,1,0:T(8,128)}, bf16[128,384]{1,0:T(8,128)(2,1)S(1)}) custom-call(s32[1]{0:T(128)} %bitcast.18.me_ref, s32[2,128]{1,0:T(2,128)} %bitcast.55, bf16[2,384,2048]{2,1,0:T(8,128)(2,1)} %get-tuple-element.33.rows_ref, ...), custom_call_target="tpu_custom_call" | custom-call | flops 150994944 | bytes 3145728 | tf_op jit(solution)/shard_map/pallas_call | solution.py:44
  135.4 2.2 %collective-permute-start.12 = (f32[3,16,768]{2,1,0:T(8,128)}, f32[3,16,768]{2,1,0:T(8,128)S(1)}, u32[]{:S(2)}, u32[]{:S(2)}) collective-permute-start(f32[3,16,768]{2,1,0:T(8,128)} %get-tuple-element.38), channel_id=1, source_target_pairs={{0,1},{1,2},{2,3},{3,0},{4,5},{5,6},{6,7},{7,4},{8,9},{9,10},{10,1... | collective-permute-start | bytes 442376 | tf_op jit(solution)/shard_map/ppermute | solution.py:474
  137.6 4.0 %collective-permute-start.13 = (f32[3,16,768]{2,1,0:T(8,128)}, f32[3,16,768]{2,1,0:T(8,128)S(1)}, u32[]{:S(2)}, u32[]{:S(2)}) collective-permute-start(f32[3,16,768]{2,1,0:T(8,128)} %get-tuple-element.39), channel_id=1, source_target_pairs={{0,2},{1,3},{2,0},{3,1},{4,6},{5,7},{6,4},{7,5},{8,10},{9,11},{10,... | collective-permute-start | bytes 442376 | tf_op jit(solution)/shard_map/ppermute | solution.py:474
  141.6 2.1 %collective-permute-start.14 = (f32[3,16,768]{2,1,0:T(8,128)}, f32[3,16,768]{2,1,0:T(8,128)S(1)}, u32[]{:S(2)}, u32[]{:S(2)}) collective-permute-start(f32[3,16,768]{2,1,0:T(8,128)} %get-tuple-element.40), channel_id=1, source_target_pairs={{0,3},{1,0},{2,1},{3,2},{4,7},{5,4},{6,5},{7,6},{8,11},{9,8},{10,9... | collective-permute-start | bytes 442376 | tf_op jit(solution)/shard_map/ppermute | solution.py:474
  143.8 0.5 collective-permute-done.12.b_ref
  144.2 2.6 %collective-permute-done.13.c_ref = f32[3,16,768]{2,1,0:T(8,128)S(1)} collective-permute-done((f32[3,16,768]{2,1,0:T(8,128)}, f32[3,16,768]{2,1,0:T(8,128)S(1)}, u32[]{:S(2)}, u32[]{:S(2)}) %collective-permute-start.13) | collective-permute-done | bytes 147488 | tf_op jit(solution)/shard_map/ppermute | solution.py:474
  146.8 3.4 %collective-permute-done.14.d_ref = f32[3,16,768]{2,1,0:T(8,128)S(1)} collective-permute-done((f32[3,16,768]{2,1,0:T(8,128)}, f32[3,16,768]{2,1,0:T(8,128)S(1)}, u32[]{:S(2)}, u32[]{:S(2)}) %collective-permute-start.14) | collective-permute-done | bytes 147488 | tf_op jit(solution)/shard_map/ppermute | solution.py:474
  150.2 0.9 copy-done
  151.2 0.7 shard_map.194
  151.8 21.6 %all-to-all-done.1.back_ref = bf16[128,48,128]{2,1,0:T(8,128)(2,1)S(1)} async-done(((bf16[128,48,128]{2,1,0:T(8,128)(2,1)}), bf16[128,48,128]{2,1,0:T(8,128)(2,1)S(1)}, u32[]{:S(2)}, u32[]{:S(2)}) %all-to-all-start.1) | async-done | bytes 1572896 | tf_op jit(solution)/shard_map/all_to_all | solution.py:457
  173.4 1.6 shard_map.193
  (4 shorter events, 0.0 us)
Async XLA Ops:
  5.4 94.2 %all-to-all-start = ((bf16[128,96,128]{2,1,0:T(8,128)(2,1)}), bf16[128,96,128]{2,1,0:T(8,128)(2,1)S(1)}, u32[]{:S(2)}, u32[]{:S(2)}) async-start(bf16[128,96,128]{2,1,0:T(8,128)(2,1)} %shard_map.189), calls=%async_computation | async-start | bytes 6291456 | tf_op jit(solution)/shard_map/all_to_all | solution.py:392
  22.7 22.5 %collective-permute-start.1 = (bf16[192,2048]{1,0:T(8,128)(2,1)}, bf16[192,2048]{1,0:T(8,128)(2,1)S(1)}, u32[]{:S(2)}, u32[]{:S(2)}) collective-permute-start(bf16[192,2048]{1,0:T(8,128)(2,1)} %bitcast.41), channel_id=1, source_target_pairs={{0,1},{1,2},{2,3},{3,0},{4,5},{5,6},{6,7},{7,4},{8,9},{9,10},{10,1... | collective-permute-start | bytes 2359304 | tf_op jit(solution)/shard_map/ppermute | solution.py:397
  25.2 23.7 %collective-permute-start = (bf16[192,2048]{1,0:T(8,128)(2,1)}, bf16[192,2048]{1,0:T(8,128)(2,1)S(1)}, u32[]{:S(2)}, u32[]{:S(2)}) collective-permute-start(bf16[192,2048]{1,0:T(8,128)(2,1)} %bitcast.42), channel_id=1, source_target_pairs={{0,3},{1,0},{2,1},{3,2},{4,7},{5,4},{6,5},{7,6},{8,11},{9,8},{10,9... | collective-permute-start | bytes 2359304 | tf_op jit(solution)/shard_map/ppermute | solution.py:398
  28.6 33.5 %collective-permute-start.5 = (bf16[192,2048]{1,0:T(8,128)(2,1)}, bf16[192,2048]{1,0:T(8,128)(2,1)S(1)}, u32[]{:S(2)}, u32[]{:S(2)}) collective-permute-start(bf16[192,2048]{1,0:T(8,128)(2,1)} %bitcast.44), channel_id=1, source_target_pairs={{0,1},{1,2},{2,3},{3,0},{4,5},{5,6},{6,7},{7,4},{8,9},{9,10},{10,1... | collective-permute-start | bytes 2359304 | tf_op jit(solution)/shard_map/ppermute | solution.py:397
  32.2 33.5 %collective-permute-start.4 = (bf16[192,2048]{1,0:T(8,128)(2,1)}, bf16[192,2048]{1,0:T(8,128)(2,1)S(1)}, u32[]{:S(2)}, u32[]{:S(2)}) collective-permute-start(bf16[192,2048]{1,0:T(8,128)(2,1)} %bitcast.45), channel_id=1, source_target_pairs={{0,3},{1,0},{2,1},{3,2},{4,7},{5,4},{6,5},{7,6},{8,11},{9,8},{10,9... | collective-permute-start | bytes 2359304 | tf_op jit(solution)/shard_map/ppermute | solution.py:398
  34.5 44.5 %collective-permute-start.9 = (bf16[192,2048]{1,0:T(8,128)(2,1)}, bf16[192,2048]{1,0:T(8,128)(2,1)S(1)}, u32[]{:S(2)}, u32[]{:S(2)}) collective-permute-start(bf16[192,2048]{1,0:T(8,128)(2,1)} %bitcast.38), channel_id=1, source_target_pairs={{0,1},{1,2},{2,3},{3,0},{4,5},{5,6},{6,7},{7,4},{8,9},{9,10},{10,1... | collective-permute-start | bytes 2359304 | tf_op jit(solution)/shard_map/ppermute | solution.py:397
  45.3 37.2 %copy-start.3 = (bf16[192,2048]{1,0:T(8,128)(2,1)}, bf16[192,2048]{1,0:T(8,128)(2,1)S(1)}, u32[]{:S(2)}) copy-start(bf16[192,2048]{1,0:T(8,128)(2,1)S(1)} %collective-permute-done.1.refs_2_) | copy-start | bytes 2359300
  45.3 37.3 %collective-permute-start.8 = (bf16[192,2048]{1,0:T(8,128)(2,1)}, bf16[192,2048]{1,0:T(8,128)(2,1)S(1)}, u32[]{:S(2)}, u32[]{:S(2)}) collective-permute-start(bf16[192,2048]{1,0:T(8,128)(2,1)} %bitcast.39), channel_id=1, source_target_pairs={{0,3},{1,0},{2,1},{3,2},{4,7},{5,4},{6,5},{7,6},{8,11},{9,8},{10,9... | collective-permute-start | bytes 2359304 | tf_op jit(solution)/shard_map/ppermute | solution.py:398
  48.9 38.8 %copy-start.4 = (bf16[192,2048]{1,0:T(8,128)(2,1)}, bf16[192,2048]{1,0:T(8,128)(2,1)S(1)}, u32[]{:S(2)}) copy-start(bf16[192,2048]{1,0:T(8,128)(2,1)S(1)} %collective-permute-done.refs_1_) | copy-start | bytes 2359300
  48.9 38.8 %collective-permute-start.2 = (bf16[96,2048]{1,0:T(8,128)(2,1)S(1)}, bf16[96,2048]{1,0:T(8,128)(2,1)S(1)}, u32[]{:S(2)}, u32[]{:S(2)}) collective-permute-start(bf16[96,2048]{1,0:T(8,128)(2,1)S(1)} %slice.24), channel_id=1, source_target_pairs={{0,1},{1,2},{2,3},{3,0},{4,5},{5,6},{6,7},{7,4},{8,9},{9,10},{10,1... | collective-permute-start | bytes 1179656 | tf_op jit(solution)/shard_map/ppermute | solution.py:399
  53.2 37.2 %copy-start.8 = (bf16[1,2048,16]{1,2,0:T(8,128)(2,1)S(1)}, bf16[1,2048,16]{1,2,0:T(8,128)(2,1)}, u32[]{:S(2)}) copy-start(bf16[1,2048,16]{1,2,0:T(8,128)(2,1)} %param.24) | copy-start | bytes 196612
  53.2 37.2 %copy-start.9 = (bf16[1,2048,16]{1,2,0:T(8,128)(2,1)S(1)}, bf16[1,2048,16]{1,2,0:T(8,128)(2,1)}, u32[]{:S(2)}) copy-start(bf16[1,2048,16]{1,2,0:T(8,128)(2,1)} %param.22) | copy-start | bytes 196612
  62.1 25.5 %copy-start.5 = (bf16[192,2048]{1,0:T(8,128)(2,1)}, bf16[192,2048]{1,0:T(8,128)(2,1)S(1)}, u32[]{:S(2)}) copy-start(bf16[192,2048]{1,0:T(8,128)(2,1)S(1)} %collective-permute-done.5.refs_7_) | copy-start | bytes 2359300
  62.1 30.5 %collective-permute-start.3 = (bf16[96,2048]{1,0:T(8,128)(2,1)}, bf16[96,2048]{1,0:T(8,128)(2,1)}, u32[]{:S(2)}, u32[]{:S(2)}) collective-permute-start(bf16[96,2048]{1,0:T(8,128)(2,1)} %slice.25), channel_id=1, source_target_pairs={{0,3},{1,0},{2,1},{3,2},{4,7},{5,4},{6,5},{7,6},{8,11},{9,8},{10,9... | collective-permute-start | bytes 1179656 | tf_op jit(solution)/shard_map/ppermute | solution.py:399
  65.7 24.6 %copy-start.6 = (bf16[192,2048]{1,0:T(8,128)(2,1)}, bf16[192,2048]{1,0:T(8,128)(2,1)S(1)}, u32[]{:S(2)}) copy-start(bf16[192,2048]{1,0:T(8,128)(2,1)S(1)} %collective-permute-done.4.refs_6_) | copy-start | bytes 2359300
  65.7 30.2 %collective-permute-start.6 = (bf16[96,2048]{1,0:T(8,128)(2,1)}, bf16[96,2048]{1,0:T(8,128)(2,1)}, u32[]{:S(2)}, u32[]{:S(2)}) collective-permute-start(bf16[96,2048]{1,0:T(8,128)(2,1)} %slice.26), channel_id=1, source_target_pairs={{0,1},{1,2},{2,3},{3,0},{4,5},{5,6},{6,7},{7,4},{8,9},{9,10},{10,1... | collective-permute-start | bytes 1179656 | tf_op jit(solution)/shard_map/ppermute | solution.py:399
  79.0 2.7 %copy-start.1 = (bf16[192,2048]{1,0:T(8,128)(2,1)}, bf16[192,2048]{1,0:T(8,128)(2,1)S(1)}, u32[]{:S(2)}) copy-start(bf16[192,2048]{1,0:T(8,128)(2,1)S(1)} %collective-permute-done.9.refs_2_) | copy-start | bytes 2359300
  79.0 20.6 %collective-permute-start.7 = (bf16[96,2048]{1,0:T(8,128)(2,1)}, bf16[96,2048]{1,0:T(8,128)(2,1)}, u32[]{:S(2)}, u32[]{:S(2)}) collective-permute-start(bf16[96,2048]{1,0:T(8,128)(2,1)} %slice.27), channel_id=1, source_target_pairs={{0,3},{1,0},{2,1},{3,2},{4,7},{5,4},{6,5},{7,6},{8,11},{9,8},{10,9... | collective-permute-start | bytes 1179656 | tf_op jit(solution)/shard_map/ppermute | solution.py:399
  82.6 4.3 %copy-start.2 = (bf16[192,2048]{1,0:T(8,128)(2,1)}, bf16[192,2048]{1,0:T(8,128)(2,1)S(1)}, u32[]{:S(2)}) copy-start(bf16[192,2048]{1,0:T(8,128)(2,1)S(1)} %collective-permute-done.8.refs_1_) | copy-start | bytes 2359300
  82.6 24.9 %collective-permute-start.10 = (bf16[96,2048]{1,0:T(8,128)(2,1)}, bf16[96,2048]{1,0:T(8,128)(2,1)}, u32[]{:S(2)}, u32[]{:S(2)}) collective-permute-start(bf16[96,2048]{1,0:T(8,128)(2,1)} %slice.28), channel_id=1, source_target_pairs={{0,1},{1,2},{2,3},{3,0},{4,5},{5,6},{6,7},{7,4},{8,9},{9,10},{10,1... | collective-permute-start | bytes 1179656 | tf_op jit(solution)/shard_map/ppermute | solution.py:399
  87.6 11.9 %copy-start.7 = (bf16[96,2048]{1,0:T(8,128)(2,1)}, bf16[96,2048]{1,0:T(8,128)(2,1)S(1)}, u32[]{:S(2)}) copy-start(bf16[96,2048]{1,0:T(8,128)(2,1)S(1)} %collective-permute-done.2.refs_3_) | copy-start | bytes 1179652
  87.7 19.8 %collective-permute-start.11 = (bf16[96,2048]{1,0:T(8,128)(2,1)}, bf16[96,2048]{1,0:T(8,128)(2,1)}, u32[]{:S(2)}, u32[]{:S(2)}) collective-permute-start(bf16[96,2048]{1,0:T(8,128)(2,1)} %slice.29), channel_id=1, source_target_pairs={{0,3},{1,0},{2,1},{3,2},{4,7},{5,4},{6,5},{7,6},{8,11},{9,8},{10,9... | collective-permute-start | bytes 1179656 | tf_op jit(solution)/shard_map/ppermute | solution.py:399
  117.1 56.3 %all-to-all-start.1 = ((bf16[128,48,128]{2,1,0:T(8,128)(2,1)}), bf16[128,48,128]{2,1,0:T(8,128)(2,1)S(1)}, u32[]{:S(2)}, u32[]{:S(2)}) async-start(bf16[128,48,128]{2,1,0:T(8,128)(2,1)} %get-tuple-element.32), calls=%async_computation.1 | async-start | bytes 3145728 | tf_op jit(solution)/shard_map/all_to_all | solution.py:457
  135.4 8.8 %collective-permute-start.12 = (f32[3,16,768]{2,1,0:T(8,128)}, f32[3,16,768]{2,1,0:T(8,128)S(1)}, u32[]{:S(2)}, u32[]{:S(2)}) collective-permute-start(f32[3,16,768]{2,1,0:T(8,128)} %get-tuple-element.38), channel_id=1, source_target_pairs={{0,1},{1,2},{2,3},{3,0},{4,5},{5,6},{6,7},{7,4},{8,9},{9,10},{10,1... | collective-permute-start | bytes 442376 | tf_op jit(solution)/shard_map/ppermute | solution.py:474
  137.6 9.2 %collective-permute-start.13 = (f32[3,16,768]{2,1,0:T(8,128)}, f32[3,16,768]{2,1,0:T(8,128)S(1)}, u32[]{:S(2)}, u32[]{:S(2)}) collective-permute-start(f32[3,16,768]{2,1,0:T(8,128)} %get-tuple-element.39), channel_id=1, source_target_pairs={{0,2},{1,3},{2,0},{3,1},{4,6},{5,7},{6,4},{7,5},{8,10},{9,11},{10,... | collective-permute-start | bytes 442376 | tf_op jit(solution)/shard_map/ppermute | solution.py:474
  141.6 8.6 %collective-permute-start.14 = (f32[3,16,768]{2,1,0:T(8,128)}, f32[3,16,768]{2,1,0:T(8,128)S(1)}, u32[]{:S(2)}, u32[]{:S(2)}) collective-permute-start(f32[3,16,768]{2,1,0:T(8,128)} %get-tuple-element.40), channel_id=1, source_target_pairs={{0,3},{1,0},{2,1},{3,2},{4,7},{5,4},{6,5},{7,6},{8,11},{9,8},{10,9... | collective-permute-start | bytes 442376 | tf_op jit(solution)/shard_map/ppermute | solution.py:474
  150.2 0.9 copy-start

commit v2 on v1

--- a/solution.py
+++ b/solution.py
@@ -157,8 +157,8 @@
 def product_body(slots, places):
     def body(recv_ref, *refs):
         weight_refs, refs = refs[: len(places)], refs[len(places) :]
-        left_ref, bdown_ref, right_ref, rows_out, s, gates, ups, lows_ref, weights = refs[:9]
-        x, wide, more, sems, osems = refs[9:]
+        left_ref, bdown_ref, right_ref, rows_out, s, gates, ups, lows_ref, weights, down = refs[:10]
+        x, wide, more, sems, osems = refs[10:]
         peers = recv_ref.shape[0]
         features = x.shape[1]
         hidden = gates.shape[1]
@@ -166,7 +166,12 @@
         depth = slots * tiles
         pitch = depth + 4
         narrow = tiles + 4
-        copies = start_copies(weight_refs, places, weights, sems)
+        copies = [[], [], []]
+        for k, (ref, (m, at, size)) in enumerate(zip(weight_refs, places)):
+            to = weights.at[m] if m < 2 else down
+            copies[m].append(pltpu.make_async_copy(ref, to.at[pl.ds(at, size)], sems.at[k]))
+        for copy in copies[0]:
+            copy.start()
         for e in range(peers):
             wide[e * pitch : e * pitch + depth, :] = recv_ref[e, :depth, :].astype(F32)
         for j in range(tiles):
@@ -175,11 +180,13 @@
                     pl.ds(c * tiles + j, peers, stride=pitch), :
                 ].astype(BF16)
         chunk = hidden // slots
-        for copy in copies[0]:
-            copy.wait()
         lows = dot(x[...], left_ref[...], NT)
         lows_ref[0] = lows[:, :16].astype(BF16)
         lows_ref[1] = lows[:, 16:].astype(BF16)
+        for copy in copies[0]:
+            copy.wait()
+        for copy in copies[1]:
+            copy.start()
 
         @pl.loop(0, slots)
         def _(c):
@@ -201,7 +208,7 @@
             pltpu.make_async_copy(x, rows_out.at[0], osems.at[0]),
             pltpu.make_async_copy(s, rows_out.at[1], osems.at[1]),
         ]
-        for copy in out_copies:
+        for copy in copies[2] + out_copies:
             copy.start()
         for n in range(slots):
             cols = slice(n * chunk, (n + 1) * chunk)
@@ -209,37 +216,42 @@
                 lows_ref[1], right_ref[1, :, cols]
             )
         lows_ref[2] = dot(s[...], bdown_ref[...], NT).astype(BF16)
-        for copy in out_copies:
+        for copy in copies[2] + out_copies:
             copy.wait()
 
     return body
 
 
-def start_copies(refs, places, weights, sems):
-    copies = [[] for _ in range(weights.shape[0])]
-    for k, (ref, (m, at, size)) in enumerate(zip(refs, places)):
-        copies[m].append(pltpu.make_async_copy(ref, weights.at[m, pl.ds(at, size)], sems.at[k]))
-        copies[m][-1].start()
-    return copies
-
-
-def expert_body(slots, places):
-    def body(s, gates, ups, lows_ref, weights, *refs):
-        weight_refs, refs = refs[: len(places)], refs[len(places) :]
-        left_ref, right_ref, send_ref, acts_out, lows_out = refs[:5]
-        wide, down, acts, all_lows, backs, stage, sems, ssems, osems = refs[5:]
+def expert_body(slots):
+    def body(s, gates, ups, lows_ref, weights, near, *refs):
+        far_refs, left_ref, right_ref, send_ref, acts_out, lows_out = refs[:2], *refs[2:7]
+        wide, far, acts, all_lows, backs, stage, sems, ssems, osems = refs[7:]
         rows, features = s.shape
         hidden = gates.shape[1]
         peers = rows // slots
         tiles = features // LANES
         pitch = slots * tiles + 4
         chunk = 2 * LANES
-        for copy in start_copies(weight_refs, places, down, sems)[0]:
-            copy.wait()
+        half = far_refs[0].shape[0]
+        held = near.shape[0] // chunk * chunk
+        keep = near.shape[0] - held
+        copies = [pltpu.make_async_copy(near.at[pl.ds(held, keep)], far.at[pl.ds(0, keep)], sems.at[2])]
+        for k in range(2):
+            copies.append(
+                pltpu.make_async_copy(far_refs[k], far.at[pl.ds(keep + k * half, half)], sems.at[k])
+            )
+        for copy in copies:
+            copy.start()
         for n in range(hidden // chunk):
             cols = slice(n * chunk, (n + 1) * chunk)
             gate, up = gates[:, cols], ups[:, cols]
-            back = dot(s[...], down[0, cols, :], NT) + SCALE * dot(lows_ref[2], right_ref[2, :, cols])
+            if (n + 1) * chunk <= held:
+                down = near[cols, :]
+            else:
+                for copy in copies:
+                    copy.wait()
+                down = far[...]
+            back = dot(s[...], down, NT) + SCALE * dot(lows_ref[2], right_ref[2, :, cols])
             sigma = jax.nn.sigmoid(gate)
             active = gate * sigma
             acts[0, :, cols] = (active * up).astype(BF16)
@@ -295,7 +307,7 @@
             at = pl.multiple_of(((me_ref[0] + k) % 4) * width, width)
             for m in range(3):
                 shares[k][m, :, 0:width] = big[m, :, pl.ds(at, width)]
-                shares[k][m, :, width : width + share] = small[m, :, k * share : (k + 1) * share]
+                shares[k][m, :, width : width + share] = small[m, :, (k + 1) % 4 * share : ((k + 1) % 4 + 1) * share]
                 shares[k][m, :, width + share :] = jnp.zeros((16, 256 - share), F32)
         _, _, either, rank = choice_masks(routes_ref, experts, tokens)
         for c in range(slots):
@@ -398,17 +410,21 @@
         ahead = lax.ppermute(w, "dp", down_ring)
         far = [lax.ppermute(behind[:half], "dp", up_ring), lax.ppermute(ahead[half:], "dp", down_ring)]
         parts.append((w, ahead, behind, *far))
-    spots = ((0, share), (share, share), (3 * share, share), (2 * share, half), (2 * share + half, half))
+    spots = ((share, share), (2 * share, share), (0, share), (3 * share, half), (3 * share + half, half))
+    near = spots[:3]
 
     left = jnp.concatenate([a_gate[0].T, a_up[0].T], axis=0)
     right = jnp.stack([b_gate[0], b_up[0], a_down[0].T])
     right = lax.dynamic_slice_in_dim(
-        jnp.concatenate([right, right], axis=2), me * share, hidden, axis=2
-    )
-    row_blocks, s_rows, gates, ups, lows, both = call(
-        product_body(slots, [(m, *spot) for m in range(2) for spot in spots]),
-        (recv, *in_hbm((*parts[0], *parts[1], left, b_down[0], right))),
-        [vmem()] + [anyspace()] * 10 + [vmem()] * 3,
+        jnp.concatenate([right, right], axis=2), (me + shards - 1) % shards * share, hidden, axis=2
+    )
+    row_blocks, s_rows, gates, ups, lows, both, near_down = call(
+        product_body(
+            slots,
+            [(m, *spot) for m in range(2) for spot in spots] + [(2, *spot) for spot in near],
+        ),
+        (recv, *in_hbm((*parts[0], *parts[1], *parts[2][:3])), *in_vmem((left, b_down[0], right))),
+        [vmem()] + [anyspace()] * 13 + [vmem()] * 3,
         [
             ((2, rows, features), BF16, pltpu.HBM),
             ((rows, features), BF16, pltpu.VMEM),
@@ -416,13 +432,14 @@
             ((rows, hidden), F32, pltpu.VMEM),
             ((3, rows, rank_dim), BF16, pltpu.VMEM),
             ((2, hidden, features), BF16, pltpu.VMEM),
+            ((3 * share, features), BF16, pltpu.VMEM),
         ],
-        [anyspace()] + [vmem()] * 5,
+        [anyspace()] + [vmem()] * 6,
         [
             pltpu.VMEM((rows, features), BF16),
             pltpu.VMEM((groups * (depth + 4), LANES), F32),
             pltpu.VMEM((groups * (tiles + 4), LANES), F32),
-            pltpu.SemaphoreType.DMA((10,)),
+            pltpu.SemaphoreType.DMA((13,)),
             pltpu.SemaphoreType.DMA((2,)),
         ],
         4 * rows * hidden * features,
@@ -430,9 +447,13 @@
         12,
     )
     send_back, acts, all_lows = call(
-        expert_body(slots, [(0, *spot) for spot in spots]),
-        (*in_vmem((s_rows, gates, ups, lows, both)), *in_hbm((*parts[2], left, right))),
-        [vmem()] * 5 + [anyspace()] * 5 + [vmem()] * 2,
+        expert_body(slots),
+        (
+            *in_vmem((s_rows, gates, ups, lows, both, near_down)),
+            *in_hbm(parts[2][3:]),
+            *in_vmem((left, right)),
+        ),
+        [vmem()] * 6 + [anyspace()] * 2 + [vmem()] * 2,
         [
             ((groups, depth, LANES), BF16, pltpu.HBM),
             ((3, rows, hidden), BF16, pltpu.HBM),
@@ -441,12 +462,12 @@
         [anyspace()] * 3,
         [
             pltpu.VMEM((groups * (depth + 4), LANES), F32),
-            pltpu.VMEM((1, hidden, features), BF16),
+            pltpu.VMEM((2 * LANES, features), BF16),
             pltpu.VMEM((3, rows, hidden), BF16),
             pltpu.VMEM((5, rows, rank_dim), BF16),
             pltpu.VMEM((rows, 2 * rank_dim), BF16),
             pltpu.VMEM((groups, depth, LANES), BF16),
-            pltpu.SemaphoreType.DMA((5,)),
+            pltpu.SemaphoreType.DMA((3,)),
             pltpu.SemaphoreType.DMA((groups // 8,)),
             pltpu.SemaphoreType.DMA((2,)),
         ],

time: 176 us -> 173 us (0.983)
  Pallas kernels: 29.1 us -> 26.3 us
  other arithmetic: 2.24 us -> 0.16 us
  waiting for transfers between devices: 59.2 us -> 61.2 us
    pallas_call x6, Pallas kernels: 29.1 us -> 26.3 us  [call(): pl.pallas_call(body, out_shape=[space(s, d) for s, d, space in outs], in_...]
  transfers between devices with their start and end apart: 17 -> 17, of which waited for: 12 -> 13; matrix products, arithmetic and copies ran while one was open for 4% -> 2% of each run, Pallas kernels for 7% -> 7%
where the time goes in v2:
time: 173 us; the launch traced here: 172 us
  starting transfers between devices  78.8 us (46%)
  waiting for transfers between devices  61.2 us (35%)
  Pallas kernels  26.3 us (15%)
  local copies, waits for them, and re-layouts  4.86 us (3%)
    pallas_call x6, Pallas kernels, call(): pl.pallas_call(body, out_shape=[space(s, d) for s, d, space in outs], in_...  26.3 us
    ppermute x3, waiting for transfers between devices, layer(): behind = lax.ppermute(w, 'dp', up_ring)  23.1 us
    all_to_all x1, waiting for transfers between devices, layer(): lax.all_to_all(send_back, 'expert', split_axis=0, concat_axis=0, tiled=True)  21.6 us
    all_to_all x1, starting transfers between devices, layer(): lax.all_to_all(send, 'expert', split_axis=0, concat_axis=0, tiled=True)  17.4 us
    all_to_all x1, starting transfers between devices, layer(): lax.all_to_all(send_back, 'expert', split_axis=0, concat_axis=0, tiled=True)  13.7 us
    ppermute x3, starting transfers between devices, layer(): lax.ppermute(behind[:half], 'dp', up_ring)  11.9 us
    ppermute x3, starting transfers between devices, layer(): behind = lax.ppermute(w, 'dp', up_ring)  10.8 us
    ppermute x3, starting transfers between devices, layer(): ahead = lax.ppermute(w, 'dp', down_ring)  8.42 us
  transfers between devices with their start and end apart: 17, of which 13 were waited for; matrix products, arithmetic and copies ran while one was open for 2% of the time, Pallas kernels for 7%

profile of v2, /device:TPU:14, one launch (start us, length us, event | category | flops | bytes accessed | tf_op | source)
XLA Modules:
  0.0 172.3 jit_solution(12831134848428188051)
XLA Ops:
  0.6 4.7 %shard_map.189 = bf16[128,96,128]{2,1,0:T(8,128)(2,1)} custom-call(s32[2,128]{1,0:T(2,128)} %bitcast.54, s32[2,128]{1,0:T(2,128)} %bitcast.56, s32[1,32]{1,0:T(1,128)} %lengths_ref.1, s32[1]{0:T(128)} %bitcast.4.start_ref, bf16[128,2048]{1,0:T(8,128)(2,1)} %bitcast.48, bf16[128,2048]{1,0:T(8,128)(2,1)} %bitcast.49), custom_call_target="tpu_custom_call" | custom-call | flops 402653184 | bytes 3145728 | tf_op jit(solution)/shard_map/pallas_call | solution.py:44
  5.4 17.4 %all-to-all-start = ((bf16[128,96,128]{2,1,0:T(8,128)(2,1)}), bf16[128,96,128]{2,1,0:T(8,128)(2,1)S(1)}, u32[]{:S(2)}, u32[]{:S(2)}) async-start(bf16[128,96,128]{2,1,0:T(8,128)(2,1)} %shard_map.189), calls=%async_computation | async-start | bytes 6291456 | tf_op jit(solution)/shard_map/all_to_all | solution.py:404
  22.7 2.4 %collective-permute-start.1 = (bf16[192,2048]{1,0:T(8,128)(2,1)}, bf16[192,2048]{1,0:T(8,128)(2,1)S(1)}, u32[]{:S(2)}, u32[]{:S(2)}) collective-permute-start(bf16[192,2048]{1,0:T(8,128)(2,1)} %bitcast.39), channel_id=1, source_target_pairs={{0,1},{1,2},{2,3},{3,0},{4,5},{5,6},{6,7},{7,4},{8,9},{9,10},{10,1... | collective-permute-start | bytes 2359304 | tf_op jit(solution)/shard_map/ppermute | solution.py:409
  25.1 3.5 %collective-permute-start = (bf16[192,2048]{1,0:T(8,128)(2,1)}, bf16[192,2048]{1,0:T(8,128)(2,1)S(1)}, u32[]{:S(2)}, u32[]{:S(2)}) collective-permute-start(bf16[192,2048]{1,0:T(8,128)(2,1)} %bitcast.40), channel_id=1, source_target_pairs={{0,3},{1,0},{2,1},{3,2},{4,7},{5,4},{6,5},{7,6},{8,11},{9,8},{10,9... | collective-permute-start | bytes 2359304 | tf_op jit(solution)/shard_map/ppermute | solution.py:410
  28.6 3.6 %collective-permute-start.5 = (bf16[192,2048]{1,0:T(8,128)(2,1)}, bf16[192,2048]{1,0:T(8,128)(2,1)S(1)}, u32[]{:S(2)}, u32[]{:S(2)}) collective-permute-start(bf16[192,2048]{1,0:T(8,128)(2,1)} %bitcast.42), channel_id=1, source_target_pairs={{0,1},{1,2},{2,3},{3,0},{4,5},{5,6},{6,7},{7,4},{8,9},{9,10},{10,1... | collective-permute-start | bytes 2359304 | tf_op jit(solution)/shard_map/ppermute | solution.py:409
  32.2 2.2 %collective-permute-start.4 = (bf16[192,2048]{1,0:T(8,128)(2,1)}, bf16[192,2048]{1,0:T(8,128)(2,1)S(1)}, u32[]{:S(2)}, u32[]{:S(2)}) collective-permute-start(bf16[192,2048]{1,0:T(8,128)(2,1)} %bitcast.43), channel_id=1, source_target_pairs={{0,3},{1,0},{2,1},{3,2},{4,7},{5,4},{6,5},{7,6},{8,11},{9,8},{10,9... | collective-permute-start | bytes 2359304 | tf_op jit(solution)/shard_map/ppermute | solution.py:410
  34.5 4.8 %collective-permute-start.9 = (bf16[192,2048]{1,0:T(8,128)(2,1)}, bf16[192,2048]{1,0:T(8,128)(2,1)S(1)}, u32[]{:S(2)}, u32[]{:S(2)}) collective-permute-start(bf16[192,2048]{1,0:T(8,128)(2,1)} %bitcast.45), channel_id=1, source_target_pairs={{0,1},{1,2},{2,3},{3,0},{4,5},{5,6},{6,7},{7,4},{8,9},{9,10},{10,1... | collective-permute-start | bytes 2359304 | tf_op jit(solution)/shard_map/ppermute | solution.py:409
  39.3 6.0 %collective-permute-done.1.refs_2_ = bf16[192,2048]{1,0:T(8,128)(2,1)S(1)} collective-permute-done((bf16[192,2048]{1,0:T(8,128)(2,1)}, bf16[192,2048]{1,0:T(8,128)(2,1)S(1)}, u32[]{:S(2)}, u32[]{:S(2)}) %collective-permute-start.1) | collective-permute-done | bytes 786464 | tf_op jit(solution)/shard_map/ppermute | solution.py:409
  45.3 2.7 %collective-permute-start.8 = (bf16[192,2048]{1,0:T(8,128)(2,1)}, bf16[192,2048]{1,0:T(8,128)(2,1)S(1)}, u32[]{:S(2)}, u32[]{:S(2)}) collective-permute-start(bf16[192,2048]{1,0:T(8,128)(2,1)} %bitcast.46), channel_id=1, source_target_pairs={{0,3},{1,0},{2,1},{3,2},{4,7},{5,4},{6,5},{7,6},{8,11},{9,8},{10,9... | collective-permute-start | bytes 2359304 | tf_op jit(solution)/shard_map/ppermute | solution.py:410
  48.0 0.8 collective-permute-done.refs_1_
  48.9 3.5 %collective-permute-start.2 = (bf16[96,2048]{1,0:T(8,128)(2,1)S(1)}, bf16[96,2048]{1,0:T(8,128)(2,1)S(1)}, u32[]{:S(2)}, u32[]{:S(2)}) collective-permute-start(bf16[96,2048]{1,0:T(8,128)(2,1)S(1)} %slice.24), channel_id=1, source_target_pairs={{0,1},{1,2},{2,3},{3,0},{4,5},{5,6},{6,7},{7,4},{8,9},{9,10},{10,1... | collective-permute-start | bytes 1179656 | tf_op jit(solution)/shard_map/ppermute | solution.py:411
  52.4 0.8 slice.25
  53.2 0.0 copy-start.14
  53.2 0.0 copy-start.2
  53.2 8.9 %collective-permute-done.5.refs_7_ = bf16[192,2048]{1,0:T(8,128)(2,1)S(1)} collective-permute-done((bf16[192,2048]{1,0:T(8,128)(2,1)}, bf16[192,2048]{1,0:T(8,128)(2,1)S(1)}, u32[]{:S(2)}, u32[]{:S(2)}) %collective-permute-start.5) | collective-permute-done | bytes 786464 | tf_op jit(solution)/shard_map/ppermute | solution.py:409
  62.1 2.7 %collective-permute-start.3 = (bf16[96,2048]{1,0:T(8,128)(2,1)}, bf16[96,2048]{1,0:T(8,128)(2,1)}, u32[]{:S(2)}, u32[]{:S(2)}) collective-permute-start(bf16[96,2048]{1,0:T(8,128)(2,1)} %slice.25), channel_id=1, source_target_pairs={{0,3},{1,0},{2,1},{3,2},{4,7},{5,4},{6,5},{7,6},{8,11},{9,8},{10,9... | collective-permute-start | bytes 1179656 | tf_op jit(solution)/shard_map/ppermute | solution.py:411
  64.8 0.8 slice.26
  65.6 0.1 collective-permute-done.4.refs_6_
  65.7 4.2 %collective-permute-start.6 = (bf16[96,2048]{1,0:T(8,128)(2,1)}, bf16[96,2048]{1,0:T(8,128)(2,1)}, u32[]{:S(2)}, u32[]{:S(2)}) collective-permute-start(bf16[96,2048]{1,0:T(8,128)(2,1)} %slice.26), channel_id=1, source_target_pairs={{0,1},{1,2},{2,3},{3,0},{4,5},{5,6},{6,7},{7,4},{8,9},{9,10},{10,1... | collective-permute-start | bytes 1179656 | tf_op jit(solution)/shard_map/ppermute | solution.py:411
  69.9 0.8 slice.27
  70.7 8.2 %collective-permute-done.9.refs_12_ = bf16[192,2048]{1,0:T(8,128)(2,1)S(1)} collective-permute-done((bf16[192,2048]{1,0:T(8,128)(2,1)}, bf16[192,2048]{1,0:T(8,128)(2,1)S(1)}, u32[]{:S(2)}, u32[]{:S(2)}) %collective-permute-start.9) | collective-permute-done | bytes 786464 | tf_op jit(solution)/shard_map/ppermute | solution.py:409
  79.0 2.7 %collective-permute-start.7 = (bf16[96,2048]{1,0:T(8,128)(2,1)}, bf16[96,2048]{1,0:T(8,128)(2,1)}, u32[]{:S(2)}, u32[]{:S(2)}) collective-permute-start(bf16[96,2048]{1,0:T(8,128)(2,1)} %slice.27), channel_id=1, source_target_pairs={{0,3},{1,0},{2,1},{3,2},{4,7},{5,4},{6,5},{7,6},{8,11},{9,8},{10,9... | collective-permute-start | bytes 1179656 | tf_op jit(solution)/shard_map/ppermute | solution.py:411
  81.7 0.8 slice.28
  82.5 0.0 copy-done.3
  82.5 0.1 collective-permute-done.8.refs_11_
  82.6 4.2 %collective-permute-start.10 = (bf16[96,2048]{1,0:T(8,128)(2,1)}, bf16[96,2048]{1,0:T(8,128)(2,1)}, u32[]{:S(2)}, u32[]{:S(2)}) collective-permute-start(bf16[96,2048]{1,0:T(8,128)(2,1)} %slice.28), channel_id=1, source_target_pairs={{0,1},{1,2},{2,3},{3,0},{4,5},{5,6},{6,7},{7,4},{8,9},{9,10},{10,1... | collective-permute-start | bytes 1179656 | tf_op jit(solution)/shard_map/ppermute | solution.py:411
  86.8 0.8 slice.29
  87.6 0.0 copy-done.4
  87.6 0.0 collective-permute-done.2.refs_3_
  87.6 2.7 %collective-permute-start.11 = (bf16[96,2048]{1,0:T(8,128)(2,1)}, bf16[96,2048]{1,0:T(8,128)(2,1)}, u32[]{:S(2)}, u32[]{:S(2)}) collective-permute-start(bf16[96,2048]{1,0:T(8,128)(2,1)} %slice.29), channel_id=1, source_target_pairs={{0,3},{1,0},{2,1},{3,2},{4,7},{5,4},{6,5},{7,6},{8,11},{9,8},{10,9... | collective-permute-start | bytes 1179656 | tf_op jit(solution)/shard_map/ppermute | solution.py:411
  90.3 0.0 copy-done.5
  90.3 0.0 copy-done.6
  90.3 0.0 copy-done.7
  90.3 0.0 copy-done.8
  90.3 0.0 copy-done.9
  90.4 0.0 copy-done.10
  90.4 0.0 copy-done.11
  90.4 0.0 copy-done.12
  90.4 0.0 copy-done.13
  90.4 0.0 copy-done.14
  90.4 0.2 fusion.2.refs_15_.refs_3_.right_ref
  90.6 0.0 copy-start
  90.6 0.5 collective-permute-done.3.refs_4_
  91.1 4.8 %collective-permute-done.6.refs_8_ = bf16[96,2048]{1,0:T(8,128)(2,1)} collective-permute-done((bf16[96,2048]{1,0:T(8,128)(2,1)}, bf16[96,2048]{1,0:T(8,128)(2,1)}, u32[]{:S(2)}, u32[]{:S(2)}) %collective-permute-start.6) | collective-permute-done | bytes 393248 | tf_op jit(solution)/shard_map/ppermute | solution.py:411
  95.9 3.6 %collective-permute-done.7.refs_9_ = bf16[96,2048]{1,0:T(8,128)(2,1)} collective-permute-done((bf16[96,2048]{1,0:T(8,128)(2,1)}, bf16[96,2048]{1,0:T(8,128)(2,1)}, u32[]{:S(2)}, u32[]{:S(2)}) %collective-permute-start.7) | collective-permute-done | bytes 393248 | tf_op jit(solution)/shard_map/ppermute | solution.py:411
  99.5 0.0 all-to-all-done.recv_ref
  99.5 0.0 copy-done.2
  99.5 7.5 %shard_map.190 = (bf16[2,384,2048]{2,1,0:T(8,128)(2,1)}, bf16[384,2048]{1,0:T(8,128)(2,1)S(1)}, f32[384,768]{1,0:T(8,128)S(1)}, f32[384,768]{1,0:T(8,128)S(1)}, ...) custom-call(bf16[128,96,128]{2,1,0:T(8,128)(2,1)S(1)} %all-to-all-done.recv_ref, ...), custom_call_target="tpu_custom_call" | custom-call | flops 2415919104 | bytes 9437184 | tf_op jit(solution)/shard_map/pallas_call | solution.py:44
  107.0 0.0 collective-permute-done.10.refs_0_
  107.0 0.0 collective-permute-done.11.refs_1_
  107.0 0.0 copy-done
  107.0 7.3 %shard_map.191 = (bf16[128,48,128]{2,1,0:T(8,128)(2,1)}, bf16[3,384,768]{2,1,0:T(8,128)(2,1)}, bf16[5,384,16]{2,1,0:T(8,128)(2,1)}) custom-call(bf16[384,2048]{1,0:T(8,128)(2,1)S(1)} %get-tuple-element.28.s, f32[384,768]{1,0:T(8,128)S(1)} %get-tuple-element.29.gates, f32[384,768]{1,0:T(8,128)S(1)} %get-tuple-element.30.ups, ...), custom_call_target="tpu_custom_call" | custom-call | flops 3623878656 | bytes 4718592 | tf_op jit(solution)/shard_map/pallas_call | solution.py:44
  114.4 13.7 %all-to-all-start.1 = ((bf16[128,48,128]{2,1,0:T(8,128)(2,1)}), bf16[128,48,128]{2,1,0:T(8,128)(2,1)S(1)}, u32[]{:S(2)}, u32[]{:S(2)}) async-start(bf16[128,48,128]{2,1,0:T(8,128)(2,1)} %get-tuple-element.34), calls=%async_computation.1 | async-start | bytes 3145728 | tf_op jit(solution)/shard_map/all_to_all | solution.py:478
  128.1 4.5 %shard_map.192 = (f32[3,16,768]{2,1,0:T(8,128)}, f32[3,16,768]{2,1,0:T(8,128)}, f32[3,16,768]{2,1,0:T(8,128)}, f32[3,16,768]{2,1,0:T(8,128)}, bf16[128,384]{1,0:T(8,128)(2,1)S(1)}) custom-call(s32[1]{0:T(128)} %bitcast.18.me_ref, s32[2,128]{1,0:T(2,128)} %bitcast.55, bf16[2,384,2048]{2,1,0:T(8,128)(2,1)} %get-tuple-element.35.rows_ref, ...), custom_call_target="tpu_custom_call" | custom-call | flops 150994944 | bytes 3145728 | tf_op jit(solution)/shard_map/pallas_call | solution.py:44
  132.6 2.2 %collective-permute-start.12 = (f32[3,16,768]{2,1,0:T(8,128)}, f32[3,16,768]{2,1,0:T(8,128)S(1)}, u32[]{:S(2)}, u32[]{:S(2)}) collective-permute-start(f32[3,16,768]{2,1,0:T(8,128)} %get-tuple-element.40), channel_id=1, source_target_pairs={{0,1},{1,2},{2,3},{3,0},{4,5},{5,6},{6,7},{7,4},{8,9},{9,10},{10,1... | collective-permute-start | bytes 442376 | tf_op jit(solution)/shard_map/ppermute | solution.py:495
  134.8 4.0 %collective-permute-start.13 = (f32[3,16,768]{2,1,0:T(8,128)}, f32[3,16,768]{2,1,0:T(8,128)S(1)}, u32[]{:S(2)}, u32[]{:S(2)}) collective-permute-start(f32[3,16,768]{2,1,0:T(8,128)} %get-tuple-element.41), channel_id=1, source_target_pairs={{0,2},{1,3},{2,0},{3,1},{4,6},{5,7},{6,4},{7,5},{8,10},{9,11},{10,... | collective-permute-start | bytes 442376 | tf_op jit(solution)/shard_map/ppermute | solution.py:495
  138.8 2.1 %collective-permute-start.14 = (f32[3,16,768]{2,1,0:T(8,128)}, f32[3,16,768]{2,1,0:T(8,128)S(1)}, u32[]{:S(2)}, u32[]{:S(2)}) collective-permute-start(f32[3,16,768]{2,1,0:T(8,128)} %get-tuple-element.42), channel_id=1, source_target_pairs={{0,3},{1,0},{2,1},{3,2},{4,7},{5,4},{6,5},{7,6},{8,11},{9,8},{10,9... | collective-permute-start | bytes 442376 | tf_op jit(solution)/shard_map/ppermute | solution.py:495
  141.0 0.5 collective-permute-done.12.b_ref
  141.4 2.6 %collective-permute-done.13.c_ref = f32[3,16,768]{2,1,0:T(8,128)S(1)} collective-permute-done((f32[3,16,768]{2,1,0:T(8,128)}, f32[3,16,768]{2,1,0:T(8,128)S(1)}, u32[]{:S(2)}, u32[]{:S(2)}) %collective-permute-start.13) | collective-permute-done | bytes 147488 | tf_op jit(solution)/shard_map/ppermute | solution.py:495
  144.0 3.4 %collective-permute-done.14.d_ref = f32[3,16,768]{2,1,0:T(8,128)S(1)} collective-permute-done((f32[3,16,768]{2,1,0:T(8,128)}, f32[3,16,768]{2,1,0:T(8,128)S(1)}, u32[]{:S(2)}, u32[]{:S(2)}) %collective-permute-start.14) | collective-permute-done | bytes 147488 | tf_op jit(solution)/shard_map/ppermute | solution.py:495
  147.4 0.9 copy-done.1
  148.4 0.7 shard_map.194
  149.0 21.6 %all-to-all-done.1.back_ref = bf16[128,48,128]{2,1,0:T(8,128)(2,1)S(1)} async-done(((bf16[128,48,128]{2,1,0:T(8,128)(2,1)}), bf16[128,48,128]{2,1,0:T(8,128)(2,1)S(1)}, u32[]{:S(2)}, u32[]{:S(2)}) %all-to-all-start.1) | async-done | bytes 1572896 | tf_op jit(solution)/shard_map/all_to_all | solution.py:478
  170.7 1.6 shard_map.193
  (14 shorter events, 0.1 us)
Async XLA Ops:
  5.4 94.2 %all-to-all-start = ((bf16[128,96,128]{2,1,0:T(8,128)(2,1)}), bf16[128,96,128]{2,1,0:T(8,128)(2,1)S(1)}, u32[]{:S(2)}, u32[]{:S(2)}) async-start(bf16[128,96,128]{2,1,0:T(8,128)(2,1)} %shard_map.189), calls=%async_computation | async-start | bytes 6291456 | tf_op jit(solution)/shard_map/all_to_all | solution.py:404
  22.7 22.5 %collective-permute-start.1 = (bf16[192,2048]{1,0:T(8,128)(2,1)}, bf16[192,2048]{1,0:T(8,128)(2,1)S(1)}, u32[]{:S(2)}, u32[]{:S(2)}) collective-permute-start(bf16[192,2048]{1,0:T(8,128)(2,1)} %bitcast.39), channel_id=1, source_target_pairs={{0,1},{1,2},{2,3},{3,0},{4,5},{5,6},{6,7},{7,4},{8,9},{9,10},{10,1... | collective-permute-start | bytes 2359304 | tf_op jit(solution)/shard_map/ppermute | solution.py:409
  25.1 23.7 %collective-permute-start = (bf16[192,2048]{1,0:T(8,128)(2,1)}, bf16[192,2048]{1,0:T(8,128)(2,1)S(1)}, u32[]{:S(2)}, u32[]{:S(2)}) collective-permute-start(bf16[192,2048]{1,0:T(8,128)(2,1)} %bitcast.40), channel_id=1, source_target_pairs={{0,3},{1,0},{2,1},{3,2},{4,7},{5,4},{6,5},{7,6},{8,11},{9,8},{10,9... | collective-permute-start | bytes 2359304 | tf_op jit(solution)/shard_map/ppermute | solution.py:410
  28.6 33.5 %collective-permute-start.5 = (bf16[192,2048]{1,0:T(8,128)(2,1)}, bf16[192,2048]{1,0:T(8,128)(2,1)S(1)}, u32[]{:S(2)}, u32[]{:S(2)}) collective-permute-start(bf16[192,2048]{1,0:T(8,128)(2,1)} %bitcast.42), channel_id=1, source_target_pairs={{0,1},{1,2},{2,3},{3,0},{4,5},{5,6},{6,7},{7,4},{8,9},{9,10},{10,1... | collective-permute-start | bytes 2359304 | tf_op jit(solution)/shard_map/ppermute | solution.py:409
  32.2 33.5 %collective-permute-start.4 = (bf16[192,2048]{1,0:T(8,128)(2,1)}, bf16[192,2048]{1,0:T(8,128)(2,1)S(1)}, u32[]{:S(2)}, u32[]{:S(2)}) collective-permute-start(bf16[192,2048]{1,0:T(8,128)(2,1)} %bitcast.43), channel_id=1, source_target_pairs={{0,3},{1,0},{2,1},{3,2},{4,7},{5,4},{6,5},{7,6},{8,11},{9,8},{10,9... | collective-permute-start | bytes 2359304 | tf_op jit(solution)/shard_map/ppermute | solution.py:410
  34.5 44.5 %collective-permute-start.9 = (bf16[192,2048]{1,0:T(8,128)(2,1)}, bf16[192,2048]{1,0:T(8,128)(2,1)S(1)}, u32[]{:S(2)}, u32[]{:S(2)}) collective-permute-start(bf16[192,2048]{1,0:T(8,128)(2,1)} %bitcast.45), channel_id=1, source_target_pairs={{0,1},{1,2},{2,3},{3,0},{4,5},{5,6},{6,7},{7,4},{8,9},{9,10},{10,1... | collective-permute-start | bytes 2359304 | tf_op jit(solution)/shard_map/ppermute | solution.py:409
  45.3 37.2 %copy-start.3 = (bf16[192,2048]{1,0:T(8,128)(2,1)}, bf16[192,2048]{1,0:T(8,128)(2,1)S(1)}, u32[]{:S(2)}) copy-start(bf16[192,2048]{1,0:T(8,128)(2,1)S(1)} %collective-permute-done.1.refs_2_) | copy-start | bytes 2359300
  45.3 37.3 %collective-permute-start.8 = (bf16[192,2048]{1,0:T(8,128)(2,1)}, bf16[192,2048]{1,0:T(8,128)(2,1)S(1)}, u32[]{:S(2)}, u32[]{:S(2)}) collective-permute-start(bf16[192,2048]{1,0:T(8,128)(2,1)} %bitcast.46), channel_id=1, source_target_pairs={{0,3},{1,0},{2,1},{3,2},{4,7},{5,4},{6,5},{7,6},{8,11},{9,8},{10,9... | collective-permute-start | bytes 2359304 | tf_op jit(solution)/shard_map/ppermute | solution.py:410
  48.9 38.7 %copy-start.4 = (bf16[192,2048]{1,0:T(8,128)(2,1)}, bf16[192,2048]{1,0:T(8,128)(2,1)S(1)}, u32[]{:S(2)}) copy-start(bf16[192,2048]{1,0:T(8,128)(2,1)S(1)} %collective-permute-done.refs_1_) | copy-start | bytes 2359300
  48.9 38.7 %collective-permute-start.2 = (bf16[96,2048]{1,0:T(8,128)(2,1)S(1)}, bf16[96,2048]{1,0:T(8,128)(2,1)S(1)}, u32[]{:S(2)}, u32[]{:S(2)}) collective-permute-start(bf16[96,2048]{1,0:T(8,128)(2,1)S(1)} %slice.24), channel_id=1, source_target_pairs={{0,1},{1,2},{2,3},{3,0},{4,5},{5,6},{6,7},{7,4},{8,9},{9,10},{10,1... | collective-permute-start | bytes 1179656 | tf_op jit(solution)/shard_map/ppermute | solution.py:411
  53.1 37.2 %copy-start.10 = (bf16[1,2048,16]{1,2,0:T(8,128)(2,1)S(1)}, bf16[1,2048,16]{1,2,0:T(8,128)(2,1)}, u32[]{:S(2)}) copy-start(bf16[1,2048,16]{1,2,0:T(8,128)(2,1)} %param.24) | copy-start | bytes 196612
  53.1 37.2 %copy-start.11 = (bf16[1,2048,16]{1,2,0:T(8,128)(2,1)S(1)}, bf16[1,2048,16]{1,2,0:T(8,128)(2,1)}, u32[]{:S(2)}) copy-start(bf16[1,2048,16]{1,2,0:T(8,128)(2,1)} %param.22) | copy-start | bytes 196612
  53.1 37.3 %copy-start.12 = (bf16[1,16,768]{2,1,0:T(8,128)(2,1)S(1)}, bf16[1,16,768]{2,1,0:T(8,128)(2,1)}, u32[]{:S(2)}) copy-start(bf16[1,16,768]{2,1,0:T(8,128)(2,1)} %param.23) | copy-start | bytes 73732
  53.1 37.3 %copy-start.13 = (bf16[1,16,768]{2,1,0:T(8,128)(2,1)S(1)}, bf16[1,16,768]{2,1,0:T(8,128)(2,1)}, u32[]{:S(2)}) copy-start(bf16[1,16,768]{2,1,0:T(8,128)(2,1)} %param.25) | copy-start | bytes 73732
  53.2 37.3 %copy-start.14 = (bf16[1,768,16]{1,2,0:T(8,128)(2,1)S(1)}, bf16[1,768,16]{1,2,0:T(8,128)(2,1)}, u32[]{:S(2)}) copy-start(bf16[1,768,16]{1,2,0:T(8,128)(2,1)} %param.26) | copy-start | bytes 73732
  53.2 46.4 %copy-start.2 = (bf16[1,16,2048]{2,1,0:T(8,128)(2,1)S(1)}, bf16[1,16,2048]{2,1,0:T(8,128)(2,1)}, u32[]{:S(2)}) copy-start(bf16[1,16,2048]{2,1,0:T(8,128)(2,1)} %param.27) | copy-start | bytes 196612
  62.1 28.2 %copy-start.5 = (bf16[192,2048]{1,0:T(8,128)(2,1)}, bf16[192,2048]{1,0:T(8,128)(2,1)S(1)}, u32[]{:S(2)}) copy-start(bf16[192,2048]{1,0:T(8,128)(2,1)S(1)} %collective-permute-done.5.refs_7_) | copy-start | bytes 2359300
  62.1 29.0 %collective-permute-start.3 = (bf16[96,2048]{1,0:T(8,128)(2,1)}, bf16[96,2048]{1,0:T(8,128)(2,1)}, u32[]{:S(2)}, u32[]{:S(2)}) collective-permute-start(bf16[96,2048]{1,0:T(8,128)(2,1)} %slice.25), channel_id=1, source_target_pairs={{0,3},{1,0},{2,1},{3,2},{4,7},{5,4},{6,5},{7,6},{8,11},{9,8},{10,9... | collective-permute-start | bytes 1179656 | tf_op jit(solution)/shard_map/ppermute | solution.py:411
  65.7 24.6 %copy-start.6 = (bf16[192,2048]{1,0:T(8,128)(2,1)}, bf16[192,2048]{1,0:T(8,128)(2,1)S(1)}, u32[]{:S(2)}) copy-start(bf16[192,2048]{1,0:T(8,128)(2,1)S(1)} %collective-permute-done.4.refs_6_) | copy-start | bytes 2359300
  65.7 30.2 %collective-permute-start.6 = (bf16[96,2048]{1,0:T(8,128)(2,1)}, bf16[96,2048]{1,0:T(8,128)(2,1)}, u32[]{:S(2)}, u32[]{:S(2)}) collective-permute-start(bf16[96,2048]{1,0:T(8,128)(2,1)} %slice.26), channel_id=1, source_target_pairs={{0,1},{1,2},{2,3},{3,0},{4,5},{5,6},{6,7},{7,4},{8,9},{9,10},{10,1... | collective-permute-start | bytes 1179656 | tf_op jit(solution)/shard_map/ppermute | solution.py:411
  79.0 11.4 %copy-start.7 = (bf16[192,2048]{1,0:T(8,128)(2,1)}, bf16[192,2048]{1,0:T(8,128)(2,1)S(1)}, u32[]{:S(2)}) copy-start(bf16[192,2048]{1,0:T(8,128)(2,1)S(1)} %collective-permute-done.9.refs_12_) | copy-start | bytes 2359300
  79.0 20.6 %collective-permute-start.7 = (bf16[96,2048]{1,0:T(8,128)(2,1)}, bf16[96,2048]{1,0:T(8,128)(2,1)}, u32[]{:S(2)}, u32[]{:S(2)}) collective-permute-start(bf16[96,2048]{1,0:T(8,128)(2,1)} %slice.27), channel_id=1, source_target_pairs={{0,3},{1,0},{2,1},{3,2},{4,7},{5,4},{6,5},{7,6},{8,11},{9,8},{10,9... | collective-permute-start | bytes 1179656 | tf_op jit(solution)/shard_map/ppermute | solution.py:411
  82.6 7.8 %copy-start.8 = (bf16[192,2048]{1,0:T(8,128)(2,1)}, bf16[192,2048]{1,0:T(8,128)(2,1)S(1)}, u32[]{:S(2)}) copy-start(bf16[192,2048]{1,0:T(8,128)(2,1)S(1)} %collective-permute-done.8.refs_11_) | copy-start | bytes 2359300
  82.6 24.4 %collective-permute-start.10 = (bf16[96,2048]{1,0:T(8,128)(2,1)}, bf16[96,2048]{1,0:T(8,128)(2,1)}, u32[]{:S(2)}, u32[]{:S(2)}) collective-permute-start(bf16[96,2048]{1,0:T(8,128)(2,1)} %slice.28), channel_id=1, source_target_pairs={{0,1},{1,2},{2,3},{3,0},{4,5},{5,6},{6,7},{7,4},{8,9},{9,10},{10,1... | collective-permute-start | bytes 1179656 | tf_op jit(solution)/shard_map/ppermute | solution.py:411
  87.6 2.8 %copy-start.9 = (bf16[96,2048]{1,0:T(8,128)(2,1)}, bf16[96,2048]{1,0:T(8,128)(2,1)S(1)}, u32[]{:S(2)}) copy-start(bf16[96,2048]{1,0:T(8,128)(2,1)S(1)} %collective-permute-done.2.refs_3_) | copy-start | bytes 1179652
  87.6 19.4 %collective-permute-start.11 = (bf16[96,2048]{1,0:T(8,128)(2,1)}, bf16[96,2048]{1,0:T(8,128)(2,1)}, u32[]{:S(2)}, u32[]{:S(2)}) collective-permute-start(bf16[96,2048]{1,0:T(8,128)(2,1)} %slice.29), channel_id=1, source_target_pairs={{0,3},{1,0},{2,1},{3,2},{4,7},{5,4},{6,5},{7,6},{8,11},{9,8},{10,9... | collective-permute-start | bytes 1179656 | tf_op jit(solution)/shard_map/ppermute | solution.py:411
  90.6 16.4 %copy-start = (bf16[3,16,768]{2,1,0:T(8,128)(2,1)}, bf16[3,16,768]{2,1,0:T(8,128)(2,1)S(1)}, u32[]{:S(2)}) copy-start(bf16[3,16,768]{2,1,0:T(8,128)(2,1)S(1)} %fusion.2.refs_15_.refs_3_.right_ref) | copy-start | bytes 221188
  114.4 56.3 %all-to-all-start.1 = ((bf16[128,48,128]{2,1,0:T(8,128)(2,1)}), bf16[128,48,128]{2,1,0:T(8,128)(2,1)S(1)}, u32[]{:S(2)}, u32[]{:S(2)}) async-start(bf16[128,48,128]{2,1,0:T(8,128)(2,1)} %get-tuple-element.34), calls=%async_computation.1 | async-start | bytes 3145728 | tf_op jit(solution)/shard_map/all_to_all | solution.py:478
  132.6 8.8 %collective-permute-start.12 = (f32[3,16,768]{2,1,0:T(8,128)}, f32[3,16,768]{2,1,0:T(8,128)S(1)}, u32[]{:S(2)}, u32[]{:S(2)}) collective-permute-start(f32[3,16,768]{2,1,0:T(8,128)} %get-tuple-element.40), channel_id=1, source_target_pairs={{0,1},{1,2},{2,3},{3,0},{4,5},{5,6},{6,7},{7,4},{8,9},{9,10},{10,1... | collective-permute-start | bytes 442376 | tf_op jit(solution)/shard_map/ppermute | solution.py:495
  134.8 9.2 %collective-permute-start.13 = (f32[3,16,768]{2,1,0:T(8,128)}, f32[3,16,768]{2,1,0:T(8,128)S(1)}, u32[]{:S(2)}, u32[]{:S(2)}) collective-permute-start(f32[3,16,768]{2,1,0:T(8,128)} %get-tuple-element.41), channel_id=1, source_target_pairs={{0,2},{1,3},{2,0},{3,1},{4,6},{5,7},{6,4},{7,5},{8,10},{9,11},{10,... | collective-permute-start | bytes 442376 | tf_op jit(solution)/shard_map/ppermute | solution.py:495
  138.8 8.6 %collective-permute-start.14 = (f32[3,16,768]{2,1,0:T(8,128)}, f32[3,16,768]{2,1,0:T(8,128)S(1)}, u32[]{:S(2)}, u32[]{:S(2)}) collective-permute-start(f32[3,16,768]{2,1,0:T(8,128)} %get-tuple-element.42), channel_id=1, source_target_pairs={{0,3},{1,0},{2,1},{3,2},{4,7},{5,4},{6,5},{7,6},{8,11},{9,8},{10,9... | collective-permute-start | bytes 442376 | tf_op jit(solution)/shard_map/ppermute | solution.py:495
  147.4 0.9 copy-start.1

commit v3 on v2

--- a/solution.py
+++ b/solution.py
@@ -94,13 +94,19 @@
 
 
 def dispatch_body(slots, group_tokens, doc_count):
-    def body(routes_ref, nums_ref, lengths_ref, start_ref, x_hbm, g_hbm, send_ref, wide, more, stage, x_ref, g_ref, lsems, sems):
+    def body(start_ref, x_hbm, g_hbm, routes_hbm, nums_hbm, lengths_hbm, send_ref, *scratches):
+        wide, more, stage, x_ref, g_ref, routes_ref, nums_ref, lengths_ref, lsems, sems = scratches
         loads = [
-            pltpu.make_async_copy(x_hbm, x_ref, lsems.at[0]),
-            pltpu.make_async_copy(g_hbm, g_ref, lsems.at[1]),
+            pltpu.make_async_copy(routes_hbm, routes_ref, lsems.at[0]),
+            pltpu.make_async_copy(nums_hbm, nums_ref, lsems.at[1]),
+            pltpu.make_async_copy(lengths_hbm, lengths_ref, lsems.at[2]),
+            pltpu.make_async_copy(x_hbm, x_ref, lsems.at[3]),
+            pltpu.make_async_copy(g_hbm, g_ref, lsems.at[4]),
         ]
         for load in loads:
             load.start()
+        for load in loads[:3]:
+            load.wait()
         experts = stage.shape[0]
         tokens, features = x_ref.shape
         tiles = features // LANES
@@ -127,7 +133,7 @@
         chunk = 2 * LANES
         copies = []
         for side, (source, scratch) in enumerate(((x_ref, wide), (g_ref, more))):
-            loads[side].wait()
+            loads[3 + side].wait()
             for j in range(features // chunk):
                 part = dot(pick, source[:, j * chunk : (j + 1) * chunk])
                 if side == 1:
@@ -165,43 +171,36 @@
         tiles = features // LANES
         depth = slots * tiles
         pitch = depth + 4
-        narrow = tiles + 4
         copies = [[], [], []]
         for k, (ref, (m, at, size)) in enumerate(zip(weight_refs, places)):
             to = weights.at[m] if m < 2 else down
             copies[m].append(pltpu.make_async_copy(ref, to.at[pl.ds(at, size)], sems.at[k]))
         for copy in copies[0]:
             copy.start()
-        for e in range(peers):
-            wide[e * pitch : e * pitch + depth, :] = recv_ref[e, :depth, :].astype(F32)
-        for j in range(tiles):
-            for c in range(slots):
-                x[c * peers : (c + 1) * peers, j * LANES : (j + 1) * LANES] = wide[
-                    pl.ds(c * tiles + j, peers, stride=pitch), :
-                ].astype(BF16)
-        chunk = hidden // slots
+        for side, (scratch, rows) in enumerate(((wide, x), (more, s))):
+            for e in range(peers):
+                scratch[e * pitch : e * pitch + depth, :] = recv_ref[
+                    e, side * depth : (side + 1) * depth, :
+                ].astype(F32)
+            for j in range(tiles):
+                for c in range(slots):
+                    rows[c * peers : (c + 1) * peers, j * LANES : (j + 1) * LANES] = scratch[
+                        pl.ds(c * tiles + j, peers, stride=pitch), :
+                    ].astype(BF16)
         lows = dot(x[...], left_ref[...], NT)
         lows_ref[0] = lows[:, :16].astype(BF16)
         lows_ref[1] = lows[:, 16:].astype(BF16)
+        lows_ref[2] = dot(s[...], bdown_ref[...], NT).astype(BF16)
+        chunk = 2 * LANES
         for copy in copies[0]:
             copy.wait()
         for copy in copies[1]:
             copy.start()
-
-        @pl.loop(0, slots)
-        def _(c):
-            cols = pl.ds(pl.multiple_of(c * chunk, chunk), chunk)
+        for n in range(hidden // chunk):
+            cols = slice(n * chunk, (n + 1) * chunk)
             gates[:, cols] = dot(x[...], weights[0, cols, :], NT) + SCALE * dot(
                 lows_ref[0], right_ref[0, :, cols]
             )
-            from_row = pl.multiple_of(depth + c * tiles, tiles)
-            for e in range(peers):
-                more[e * narrow : e * narrow + tiles, :] = recv_ref[e, pl.ds(from_row, tiles), :].astype(F32)
-            for j in range(tiles):
-                s[pl.ds(pl.multiple_of(c * peers, peers), peers), j * LANES : (j + 1) * LANES] = more[
-                    pl.ds(j, peers, stride=narrow), :
-                ].astype(BF16)
-
         for copy in copies[1]:
             copy.wait()
         out_copies = [
@@ -210,12 +209,11 @@
         ]
         for copy in copies[2] + out_copies:
             copy.start()
-        for n in range(slots):
+        for n in range(hidden // chunk):
             cols = slice(n * chunk, (n + 1) * chunk)
             ups[:, cols] = dot(x[...], weights[1, cols, :], NT) + SCALE * dot(
                 lows_ref[1], right_ref[1, :, cols]
             )
-        lows_ref[2] = dot(s[...], bdown_ref[...], NT).astype(BF16)
         for copy in copies[2] + out_copies:
             copy.wait()
 
@@ -383,8 +381,8 @@
     down_ring = [(i, (i - 1) % shards) for i in range(shards)]
     (send,) = call(
         dispatch_body(slots, tokens * groups, doc_lengths.shape[1]),
-        (*in_hbm((routes_t, gate_num[0].T, doc_lengths)), start, *in_hbm((x, g))),
-        [vmem(), vmem(), smem(), smem(), anyspace(), anyspace()],
+        (start, *in_hbm((x, g, routes_t, gate_num[0].T, doc_lengths))),
+        [smem()] + [anyspace()] * 5,
         [((groups, 2 * depth, LANES), BF16, pltpu.HBM)],
         [anyspace()],
         [
@@ -393,7 +391,10 @@
             pltpu.VMEM((groups, 2 * depth, LANES), BF16),
             pltpu.VMEM((tokens, features), BF16),
             pltpu.VMEM((tokens, features), BF16),
-            pltpu.SemaphoreType.DMA((2,)),
+            pltpu.VMEM(routes_t.shape, jnp.int32),
+            pltpu.VMEM(routes_t.shape, jnp.int32),
+            pltpu.SMEM(doc_lengths.shape, jnp.int32),
+            pltpu.SemaphoreType.DMA((5,)),
             pltpu.SemaphoreType.DMA((2, groups // 8)),
         ],
         4 * rows * tokens * features,
@@ -405,13 +406,18 @@
 
     half = share // 2
     parts = []
-    for w in own:
+    for w, name in zip(own, ("gatering", "upring", "lastring")):
         behind = lax.ppermute(w, "dp", up_ring)
         ahead = lax.ppermute(w, "dp", down_ring)
-        far = [lax.ppermute(behind[:half], "dp", up_ring), lax.ppermute(ahead[half:], "dp", down_ring)]
+        if name == "gatering":
+            far = [lax.ppermute(ahead, "dp", down_ring)]
+        elif name == "upring":
+            far = [lax.ppermute(behind, "dp", up_ring)]
+        else:
+            far = [lax.ppermute(behind[:half], "dp", up_ring), lax.ppermute(ahead[half:], "dp", down_ring)]
         parts.append((w, ahead, behind, *far))
-    spots = ((share, share), (2 * share, share), (0, share), (3 * share, half), (3 * share + half, half))
-    near = spots[:3]
+    near = ((share, share), (2 * share, share), (0, share))
+    spots = (*near, (3 * share, share))
 
     left = jnp.concatenate([a_gate[0].T, a_up[0].T], axis=0)
     right = jnp.stack([b_gate[0], b_up[0], a_down[0].T])
@@ -424,7 +430,7 @@
             [(m, *spot) for m in range(2) for spot in spots] + [(2, *spot) for spot in near],
         ),
         (recv, *in_hbm((*parts[0], *parts[1], *parts[2][:3])), *in_vmem((left, b_down[0], right))),
-        [vmem()] + [anyspace()] * 13 + [vmem()] * 3,
+        [vmem()] + [anyspace()] * 11 + [vmem()] * 3,
         [
             ((2, rows, features), BF16, pltpu.HBM),
             ((rows, features), BF16, pltpu.VMEM),
@@ -438,13 +444,13 @@
         [
             pltpu.VMEM((rows, features), BF16),
             pltpu.VMEM((groups * (depth + 4), LANES), F32),
-            pltpu.VMEM((groups * (tiles + 4), LANES), F32),
-            pltpu.SemaphoreType.DMA((13,)),
+            pltpu.VMEM((groups * (depth + 4), LANES), F32),
+            pltpu.SemaphoreType.DMA((11,)),
             pltpu.SemaphoreType.DMA((2,)),
         ],
         4 * rows * hidden * features,
         4 * hidden * features + 4 * rows * features,
-        12,
+        14,
     )
     send_back, acts, all_lows = call(
         expert_body(slots),

time: 173 us -> 175 us (1.012)
  the two profiles are of different devices: /device:TPU:14 before, /device:TPU:8 now
where the time goes in v3:
time: 175 us
  waiting for transfers between devices  75.6 us (43%)
  starting transfers between devices  69.3 us (40%)
  Pallas kernels  25.9 us (15%)
  local copies, waits for them, and re-layouts  2.54 us (1%)
    ppermute x3, waiting for transfers between devices, layer(): behind = lax.ppermute(w, 'dp', up_ring)  26.3 us
    pallas_call x6, Pallas kernels, call(): pl.pallas_call(body, out_shape=[space(s, d) for s, d, space in outs], in_...  25.9 us
    all_to_all x1, waiting for transfers between devices, layer(): lax.all_to_all(send_back, 'expert', split_axis=0, concat_axis=0, tiled=True)  21.6 us
    all_to_all x1, starting transfers between devices, layer(): lax.all_to_all(send, 'expert', split_axis=0, concat_axis=0, tiled=True)  17.5 us
    ppermute x3, starting transfers between devices, layer(): ahead = lax.ppermute(w, 'dp', down_ring)  14.8 us
    all_to_all x1, starting transfers between devices, layer(): lax.all_to_all(send_back, 'expert', split_axis=0, concat_axis=0, tiled=True)  13.7 us
    ppermute x3, starting transfers between devices, layer(): lax.ppermute(shares[k], 'dp', [(i, (i + k) % shards) for i in range(shard...  8.96 us
    ppermute x1, waiting for transfers between devices, layer(): far = [lax.ppermute(ahead, 'dp', down_ring)]  8.95 us
  transfers between devices with their start and end apart: 15, of which 8 were waited for; matrix products, arithmetic and copies ran while one was open for 1% of the time, Pallas kernels for 7%

profile of v3, /device:TPU:8, one launch (start us, length us, event | category | flops | bytes accessed | tf_op | source)
XLA Modules:
  0.0 174.5 jit_solution(12729826652258654177)
XLA Ops:
  0.6 3.9 %shard_map.189 = bf16[128,96,128]{2,1,0:T(8,128)(2,1)} custom-call(s32[1]{0:T(128)} %bitcast.start_ref, bf16[128,2048]{1,0:T(8,128)(2,1)} %bitcast.48, bf16[128,2048]{1,0:T(8,128)(2,1)} %bitcast.49, s32[2,128]{1,0:T(2,128)} %bitcast.54, s32[2,128]{1,0:T(2,128)} %bitcast.56, s32[1,32]{1,0:T(1,128)} %lengths_hbm.1), custom_call_target="tpu_custom_call" | custom-call | flops 402653184 | bytes 3145728 | tf_op jit(solution)/shard_map/pallas_call | solution.py:44
  4.6 0.0 copy-start.6
  4.6 0.0 copy-start.7
  4.6 17.5 %all-to-all-start = ((bf16[128,96,128]{2,1,0:T(8,128)(2,1)}), bf16[128,96,128]{2,1,0:T(8,128)(2,1)S(1)}, u32[]{:S(2)}, u32[]{:S(2)}) async-start(bf16[128,96,128]{2,1,0:T(8,128)(2,1)} %shard_map.189), calls=%async_computation | async-start | bytes 6291456 | tf_op jit(solution)/shard_map/all_to_all | solution.py:405
  22.1 0.0 copy-start.8
  22.1 0.0 copy-start.9
  22.1 0.0 copy-start.10
  22.2 0.0 copy-start.2
  22.2 4.8 %collective-permute-start = (bf16[192,2048]{1,0:T(8,128)(2,1)}, bf16[192,2048]{1,0:T(8,128)(2,1)}, u32[]{:S(2)}, u32[]{:S(2)}) collective-permute-start(bf16[192,2048]{1,0:T(8,128)(2,1)} %bitcast.39), channel_id=1, source_target_pairs={{0,3},{1,0},{2,1},{3,2},{4,7},{5,4},{6,5},{7,6},{8,11},{9,8},{10,9... | collective-permute-start | bytes 2359304 | tf_op jit(solution)/shard_map/ppermute | solution.py:411
  27.0 1.9 %collective-permute-start.4 = (bf16[192,2048]{1,0:T(8,128)(2,1)}, bf16[192,2048]{1,0:T(8,128)(2,1)}, u32[]{:S(2)}, u32[]{:S(2)}) collective-permute-start(bf16[192,2048]{1,0:T(8,128)(2,1)} %bitcast.42), channel_id=1, source_target_pairs={{0,1},{1,2},{2,3},{3,0},{4,5},{5,6},{6,7},{7,4},{8,9},{9,10},{10,1... | collective-permute-start | bytes 2359304 | tf_op jit(solution)/shard_map/ppermute | solution.py:410
  28.9 2.7 %collective-permute-start.7 = (bf16[192,2048]{1,0:T(8,128)(2,1)}, bf16[192,2048]{1,0:T(8,128)(2,1)S(1)}, u32[]{:S(2)}, u32[]{:S(2)}) collective-permute-start(bf16[192,2048]{1,0:T(8,128)(2,1)} %bitcast.45), channel_id=1, source_target_pairs={{0,1},{1,2},{2,3},{3,0},{4,5},{5,6},{6,7},{7,4},{8,9},{9,10},{10,1... | collective-permute-start | bytes 2359304 | tf_op jit(solution)/shard_map/ppermute | solution.py:410
  31.6 4.4 %collective-permute-start.6 = (bf16[192,2048]{1,0:T(8,128)(2,1)}, bf16[192,2048]{1,0:T(8,128)(2,1)S(1)}, u32[]{:S(2)}, u32[]{:S(2)}) collective-permute-start(bf16[192,2048]{1,0:T(8,128)(2,1)} %bitcast.46), channel_id=1, source_target_pairs={{0,3},{1,0},{2,1},{3,2},{4,7},{5,4},{6,5},{7,6},{8,11},{9,8},{10,9... | collective-permute-start | bytes 2359304 | tf_op jit(solution)/shard_map/ppermute | solution.py:411
  36.0 1.9 %collective-permute-start.1 = (bf16[192,2048]{1,0:T(8,128)(2,1)}, bf16[192,2048]{1,0:T(8,128)(2,1)S(1)}, u32[]{:S(2)}, u32[]{:S(2)}) collective-permute-start(bf16[192,2048]{1,0:T(8,128)(2,1)} %bitcast.40), channel_id=1, source_target_pairs={{0,1},{1,2},{2,3},{3,0},{4,5},{5,6},{6,7},{7,4},{8,9},{9,10},{10,1... | collective-permute-start | bytes 2359304 | tf_op jit(solution)/shard_map/ppermute | solution.py:410
  37.9 7.3 %collective-permute-done.refs_1_ = bf16[192,2048]{1,0:T(8,128)(2,1)} collective-permute-done((bf16[192,2048]{1,0:T(8,128)(2,1)}, bf16[192,2048]{1,0:T(8,128)(2,1)}, u32[]{:S(2)}, u32[]{:S(2)}) %collective-permute-start) | collective-permute-done | bytes 786464 | tf_op jit(solution)/shard_map/ppermute | solution.py:411
  45.2 5.6 %collective-permute-start.3 = (bf16[192,2048]{1,0:T(8,128)(2,1)}, bf16[192,2048]{1,0:T(8,128)(2,1)}, u32[]{:S(2)}, u32[]{:S(2)}) collective-permute-start(bf16[192,2048]{1,0:T(8,128)(2,1)} %bitcast.43), channel_id=1, source_target_pairs={{0,3},{1,0},{2,1},{3,2},{4,7},{5,4},{6,5},{7,6},{8,11},{9,8},{10,9... | collective-permute-start | bytes 2359304 | tf_op jit(solution)/shard_map/ppermute | solution.py:411
  50.8 0.0 collective-permute-done.4.refs_6_
  50.8 1.9 %collective-permute-start.2 = (bf16[192,2048]{1,0:T(8,128)(2,1)}, bf16[192,2048]{1,0:T(8,128)(2,1)}, u32[]{:S(2)}, u32[]{:S(2)}) collective-permute-start(bf16[192,2048]{1,0:T(8,128)(2,1)} %collective-permute-done.refs_1_), channel_id=1, source_target_pairs={{0,3},{1,0},{2,1},{3,2},{4,7},{5,4},{6,5},{7,6},{8,11},{9,8},{10,9... | collective-permute-start | bytes 2359304 | tf_op jit(solution)/shard_map/ppermute | solution.py:413
  52.7 14.8 %collective-permute-done.7.refs_10_ = bf16[192,2048]{1,0:T(8,128)(2,1)S(1)} collective-permute-done((bf16[192,2048]{1,0:T(8,128)(2,1)}, bf16[192,2048]{1,0:T(8,128)(2,1)S(1)}, u32[]{:S(2)}, u32[]{:S(2)}) %collective-permute-start.7) | collective-permute-done | bytes 786464 | tf_op jit(solution)/shard_map/ppermute | solution.py:410
  67.6 0.0 copy-start.3
  67.6 1.9 %collective-permute-start.5 = (bf16[192,2048]{1,0:T(8,128)(2,1)}, bf16[192,2048]{1,0:T(8,128)(2,1)}, u32[]{:S(2)}, u32[]{:S(2)}) collective-permute-start(bf16[192,2048]{1,0:T(8,128)(2,1)} %collective-permute-done.4.refs_6_), channel_id=1, source_target_pairs={{0,1},{1,2},{2,3},{3,0},{4,5},{5,6},{6,7},{7,4},{8,9},{9,10},{10,1... | collective-permute-start | bytes 2359304 | tf_op jit(solution)/shard_map/ppermute | solution.py:415
  69.5 0.8 slice.8
  70.2 0.0 collective-permute-done.6.refs_9_
  70.3 0.0 copy-start.4
  70.3 1.9 %collective-permute-start.8 = (bf16[96,2048]{1,0:T(8,128)(2,1)}, bf16[96,2048]{1,0:T(8,128)(2,1)}, u32[]{:S(2)}, u32[]{:S(2)}) collective-permute-start(bf16[96,2048]{1,0:T(8,128)(2,1)} %slice.8), channel_id=1, source_target_pairs={{0,1},{1,2},{2,3},{3,0},{4,5},{5,6},{6,7},{7,4},{8,9},{9,10},{10,1... | collective-permute-start | bytes 1179656 | tf_op jit(solution)/shard_map/ppermute | solution.py:417
  72.2 0.8 slice.9
  73.0 11.4 %collective-permute-done.1.refs_2_ = bf16[192,2048]{1,0:T(8,128)(2,1)S(1)} collective-permute-done((bf16[192,2048]{1,0:T(8,128)(2,1)}, bf16[192,2048]{1,0:T(8,128)(2,1)S(1)}, u32[]{:S(2)}, u32[]{:S(2)}) %collective-permute-start.1) | collective-permute-done | bytes 786464 | tf_op jit(solution)/shard_map/ppermute | solution.py:410
  84.4 0.0 copy-start.5
  84.4 2.1 %collective-permute-start.9 = (bf16[96,2048]{1,0:T(8,128)(2,1)}, bf16[96,2048]{1,0:T(8,128)(2,1)}, u32[]{:S(2)}, u32[]{:S(2)}) collective-permute-start(bf16[96,2048]{1,0:T(8,128)(2,1)} %slice.9), channel_id=1, source_target_pairs={{0,3},{1,0},{2,1},{3,2},{4,7},{5,4},{6,5},{7,6},{8,11},{9,8},{10,9... | collective-permute-start | bytes 1179656 | tf_op jit(solution)/shard_map/ppermute | solution.py:417
  86.5 0.0 copy-done.3
  86.5 0.0 copy-done.4
  86.5 0.0 copy-done.5
  86.5 0.0 copy-done.6
  86.5 0.0 copy-done.7
  86.6 0.0 copy-done.8
  86.6 0.0 copy-done.9
  86.6 0.0 copy-done.10
  86.6 0.2 fusion.2.refs_13_.refs_3_.right_ref
  86.8 0.0 copy-start
  86.8 0.0 collective-permute-done.3.refs_5_
  86.8 9.0 %collective-permute-done.2.refs_3_ = bf16[192,2048]{1,0:T(8,128)(2,1)} collective-permute-done((bf16[192,2048]{1,0:T(8,128)(2,1)}, bf16[192,2048]{1,0:T(8,128)(2,1)}, u32[]{:S(2)}, u32[]{:S(2)}) %collective-permute-start.2) | collective-permute-done | bytes 786464 | tf_op jit(solution)/shard_map/ppermute | solution.py:413
  95.8 5.6 %collective-permute-done.5.refs_7_ = bf16[192,2048]{1,0:T(8,128)(2,1)} collective-permute-done((bf16[192,2048]{1,0:T(8,128)(2,1)}, bf16[192,2048]{1,0:T(8,128)(2,1)}, u32[]{:S(2)}, u32[]{:S(2)}) %collective-permute-start.5) | collective-permute-done | bytes 786464 | tf_op jit(solution)/shard_map/ppermute | solution.py:415
  101.4 0.0 all-to-all-done.recv_ref
  101.4 0.0 copy-done.2
  101.4 7.8 %shard_map.190 = (bf16[2,384,2048]{2,1,0:T(8,128)(2,1)}, bf16[384,2048]{1,0:T(8,128)(2,1)S(1)}, f32[384,768]{1,0:T(8,128)S(1)}, f32[384,768]{1,0:T(8,128)S(1)}, ...) custom-call(bf16[128,96,128]{2,1,0:T(8,128)(2,1)S(1)} %all-to-all-done.recv_ref, ...), custom_call_target="tpu_custom_call" | custom-call | flops 2415919104 | bytes 9437184 | tf_op jit(solution)/shard_map/pallas_call | solution.py:44
  109.2 0.0 collective-permute-done.8.refs_0_
  109.2 0.0 collective-permute-done.9.refs_1_
  109.2 0.0 copy-done
  109.2 7.3 %shard_map.191 = (bf16[128,48,128]{2,1,0:T(8,128)(2,1)}, bf16[3,384,768]{2,1,0:T(8,128)(2,1)}, bf16[5,384,16]{2,1,0:T(8,128)(2,1)}) custom-call(bf16[384,2048]{1,0:T(8,128)(2,1)S(1)} %get-tuple-element.28.s, f32[384,768]{1,0:T(8,128)S(1)} %get-tuple-element.29.gates, f32[384,768]{1,0:T(8,128)S(1)} %get-tuple-element.30.ups, ...), custom_call_target="tpu_custom_call" | custom-call | flops 3623878656 | bytes 4718592 | tf_op jit(solution)/shard_map/pallas_call | solution.py:44
  116.6 13.7 %all-to-all-start.1 = ((bf16[128,48,128]{2,1,0:T(8,128)(2,1)}), bf16[128,48,128]{2,1,0:T(8,128)(2,1)S(1)}, u32[]{:S(2)}, u32[]{:S(2)}) async-start(bf16[128,48,128]{2,1,0:T(8,128)(2,1)} %get-tuple-element.34), calls=%async_computation.1 | async-start | bytes 3145728 | tf_op jit(solution)/shard_map/all_to_all | solution.py:484
  130.3 4.5 %shard_map.192 = (f32[3,16,768]{2,1,0:T(8,128)}, f32[3,16,768]{2,1,0:T(8,128)}, f32[3,16,768]{2,1,0:T(8,128)}, f32[3,16,768]{2,1,0:T(8,128)}, bf16[128,384]{1,0:T(8,128)(2,1)S(1)}) custom-call(s32[1]{0:T(128)} %bitcast.18.me_ref, s32[2,128]{1,0:T(2,128)} %bitcast.55, bf16[2,384,2048]{2,1,0:T(8,128)(2,1)} %get-tuple-element.35.rows_ref, ...), custom_call_target="tpu_custom_call" | custom-call | flops 150994944 | bytes 3145728 | tf_op jit(solution)/shard_map/pallas_call | solution.py:44
  134.8 1.9 %collective-permute-start.10 = (f32[3,16,768]{2,1,0:T(8,128)}, f32[3,16,768]{2,1,0:T(8,128)S(1)}, u32[]{:S(2)}, u32[]{:S(2)}) collective-permute-start(f32[3,16,768]{2,1,0:T(8,128)} %get-tuple-element.40), channel_id=1, source_target_pairs={{0,1},{1,2},{2,3},{3,0},{4,5},{5,6},{6,7},{7,4},{8,9},{9,10},{10,1... | collective-permute-start | bytes 442376 | tf_op jit(solution)/shard_map/ppermute | solution.py:501
  136.7 3.0 %collective-permute-start.11 = (f32[3,16,768]{2,1,0:T(8,128)}, f32[3,16,768]{2,1,0:T(8,128)S(1)}, u32[]{:S(2)}, u32[]{:S(2)}) collective-permute-start(f32[3,16,768]{2,1,0:T(8,128)} %get-tuple-element.41), channel_id=1, source_target_pairs={{0,2},{1,3},{2,0},{3,1},{4,6},{5,7},{6,4},{7,5},{8,10},{9,11},{10,... | collective-permute-start | bytes 442376 | tf_op jit(solution)/shard_map/ppermute | solution.py:501
  139.7 4.1 %collective-permute-start.12 = (f32[3,16,768]{2,1,0:T(8,128)}, f32[3,16,768]{2,1,0:T(8,128)S(1)}, u32[]{:S(2)}, u32[]{:S(2)}) collective-permute-start(f32[3,16,768]{2,1,0:T(8,128)} %get-tuple-element.42), channel_id=1, source_target_pairs={{0,3},{1,0},{2,1},{3,2},{4,7},{5,4},{6,5},{7,6},{8,11},{9,8},{10,9... | collective-permute-start | bytes 442376 | tf_op jit(solution)/shard_map/ppermute | solution.py:501
  143.8 3.3 %collective-permute-done.10.b_ref = f32[3,16,768]{2,1,0:T(8,128)S(1)} collective-permute-done((f32[3,16,768]{2,1,0:T(8,128)}, f32[3,16,768]{2,1,0:T(8,128)S(1)}, u32[]{:S(2)}, u32[]{:S(2)}) %collective-permute-start.10) | collective-permute-done | bytes 147488 | tf_op jit(solution)/shard_map/ppermute | solution.py:501
  147.2 0.0 collective-permute-done.11.c_ref
  147.2 2.5 %collective-permute-done.12.d_ref = f32[3,16,768]{2,1,0:T(8,128)S(1)} collective-permute-done((f32[3,16,768]{2,1,0:T(8,128)}, f32[3,16,768]{2,1,0:T(8,128)S(1)}, u32[]{:S(2)}, u32[]{:S(2)}) %collective-permute-start.12) | collective-permute-done | bytes 147488 | tf_op jit(solution)/shard_map/ppermute | solution.py:501
  149.7 0.0 copy-start.1
  149.7 0.9 copy-done.1
  150.6 0.7 shard_map.194
  151.2 21.6 %all-to-all-done.1.back_ref = bf16[128,48,128]{2,1,0:T(8,128)(2,1)S(1)} async-done(((bf16[128,48,128]{2,1,0:T(8,128)(2,1)}), bf16[128,48,128]{2,1,0:T(8,128)(2,1)S(1)}, u32[]{:S(2)}, u32[]{:S(2)}) %all-to-all-start.1) | async-done | bytes 1572896 | tf_op jit(solution)/shard_map/all_to_all | solution.py:484
  172.9 1.6 shard_map.193
  (1 shorter events, 0.0 us)
Async XLA Ops:
  4.6 82.0 %copy-start.6 = (bf16[1,2048,16]{1,2,0:T(8,128)(2,1)S(1)}, bf16[1,2048,16]{1,2,0:T(8,128)(2,1)}, u32[]{:S(2)}) copy-start(bf16[1,2048,16]{1,2,0:T(8,128)(2,1)} %param.24) | copy-start | bytes 196612
  4.6 82.0 %copy-start.7 = (bf16[1,2048,16]{1,2,0:T(8,128)(2,1)S(1)}, bf16[1,2048,16]{1,2,0:T(8,128)(2,1)}, u32[]{:S(2)}) copy-start(bf16[1,2048,16]{1,2,0:T(8,128)(2,1)} %param.22) | copy-start | bytes 196612
  4.6 96.8 %all-to-all-start = ((bf16[128,96,128]{2,1,0:T(8,128)(2,1)}), bf16[128,96,128]{2,1,0:T(8,128)(2,1)S(1)}, u32[]{:S(2)}, u32[]{:S(2)}) async-start(bf16[128,96,128]{2,1,0:T(8,128)(2,1)} %shard_map.189), calls=%async_computation | async-start | bytes 6291456 | tf_op jit(solution)/shard_map/all_to_all | solution.py:405
  22.1 64.5 %copy-start.8 = (bf16[1,16,768]{2,1,0:T(8,128)(2,1)S(1)}, bf16[1,16,768]{2,1,0:T(8,128)(2,1)}, u32[]{:S(2)}) copy-start(bf16[1,16,768]{2,1,0:T(8,128)(2,1)} %param.23) | copy-start | bytes 73732
  22.1 64.5 %copy-start.9 = (bf16[1,16,768]{2,1,0:T(8,128)(2,1)S(1)}, bf16[1,16,768]{2,1,0:T(8,128)(2,1)}, u32[]{:S(2)}) copy-start(bf16[1,16,768]{2,1,0:T(8,128)(2,1)} %param.25) | copy-start | bytes 73732
  22.1 64.5 %copy-start.10 = (bf16[1,768,16]{1,2,0:T(8,128)(2,1)S(1)}, bf16[1,768,16]{1,2,0:T(8,128)(2,1)}, u32[]{:S(2)}) copy-start(bf16[1,768,16]{1,2,0:T(8,128)(2,1)} %param.26) | copy-start | bytes 73732
  22.2 79.2 %copy-start.2 = (bf16[1,16,2048]{2,1,0:T(8,128)(2,1)S(1)}, bf16[1,16,2048]{2,1,0:T(8,128)(2,1)}, u32[]{:S(2)}) copy-start(bf16[1,16,2048]{2,1,0:T(8,128)(2,1)} %param.27) | copy-start | bytes 196612
  22.2 23.0 %collective-permute-start = (bf16[192,2048]{1,0:T(8,128)(2,1)}, bf16[192,2048]{1,0:T(8,128)(2,1)}, u32[]{:S(2)}, u32[]{:S(2)}) collective-permute-start(bf16[192,2048]{1,0:T(8,128)(2,1)} %bitcast.39), channel_id=1, source_target_pairs={{0,3},{1,0},{2,1},{3,2},{4,7},{5,4},{6,5},{7,6},{8,11},{9,8},{10,9... | collective-permute-start | bytes 2359304 | tf_op jit(solution)/shard_map/ppermute | solution.py:411
  27.0 23.8 %collective-permute-start.4 = (bf16[192,2048]{1,0:T(8,128)(2,1)}, bf16[192,2048]{1,0:T(8,128)(2,1)}, u32[]{:S(2)}, u32[]{:S(2)}) collective-permute-start(bf16[192,2048]{1,0:T(8,128)(2,1)} %bitcast.42), channel_id=1, source_target_pairs={{0,1},{1,2},{2,3},{3,0},{4,5},{5,6},{6,7},{7,4},{8,9},{9,10},{10,1... | collective-permute-start | bytes 2359304 | tf_op jit(solution)/shard_map/ppermute | solution.py:410
  28.9 38.7 %collective-permute-start.7 = (bf16[192,2048]{1,0:T(8,128)(2,1)}, bf16[192,2048]{1,0:T(8,128)(2,1)S(1)}, u32[]{:S(2)}, u32[]{:S(2)}) collective-permute-start(bf16[192,2048]{1,0:T(8,128)(2,1)} %bitcast.45), channel_id=1, source_target_pairs={{0,1},{1,2},{2,3},{3,0},{4,5},{5,6},{6,7},{7,4},{8,9},{9,10},{10,1... | collective-permute-start | bytes 2359304 | tf_op jit(solution)/shard_map/ppermute | solution.py:410
  31.6 38.7 %collective-permute-start.6 = (bf16[192,2048]{1,0:T(8,128)(2,1)}, bf16[192,2048]{1,0:T(8,128)(2,1)S(1)}, u32[]{:S(2)}, u32[]{:S(2)}) collective-permute-start(bf16[192,2048]{1,0:T(8,128)(2,1)} %bitcast.46), channel_id=1, source_target_pairs={{0,3},{1,0},{2,1},{3,2},{4,7},{5,4},{6,5},{7,6},{8,11},{9,8},{10,9... | collective-permute-start | bytes 2359304 | tf_op jit(solution)/shard_map/ppermute | solution.py:411
  36.0 48.4 %collective-permute-start.1 = (bf16[192,2048]{1,0:T(8,128)(2,1)}, bf16[192,2048]{1,0:T(8,128)(2,1)S(1)}, u32[]{:S(2)}, u32[]{:S(2)}) collective-permute-start(bf16[192,2048]{1,0:T(8,128)(2,1)} %bitcast.40), channel_id=1, source_target_pairs={{0,1},{1,2},{2,3},{3,0},{4,5},{5,6},{6,7},{7,4},{8,9},{9,10},{10,1... | collective-permute-start | bytes 2359304 | tf_op jit(solution)/shard_map/ppermute | solution.py:410
  45.2 41.6 %collective-permute-start.3 = (bf16[192,2048]{1,0:T(8,128)(2,1)}, bf16[192,2048]{1,0:T(8,128)(2,1)}, u32[]{:S(2)}, u32[]{:S(2)}) collective-permute-start(bf16[192,2048]{1,0:T(8,128)(2,1)} %bitcast.43), channel_id=1, source_target_pairs={{0,3},{1,0},{2,1},{3,2},{4,7},{5,4},{6,5},{7,6},{8,11},{9,8},{10,9... | collective-permute-start | bytes 2359304 | tf_op jit(solution)/shard_map/ppermute | solution.py:411
  50.8 44.9 %collective-permute-start.2 = (bf16[192,2048]{1,0:T(8,128)(2,1)}, bf16[192,2048]{1,0:T(8,128)(2,1)}, u32[]{:S(2)}, u32[]{:S(2)}) collective-permute-start(bf16[192,2048]{1,0:T(8,128)(2,1)} %collective-permute-done.refs_1_), channel_id=1, source_target_pairs={{0,3},{1,0},{2,1},{3,2},{4,7},{5,4},{6,5},{7,6},{8,11},{9,8},{10,9... | collective-permute-start | bytes 2359304 | tf_op jit(solution)/shard_map/ppermute | solution.py:413
  67.6 19.0 %copy-start.3 = (bf16[192,2048]{1,0:T(8,128)(2,1)}, bf16[192,2048]{1,0:T(8,128)(2,1)S(1)}, u32[]{:S(2)}) copy-start(bf16[192,2048]{1,0:T(8,128)(2,1)S(1)} %collective-permute-done.7.refs_10_) | copy-start | bytes 2359300
  67.6 33.8 %collective-permute-start.5 = (bf16[192,2048]{1,0:T(8,128)(2,1)}, bf16[192,2048]{1,0:T(8,128)(2,1)}, u32[]{:S(2)}, u32[]{:S(2)}) collective-permute-start(bf16[192,2048]{1,0:T(8,128)(2,1)} %collective-permute-done.4.refs_6_), channel_id=1, source_target_pairs={{0,1},{1,2},{2,3},{3,0},{4,5},{5,6},{6,7},{7,4},{8,9},{9,10},{10,1... | collective-permute-start | bytes 2359304 | tf_op jit(solution)/shard_map/ppermute | solution.py:415
  70.3 16.3 %copy-start.4 = (bf16[192,2048]{1,0:T(8,128)(2,1)}, bf16[192,2048]{1,0:T(8,128)(2,1)S(1)}, u32[]{:S(2)}) copy-start(bf16[192,2048]{1,0:T(8,128)(2,1)S(1)} %collective-permute-done.6.refs_9_) | copy-start | bytes 2359300
  70.3 38.9 %collective-permute-start.8 = (bf16[96,2048]{1,0:T(8,128)(2,1)}, bf16[96,2048]{1,0:T(8,128)(2,1)}, u32[]{:S(2)}, u32[]{:S(2)}) collective-permute-start(bf16[96,2048]{1,0:T(8,128)(2,1)} %slice.8), channel_id=1, source_target_pairs={{0,1},{1,2},{2,3},{3,0},{4,5},{5,6},{6,7},{7,4},{8,9},{9,10},{10,1... | collective-permute-start | bytes 1179656 | tf_op jit(solution)/shard_map/ppermute | solution.py:417
  84.4 2.1 %copy-start.5 = (bf16[192,2048]{1,0:T(8,128)(2,1)}, bf16[192,2048]{1,0:T(8,128)(2,1)S(1)}, u32[]{:S(2)}) copy-start(bf16[192,2048]{1,0:T(8,128)(2,1)S(1)} %collective-permute-done.1.refs_2_) | copy-start | bytes 2359300
  84.4 24.8 %collective-permute-start.9 = (bf16[96,2048]{1,0:T(8,128)(2,1)}, bf16[96,2048]{1,0:T(8,128)(2,1)}, u32[]{:S(2)}, u32[]{:S(2)}) collective-permute-start(bf16[96,2048]{1,0:T(8,128)(2,1)} %slice.9), channel_id=1, source_target_pairs={{0,3},{1,0},{2,1},{3,2},{4,7},{5,4},{6,5},{7,6},{8,11},{9,8},{10,9... | collective-permute-start | bytes 1179656 | tf_op jit(solution)/shard_map/ppermute | solution.py:417
  86.8 22.4 %copy-start = (bf16[3,16,768]{2,1,0:T(8,128)(2,1)}, bf16[3,16,768]{2,1,0:T(8,128)(2,1)S(1)}, u32[]{:S(2)}) copy-start(bf16[3,16,768]{2,1,0:T(8,128)(2,1)S(1)} %fusion.2.refs_13_.refs_3_.right_ref) | copy-start | bytes 221188
  116.6 56.3 %all-to-all-start.1 = ((bf16[128,48,128]{2,1,0:T(8,128)(2,1)}), bf16[128,48,128]{2,1,0:T(8,128)(2,1)S(1)}, u32[]{:S(2)}, u32[]{:S(2)}) async-start(bf16[128,48,128]{2,1,0:T(8,128)(2,1)} %get-tuple-element.34), calls=%async_computation.1 | async-start | bytes 3145728 | tf_op jit(solution)/shard_map/all_to_all | solution.py:484
  134.8 12.3 %collective-permute-start.10 = (f32[3,16,768]{2,1,0:T(8,128)}, f32[3,16,768]{2,1,0:T(8,128)S(1)}, u32[]{:S(2)}, u32[]{:S(2)}) collective-permute-start(f32[3,16,768]{2,1,0:T(8,128)} %get-tuple-element.40), channel_id=1, source_target_pairs={{0,1},{1,2},{2,3},{3,0},{4,5},{5,6},{6,7},{7,4},{8,9},{9,10},{10,1... | collective-permute-start | bytes 442376 | tf_op jit(solution)/shard_map/ppermute | solution.py:501
  136.7 10.4 %collective-permute-start.11 = (f32[3,16,768]{2,1,0:T(8,128)}, f32[3,16,768]{2,1,0:T(8,128)S(1)}, u32[]{:S(2)}, u32[]{:S(2)}) collective-permute-start(f32[3,16,768]{2,1,0:T(8,128)} %get-tuple-element.41), channel_id=1, source_target_pairs={{0,2},{1,3},{2,0},{3,1},{4,6},{5,7},{6,4},{7,5},{8,10},{9,11},{10,... | collective-permute-start | bytes 442376 | tf_op jit(solution)/shard_map/ppermute | solution.py:501
  139.7 9.9 %collective-permute-start.12 = (f32[3,16,768]{2,1,0:T(8,128)}, f32[3,16,768]{2,1,0:T(8,128)S(1)}, u32[]{:S(2)}, u32[]{:S(2)}) collective-permute-start(f32[3,16,768]{2,1,0:T(8,128)} %get-tuple-element.42), channel_id=1, source_target_pairs={{0,3},{1,0},{2,1},{3,2},{4,7},{5,4},{6,5},{7,6},{8,11},{9,8},{10,9... | collective-permute-start | bytes 442376 | tf_op jit(solution)/shard_map/ppermute | solution.py:501
  149.7 0.9 copy-start.1

commit v4 on v2

--- a/solution.py
+++ b/solution.py
@@ -94,13 +94,19 @@
 
 
 def dispatch_body(slots, group_tokens, doc_count):
-    def body(routes_ref, nums_ref, lengths_ref, start_ref, x_hbm, g_hbm, send_ref, wide, more, stage, x_ref, g_ref, lsems, sems):
+    def body(start_ref, x_hbm, g_hbm, routes_hbm, nums_hbm, lengths_hbm, send_ref, *scratches):
+        wide, more, stage, x_ref, g_ref, routes_ref, nums_ref, lengths_ref, lsems, sems = scratches
         loads = [
-            pltpu.make_async_copy(x_hbm, x_ref, lsems.at[0]),
-            pltpu.make_async_copy(g_hbm, g_ref, lsems.at[1]),
+            pltpu.make_async_copy(routes_hbm, routes_ref, lsems.at[0]),
+            pltpu.make_async_copy(nums_hbm, nums_ref, lsems.at[1]),
+            pltpu.make_async_copy(lengths_hbm, lengths_ref, lsems.at[2]),
+            pltpu.make_async_copy(x_hbm, x_ref, lsems.at[3]),
+            pltpu.make_async_copy(g_hbm, g_ref, lsems.at[4]),
         ]
         for load in loads:
             load.start()
+        for load in loads[:3]:
+            load.wait()
         experts = stage.shape[0]
         tokens, features = x_ref.shape
         tiles = features // LANES
@@ -127,7 +133,7 @@
         chunk = 2 * LANES
         copies = []
         for side, (source, scratch) in enumerate(((x_ref, wide), (g_ref, more))):
-            loads[side].wait()
+            loads[3 + side].wait()
             for j in range(features // chunk):
                 part = dot(pick, source[:, j * chunk : (j + 1) * chunk])
                 if side == 1:
@@ -383,8 +389,8 @@
     down_ring = [(i, (i - 1) % shards) for i in range(shards)]
     (send,) = call(
         dispatch_body(slots, tokens * groups, doc_lengths.shape[1]),
-        (*in_hbm((routes_t, gate_num[0].T, doc_lengths)), start, *in_hbm((x, g))),
-        [vmem(), vmem(), smem(), smem(), anyspace(), anyspace()],
+        (start, *in_hbm((x, g, routes_t, gate_num[0].T, doc_lengths))),
+        [smem()] + [anyspace()] * 5,
         [((groups, 2 * depth, LANES), BF16, pltpu.HBM)],
         [anyspace()],
         [
@@ -393,7 +399,10 @@
             pltpu.VMEM((groups, 2 * depth, LANES), BF16),
             pltpu.VMEM((tokens, features), BF16),
             pltpu.VMEM((tokens, features), BF16),
-            pltpu.SemaphoreType.DMA((2,)),
+            pltpu.VMEM(routes_t.shape, jnp.int32),
+            pltpu.VMEM(routes_t.shape, jnp.int32),
+            pltpu.SMEM(doc_lengths.shape, jnp.int32),
+            pltpu.SemaphoreType.DMA((5,)),
             pltpu.SemaphoreType.DMA((2, groups // 8)),
         ],
         4 * rows * tokens * features,

time: 173 us -> 172 us (level)
  no operation moved by 1% of the time
where the time goes in v4:
time: 172 us
  starting transfers between devices  78.8 us (46%)
  waiting for transfers between devices  61.2 us (36%)
  Pallas kernels  25.5 us (15%)
  local copies, waits for them, and re-layouts  4.86 us (3%)
    pallas_call x6, Pallas kernels, call(): pl.pallas_call(body, out_shape=[space(s, d) for s, d, space in outs], in_...  25.5 us
    ppermute x3, waiting for transfers between devices, layer(): behind = lax.ppermute(w, 'dp', up_ring)  23.2 us
    all_to_all x1, waiting for transfers between devices, layer(): lax.all_to_all(send_back, 'expert', split_axis=0, concat_axis=0, tiled=True)  21.6 us
    all_to_all x1, starting transfers between devices, layer(): lax.all_to_all(send, 'expert', split_axis=0, concat_axis=0, tiled=True)  17.4 us
    all_to_all x1, starting transfers between devices, layer(): lax.all_to_all(send_back, 'expert', split_axis=0, concat_axis=0, tiled=True)  13.7 us
    ppermute x3, starting transfers between devices, layer(): lax.ppermute(behind[:half], 'dp', up_ring)  11.9 us
    ppermute x3, starting transfers between devices, layer(): behind = lax.ppermute(w, 'dp', up_ring)  10.8 us
    ppermute x3, starting transfers between devices, layer(): ahead = lax.ppermute(w, 'dp', down_ring)  8.44 us
  transfers between devices with their start and end apart: 17, of which 13 were waited for; matrix products, arithmetic and copies ran while one was open for 2% of the time, Pallas kernels for 7%

profile of v4, /device:TPU:14, one launch (start us, length us, event | category | flops | bytes accessed | tf_op | source)
XLA Modules:
  0.0 171.5 jit_solution(3127593723336073433)
XLA Ops:
  0.6 3.9 %shard_map.189 = bf16[128,96,128]{2,1,0:T(8,128)(2,1)} custom-call(s32[1]{0:T(128)} %bitcast.start_ref, bf16[128,2048]{1,0:T(8,128)(2,1)} %bitcast.48, bf16[128,2048]{1,0:T(8,128)(2,1)} %bitcast.49, s32[2,128]{1,0:T(2,128)} %bitcast.54, s32[2,128]{1,0:T(2,128)} %bitcast.56, s32[1,32]{1,0:T(1,128)} %lengths_hbm.1), custom_call_target="tpu_custom_call" | custom-call | flops 402653184 | bytes 3145728 | tf_op jit(solution)/shard_map/pallas_call | solution.py:44
  4.6 17.4 %all-to-all-start = ((bf16[128,96,128]{2,1,0:T(8,128)(2,1)}), bf16[128,96,128]{2,1,0:T(8,128)(2,1)S(1)}, u32[]{:S(2)}, u32[]{:S(2)}) async-start(bf16[128,96,128]{2,1,0:T(8,128)(2,1)} %shard_map.189), calls=%async_computation | async-start | bytes 6291456 | tf_op jit(solution)/shard_map/all_to_all | solution.py:413
  22.0 2.4 %collective-permute-start.1 = (bf16[192,2048]{1,0:T(8,128)(2,1)}, bf16[192,2048]{1,0:T(8,128)(2,1)S(1)}, u32[]{:S(2)}, u32[]{:S(2)}) collective-permute-start(bf16[192,2048]{1,0:T(8,128)(2,1)} %bitcast.39), channel_id=1, source_target_pairs={{0,1},{1,2},{2,3},{3,0},{4,5},{5,6},{6,7},{7,4},{8,9},{9,10},{10,1... | collective-permute-start | bytes 2359304 | tf_op jit(solution)/shard_map/ppermute | solution.py:418
  24.4 3.5 %collective-permute-start = (bf16[192,2048]{1,0:T(8,128)(2,1)}, bf16[192,2048]{1,0:T(8,128)(2,1)S(1)}, u32[]{:S(2)}, u32[]{:S(2)}) collective-permute-start(bf16[192,2048]{1,0:T(8,128)(2,1)} %bitcast.40), channel_id=1, source_target_pairs={{0,3},{1,0},{2,1},{3,2},{4,7},{5,4},{6,5},{7,6},{8,11},{9,8},{10,9... | collective-permute-start | bytes 2359304 | tf_op jit(solution)/shard_map/ppermute | solution.py:419
  27.8 3.6 %collective-permute-start.5 = (bf16[192,2048]{1,0:T(8,128)(2,1)}, bf16[192,2048]{1,0:T(8,128)(2,1)S(1)}, u32[]{:S(2)}, u32[]{:S(2)}) collective-permute-start(bf16[192,2048]{1,0:T(8,128)(2,1)} %bitcast.42), channel_id=1, source_target_pairs={{0,1},{1,2},{2,3},{3,0},{4,5},{5,6},{6,7},{7,4},{8,9},{9,10},{10,1... | collective-permute-start | bytes 2359304 | tf_op jit(solution)/shard_map/ppermute | solution.py:418
  31.4 2.2 %collective-permute-start.4 = (bf16[192,2048]{1,0:T(8,128)(2,1)}, bf16[192,2048]{1,0:T(8,128)(2,1)S(1)}, u32[]{:S(2)}, u32[]{:S(2)}) collective-permute-start(bf16[192,2048]{1,0:T(8,128)(2,1)} %bitcast.43), channel_id=1, source_target_pairs={{0,3},{1,0},{2,1},{3,2},{4,7},{5,4},{6,5},{7,6},{8,11},{9,8},{10,9... | collective-permute-start | bytes 2359304 | tf_op jit(solution)/shard_map/ppermute | solution.py:419
  33.7 4.8 %collective-permute-start.9 = (bf16[192,2048]{1,0:T(8,128)(2,1)}, bf16[192,2048]{1,0:T(8,128)(2,1)S(1)}, u32[]{:S(2)}, u32[]{:S(2)}) collective-permute-start(bf16[192,2048]{1,0:T(8,128)(2,1)} %bitcast.45), channel_id=1, source_target_pairs={{0,1},{1,2},{2,3},{3,0},{4,5},{5,6},{6,7},{7,4},{8,9},{9,10},{10,1... | collective-permute-start | bytes 2359304 | tf_op jit(solution)/shard_map/ppermute | solution.py:418
  38.5 6.0 %collective-permute-done.1.refs_2_ = bf16[192,2048]{1,0:T(8,128)(2,1)S(1)} collective-permute-done((bf16[192,2048]{1,0:T(8,128)(2,1)}, bf16[192,2048]{1,0:T(8,128)(2,1)S(1)}, u32[]{:S(2)}, u32[]{:S(2)}) %collective-permute-start.1) | collective-permute-done | bytes 786464 | tf_op jit(solution)/shard_map/ppermute | solution.py:418
  44.5 2.7 %collective-permute-start.8 = (bf16[192,2048]{1,0:T(8,128)(2,1)}, bf16[192,2048]{1,0:T(8,128)(2,1)S(1)}, u32[]{:S(2)}, u32[]{:S(2)}) collective-permute-start(bf16[192,2048]{1,0:T(8,128)(2,1)} %bitcast.46), channel_id=1, source_target_pairs={{0,3},{1,0},{2,1},{3,2},{4,7},{5,4},{6,5},{7,6},{8,11},{9,8},{10,9... | collective-permute-start | bytes 2359304 | tf_op jit(solution)/shard_map/ppermute | solution.py:419
  47.3 0.8 collective-permute-done.refs_1_
  48.1 3.5 %collective-permute-start.2 = (bf16[96,2048]{1,0:T(8,128)(2,1)S(1)}, bf16[96,2048]{1,0:T(8,128)(2,1)S(1)}, u32[]{:S(2)}, u32[]{:S(2)}) collective-permute-start(bf16[96,2048]{1,0:T(8,128)(2,1)S(1)} %slice.24), channel_id=1, source_target_pairs={{0,1},{1,2},{2,3},{3,0},{4,5},{5,6},{6,7},{7,4},{8,9},{9,10},{10,1... | collective-permute-start | bytes 1179656 | tf_op jit(solution)/shard_map/ppermute | solution.py:420
  51.6 0.8 slice.25
  52.4 0.0 copy-start.14
  52.4 0.0 copy-start.2
  52.4 8.9 %collective-permute-done.5.refs_7_ = bf16[192,2048]{1,0:T(8,128)(2,1)S(1)} collective-permute-done((bf16[192,2048]{1,0:T(8,128)(2,1)}, bf16[192,2048]{1,0:T(8,128)(2,1)S(1)}, u32[]{:S(2)}, u32[]{:S(2)}) %collective-permute-start.5) | collective-permute-done | bytes 786464 | tf_op jit(solution)/shard_map/ppermute | solution.py:418
  61.4 2.7 %collective-permute-start.3 = (bf16[96,2048]{1,0:T(8,128)(2,1)}, bf16[96,2048]{1,0:T(8,128)(2,1)}, u32[]{:S(2)}, u32[]{:S(2)}) collective-permute-start(bf16[96,2048]{1,0:T(8,128)(2,1)} %slice.25), channel_id=1, source_target_pairs={{0,3},{1,0},{2,1},{3,2},{4,7},{5,4},{6,5},{7,6},{8,11},{9,8},{10,9... | collective-permute-start | bytes 1179656 | tf_op jit(solution)/shard_map/ppermute | solution.py:420
  64.1 0.8 slice.26
  64.9 0.1 collective-permute-done.4.refs_6_
  65.0 4.2 %collective-permute-start.6 = (bf16[96,2048]{1,0:T(8,128)(2,1)}, bf16[96,2048]{1,0:T(8,128)(2,1)}, u32[]{:S(2)}, u32[]{:S(2)}) collective-permute-start(bf16[96,2048]{1,0:T(8,128)(2,1)} %slice.26), channel_id=1, source_target_pairs={{0,1},{1,2},{2,3},{3,0},{4,5},{5,6},{6,7},{7,4},{8,9},{9,10},{10,1... | collective-permute-start | bytes 1179656 | tf_op jit(solution)/shard_map/ppermute | solution.py:420
  69.2 0.8 slice.27
  70.0 8.2 %collective-permute-done.9.refs_12_ = bf16[192,2048]{1,0:T(8,128)(2,1)S(1)} collective-permute-done((bf16[192,2048]{1,0:T(8,128)(2,1)}, bf16[192,2048]{1,0:T(8,128)(2,1)S(1)}, u32[]{:S(2)}, u32[]{:S(2)}) %collective-permute-start.9) | collective-permute-done | bytes 786464 | tf_op jit(solution)/shard_map/ppermute | solution.py:418
  78.2 2.7 %collective-permute-start.7 = (bf16[96,2048]{1,0:T(8,128)(2,1)}, bf16[96,2048]{1,0:T(8,128)(2,1)}, u32[]{:S(2)}, u32[]{:S(2)}) collective-permute-start(bf16[96,2048]{1,0:T(8,128)(2,1)} %slice.27), channel_id=1, source_target_pairs={{0,3},{1,0},{2,1},{3,2},{4,7},{5,4},{6,5},{7,6},{8,11},{9,8},{10,9... | collective-permute-start | bytes 1179656 | tf_op jit(solution)/shard_map/ppermute | solution.py:420
  80.9 0.8 slice.28
  81.7 0.0 copy-done.3
  81.7 0.1 collective-permute-done.8.refs_11_
  81.8 4.2 %collective-permute-start.10 = (bf16[96,2048]{1,0:T(8,128)(2,1)}, bf16[96,2048]{1,0:T(8,128)(2,1)}, u32[]{:S(2)}, u32[]{:S(2)}) collective-permute-start(bf16[96,2048]{1,0:T(8,128)(2,1)} %slice.28), channel_id=1, source_target_pairs={{0,1},{1,2},{2,3},{3,0},{4,5},{5,6},{6,7},{7,4},{8,9},{9,10},{10,1... | collective-permute-start | bytes 1179656 | tf_op jit(solution)/shard_map/ppermute | solution.py:420
  86.0 0.8 slice.29
  86.8 0.0 copy-done.4
  86.8 0.0 collective-permute-done.2.refs_3_
  86.8 2.7 %collective-permute-start.11 = (bf16[96,2048]{1,0:T(8,128)(2,1)}, bf16[96,2048]{1,0:T(8,128)(2,1)}, u32[]{:S(2)}, u32[]{:S(2)}) collective-permute-start(bf16[96,2048]{1,0:T(8,128)(2,1)} %slice.29), channel_id=1, source_target_pairs={{0,3},{1,0},{2,1},{3,2},{4,7},{5,4},{6,5},{7,6},{8,11},{9,8},{10,9... | collective-permute-start | bytes 1179656 | tf_op jit(solution)/shard_map/ppermute | solution.py:420
  89.5 0.0 copy-done.5
  89.6 0.0 copy-done.6
  89.6 0.0 copy-done.7
  89.6 0.0 copy-done.8
  89.6 0.0 copy-done.9
  89.6 0.0 copy-done.10
  89.6 0.0 copy-done.11
  89.7 0.0 copy-done.12
  89.7 0.0 copy-done.13
  89.7 0.0 copy-done.14
  89.7 0.2 fusion.2.refs_15_.refs_3_.right_ref
  89.8 0.0 copy-start
  89.9 0.5 collective-permute-done.3.refs_4_
  90.3 4.8 %collective-permute-done.6.refs_8_ = bf16[96,2048]{1,0:T(8,128)(2,1)} collective-permute-done((bf16[96,2048]{1,0:T(8,128)(2,1)}, bf16[96,2048]{1,0:T(8,128)(2,1)}, u32[]{:S(2)}, u32[]{:S(2)}) %collective-permute-start.6) | collective-permute-done | bytes 393248 | tf_op jit(solution)/shard_map/ppermute | solution.py:420
  95.2 3.6 %collective-permute-done.7.refs_9_ = bf16[96,2048]{1,0:T(8,128)(2,1)} collective-permute-done((bf16[96,2048]{1,0:T(8,128)(2,1)}, bf16[96,2048]{1,0:T(8,128)(2,1)}, u32[]{:S(2)}, u32[]{:S(2)}) %collective-permute-start.7) | collective-permute-done | bytes 393248 | tf_op jit(solution)/shard_map/ppermute | solution.py:420
  98.8 0.0 all-to-all-done.recv_ref
  98.8 0.0 copy-done.2
  98.8 7.5 %shard_map.190 = (bf16[2,384,2048]{2,1,0:T(8,128)(2,1)}, bf16[384,2048]{1,0:T(8,128)(2,1)S(1)}, f32[384,768]{1,0:T(8,128)S(1)}, f32[384,768]{1,0:T(8,128)S(1)}, ...) custom-call(bf16[128,96,128]{2,1,0:T(8,128)(2,1)S(1)} %all-to-all-done.recv_ref, ...), custom_call_target="tpu_custom_call" | custom-call | flops 2415919104 | bytes 9437184 | tf_op jit(solution)/shard_map/pallas_call | solution.py:44
  106.2 0.0 collective-permute-done.10.refs_0_
  106.2 0.0 collective-permute-done.11.refs_1_
  106.3 0.0 copy-done
  106.3 7.3 %shard_map.191 = (bf16[128,48,128]{2,1,0:T(8,128)(2,1)}, bf16[3,384,768]{2,1,0:T(8,128)(2,1)}, bf16[5,384,16]{2,1,0:T(8,128)(2,1)}) custom-call(bf16[384,2048]{1,0:T(8,128)(2,1)S(1)} %get-tuple-element.28.s, f32[384,768]{1,0:T(8,128)S(1)} %get-tuple-element.29.gates, f32[384,768]{1,0:T(8,128)S(1)} %get-tuple-element.30.ups, ...), custom_call_target="tpu_custom_call" | custom-call | flops 3623878656 | bytes 4718592 | tf_op jit(solution)/shard_map/pallas_call | solution.py:44
  113.6 13.7 %all-to-all-start.1 = ((bf16[128,48,128]{2,1,0:T(8,128)(2,1)}), bf16[128,48,128]{2,1,0:T(8,128)(2,1)S(1)}, u32[]{:S(2)}, u32[]{:S(2)}) async-start(bf16[128,48,128]{2,1,0:T(8,128)(2,1)} %get-tuple-element.34), calls=%async_computation.1 | async-start | bytes 3145728 | tf_op jit(solution)/shard_map/all_to_all | solution.py:487
  127.3 4.5 %shard_map.192 = (f32[3,16,768]{2,1,0:T(8,128)}, f32[3,16,768]{2,1,0:T(8,128)}, f32[3,16,768]{2,1,0:T(8,128)}, f32[3,16,768]{2,1,0:T(8,128)}, bf16[128,384]{1,0:T(8,128)(2,1)S(1)}) custom-call(s32[1]{0:T(128)} %bitcast.18.me_ref, s32[2,128]{1,0:T(2,128)} %bitcast.55, bf16[2,384,2048]{2,1,0:T(8,128)(2,1)} %get-tuple-element.35.rows_ref, ...), custom_call_target="tpu_custom_call" | custom-call | flops 150994944 | bytes 3145728 | tf_op jit(solution)/shard_map/pallas_call | solution.py:44
  131.8 2.2 %collective-permute-start.12 = (f32[3,16,768]{2,1,0:T(8,128)}, f32[3,16,768]{2,1,0:T(8,128)S(1)}, u32[]{:S(2)}, u32[]{:S(2)}) collective-permute-start(f32[3,16,768]{2,1,0:T(8,128)} %get-tuple-element.40), channel_id=1, source_target_pairs={{0,1},{1,2},{2,3},{3,0},{4,5},{5,6},{6,7},{7,4},{8,9},{9,10},{10,1... | collective-permute-start | bytes 442376 | tf_op jit(solution)/shard_map/ppermute | solution.py:504
  134.0 4.0 %collective-permute-start.13 = (f32[3,16,768]{2,1,0:T(8,128)}, f32[3,16,768]{2,1,0:T(8,128)S(1)}, u32[]{:S(2)}, u32[]{:S(2)}) collective-permute-start(f32[3,16,768]{2,1,0:T(8,128)} %get-tuple-element.41), channel_id=1, source_target_pairs={{0,2},{1,3},{2,0},{3,1},{4,6},{5,7},{6,4},{7,5},{8,10},{9,11},{10,... | collective-permute-start | bytes 442376 | tf_op jit(solution)/shard_map/ppermute | solution.py:504
  138.1 2.1 %collective-permute-start.14 = (f32[3,16,768]{2,1,0:T(8,128)}, f32[3,16,768]{2,1,0:T(8,128)S(1)}, u32[]{:S(2)}, u32[]{:S(2)}) collective-permute-start(f32[3,16,768]{2,1,0:T(8,128)} %get-tuple-element.42), channel_id=1, source_target_pairs={{0,3},{1,0},{2,1},{3,2},{4,7},{5,4},{6,5},{7,6},{8,11},{9,8},{10,9... | collective-permute-start | bytes 442376 | tf_op jit(solution)/shard_map/ppermute | solution.py:504
  140.2 0.4 collective-permute-done.12.b_ref
  140.7 2.6 %collective-permute-done.13.c_ref = f32[3,16,768]{2,1,0:T(8,128)S(1)} collective-permute-done((f32[3,16,768]{2,1,0:T(8,128)}, f32[3,16,768]{2,1,0:T(8,128)S(1)}, u32[]{:S(2)}, u32[]{:S(2)}) %collective-permute-start.13) | collective-permute-done | bytes 147488 | tf_op jit(solution)/shard_map/ppermute | solution.py:504
  143.2 3.5 %collective-permute-done.14.d_ref = f32[3,16,768]{2,1,0:T(8,128)S(1)} collective-permute-done((f32[3,16,768]{2,1,0:T(8,128)}, f32[3,16,768]{2,1,0:T(8,128)S(1)}, u32[]{:S(2)}, u32[]{:S(2)}) %collective-permute-start.14) | collective-permute-done | bytes 147488 | tf_op jit(solution)/shard_map/ppermute | solution.py:504
  146.7 0.9 copy-done.1
  147.6 0.7 shard_map.194
  148.3 21.6 %all-to-all-done.1.back_ref = bf16[128,48,128]{2,1,0:T(8,128)(2,1)S(1)} async-done(((bf16[128,48,128]{2,1,0:T(8,128)(2,1)}), bf16[128,48,128]{2,1,0:T(8,128)(2,1)S(1)}, u32[]{:S(2)}, u32[]{:S(2)}) %all-to-all-start.1) | async-done | bytes 1572896 | tf_op jit(solution)/shard_map/all_to_all | solution.py:487
  169.9 1.6 shard_map.193
  (14 shorter events, 0.1 us)
Async XLA Ops:
  4.6 94.2 %all-to-all-start = ((bf16[128,96,128]{2,1,0:T(8,128)(2,1)}), bf16[128,96,128]{2,1,0:T(8,128)(2,1)S(1)}, u32[]{:S(2)}, u32[]{:S(2)}) async-start(bf16[128,96,128]{2,1,0:T(8,128)(2,1)} %shard_map.189), calls=%async_computation | async-start | bytes 6291456 | tf_op jit(solution)/shard_map/all_to_all | solution.py:413
  22.0 22.5 %collective-permute-start.1 = (bf16[192,2048]{1,0:T(8,128)(2,1)}, bf16[192,2048]{1,0:T(8,128)(2,1)S(1)}, u32[]{:S(2)}, u32[]{:S(2)}) collective-permute-start(bf16[192,2048]{1,0:T(8,128)(2,1)} %bitcast.39), channel_id=1, source_target_pairs={{0,1},{1,2},{2,3},{3,0},{4,5},{5,6},{6,7},{7,4},{8,9},{9,10},{10,1... | collective-permute-start | bytes 2359304 | tf_op jit(solution)/shard_map/ppermute | solution.py:418
  24.4 23.7 %collective-permute-start = (bf16[192,2048]{1,0:T(8,128)(2,1)}, bf16[192,2048]{1,0:T(8,128)(2,1)S(1)}, u32[]{:S(2)}, u32[]{:S(2)}) collective-permute-start(bf16[192,2048]{1,0:T(8,128)(2,1)} %bitcast.40), channel_id=1, source_target_pairs={{0,3},{1,0},{2,1},{3,2},{4,7},{5,4},{6,5},{7,6},{8,11},{9,8},{10,9... | collective-permute-start | bytes 2359304 | tf_op jit(solution)/shard_map/ppermute | solution.py:419
  27.8 33.5 %collective-permute-start.5 = (bf16[192,2048]{1,0:T(8,128)(2,1)}, bf16[192,2048]{1,0:T(8,128)(2,1)S(1)}, u32[]{:S(2)}, u32[]{:S(2)}) collective-permute-start(bf16[192,2048]{1,0:T(8,128)(2,1)} %bitcast.42), channel_id=1, source_target_pairs={{0,1},{1,2},{2,3},{3,0},{4,5},{5,6},{6,7},{7,4},{8,9},{9,10},{10,1... | collective-permute-start | bytes 2359304 | tf_op jit(solution)/shard_map/ppermute | solution.py:418
  31.4 33.5 %collective-permute-start.4 = (bf16[192,2048]{1,0:T(8,128)(2,1)}, bf16[192,2048]{1,0:T(8,128)(2,1)S(1)}, u32[]{:S(2)}, u32[]{:S(2)}) collective-permute-start(bf16[192,2048]{1,0:T(8,128)(2,1)} %bitcast.43), channel_id=1, source_target_pairs={{0,3},{1,0},{2,1},{3,2},{4,7},{5,4},{6,5},{7,6},{8,11},{9,8},{10,9... | collective-permute-start | bytes 2359304 | tf_op jit(solution)/shard_map/ppermute | solution.py:419
  33.7 44.5 %collective-permute-start.9 = (bf16[192,2048]{1,0:T(8,128)(2,1)}, bf16[192,2048]{1,0:T(8,128)(2,1)S(1)}, u32[]{:S(2)}, u32[]{:S(2)}) collective-permute-start(bf16[192,2048]{1,0:T(8,128)(2,1)} %bitcast.45), channel_id=1, source_target_pairs={{0,1},{1,2},{2,3},{3,0},{4,5},{5,6},{6,7},{7,4},{8,9},{9,10},{10,1... | collective-permute-start | bytes 2359304 | tf_op jit(solution)/shard_map/ppermute | solution.py:418
  44.5 37.2 %copy-start.3 = (bf16[192,2048]{1,0:T(8,128)(2,1)}, bf16[192,2048]{1,0:T(8,128)(2,1)S(1)}, u32[]{:S(2)}) copy-start(bf16[192,2048]{1,0:T(8,128)(2,1)S(1)} %collective-permute-done.1.refs_2_) | copy-start | bytes 2359300
  44.5 37.3 %collective-permute-start.8 = (bf16[192,2048]{1,0:T(8,128)(2,1)}, bf16[192,2048]{1,0:T(8,128)(2,1)S(1)}, u32[]{:S(2)}, u32[]{:S(2)}) collective-permute-start(bf16[192,2048]{1,0:T(8,128)(2,1)} %bitcast.46), channel_id=1, source_target_pairs={{0,3},{1,0},{2,1},{3,2},{4,7},{5,4},{6,5},{7,6},{8,11},{9,8},{10,9... | collective-permute-start | bytes 2359304 | tf_op jit(solution)/shard_map/ppermute | solution.py:419
  48.1 38.7 %copy-start.4 = (bf16[192,2048]{1,0:T(8,128)(2,1)}, bf16[192,2048]{1,0:T(8,128)(2,1)S(1)}, u32[]{:S(2)}) copy-start(bf16[192,2048]{1,0:T(8,128)(2,1)S(1)} %collective-permute-done.refs_1_) | copy-start | bytes 2359300
  48.1 38.7 %collective-permute-start.2 = (bf16[96,2048]{1,0:T(8,128)(2,1)S(1)}, bf16[96,2048]{1,0:T(8,128)(2,1)S(1)}, u32[]{:S(2)}, u32[]{:S(2)}) collective-permute-start(bf16[96,2048]{1,0:T(8,128)(2,1)S(1)} %slice.24), channel_id=1, source_target_pairs={{0,1},{1,2},{2,3},{3,0},{4,5},{5,6},{6,7},{7,4},{8,9},{9,10},{10,1... | collective-permute-start | bytes 1179656 | tf_op jit(solution)/shard_map/ppermute | solution.py:420
  52.4 37.2 %copy-start.10 = (bf16[1,2048,16]{1,2,0:T(8,128)(2,1)S(1)}, bf16[1,2048,16]{1,2,0:T(8,128)(2,1)}, u32[]{:S(2)}) copy-start(bf16[1,2048,16]{1,2,0:T(8,128)(2,1)} %param.24) | copy-start | bytes 196612
  52.4 37.2 %copy-start.11 = (bf16[1,2048,16]{1,2,0:T(8,128)(2,1)S(1)}, bf16[1,2048,16]{1,2,0:T(8,128)(2,1)}, u32[]{:S(2)}) copy-start(bf16[1,2048,16]{1,2,0:T(8,128)(2,1)} %param.22) | copy-start | bytes 196612
  52.4 37.3 %copy-start.12 = (bf16[1,16,768]{2,1,0:T(8,128)(2,1)S(1)}, bf16[1,16,768]{2,1,0:T(8,128)(2,1)}, u32[]{:S(2)}) copy-start(bf16[1,16,768]{2,1,0:T(8,128)(2,1)} %param.23) | copy-start | bytes 73732
  52.4 37.3 %copy-start.13 = (bf16[1,16,768]{2,1,0:T(8,128)(2,1)S(1)}, bf16[1,16,768]{2,1,0:T(8,128)(2,1)}, u32[]{:S(2)}) copy-start(bf16[1,16,768]{2,1,0:T(8,128)(2,1)} %param.25) | copy-start | bytes 73732
  52.4 37.3 %copy-start.14 = (bf16[1,768,16]{1,2,0:T(8,128)(2,1)S(1)}, bf16[1,768,16]{1,2,0:T(8,128)(2,1)}, u32[]{:S(2)}) copy-start(bf16[1,768,16]{1,2,0:T(8,128)(2,1)} %param.26) | copy-start | bytes 73732
  52.4 46.4 %copy-start.2 = (bf16[1,16,2048]{2,1,0:T(8,128)(2,1)S(1)}, bf16[1,16,2048]{2,1,0:T(8,128)(2,1)}, u32[]{:S(2)}) copy-start(bf16[1,16,2048]{2,1,0:T(8,128)(2,1)} %param.27) | copy-start | bytes 196612
  61.3 28.2 %copy-start.5 = (bf16[192,2048]{1,0:T(8,128)(2,1)}, bf16[192,2048]{1,0:T(8,128)(2,1)S(1)}, u32[]{:S(2)}) copy-start(bf16[192,2048]{1,0:T(8,128)(2,1)S(1)} %collective-permute-done.5.refs_7_) | copy-start | bytes 2359300
  61.4 29.0 %collective-permute-start.3 = (bf16[96,2048]{1,0:T(8,128)(2,1)}, bf16[96,2048]{1,0:T(8,128)(2,1)}, u32[]{:S(2)}, u32[]{:S(2)}) collective-permute-start(bf16[96,2048]{1,0:T(8,128)(2,1)} %slice.25), channel_id=1, source_target_pairs={{0,3},{1,0},{2,1},{3,2},{4,7},{5,4},{6,5},{7,6},{8,11},{9,8},{10,9... | collective-permute-start | bytes 1179656 | tf_op jit(solution)/shard_map/ppermute | solution.py:420
  65.0 24.6 %copy-start.6 = (bf16[192,2048]{1,0:T(8,128)(2,1)}, bf16[192,2048]{1,0:T(8,128)(2,1)S(1)}, u32[]{:S(2)}) copy-start(bf16[192,2048]{1,0:T(8,128)(2,1)S(1)} %collective-permute-done.4.refs_6_) | copy-start | bytes 2359300
  65.0 30.2 %collective-permute-start.6 = (bf16[96,2048]{1,0:T(8,128)(2,1)}, bf16[96,2048]{1,0:T(8,128)(2,1)}, u32[]{:S(2)}, u32[]{:S(2)}) collective-permute-start(bf16[96,2048]{1,0:T(8,128)(2,1)} %slice.26), channel_id=1, source_target_pairs={{0,1},{1,2},{2,3},{3,0},{4,5},{5,6},{6,7},{7,4},{8,9},{9,10},{10,1... | collective-permute-start | bytes 1179656 | tf_op jit(solution)/shard_map/ppermute | solution.py:420
  78.2 11.4 %copy-start.7 = (bf16[192,2048]{1,0:T(8,128)(2,1)}, bf16[192,2048]{1,0:T(8,128)(2,1)S(1)}, u32[]{:S(2)}) copy-start(bf16[192,2048]{1,0:T(8,128)(2,1)S(1)} %collective-permute-done.9.refs_12_) | copy-start | bytes 2359300
  78.2 20.6 %collective-permute-start.7 = (bf16[96,2048]{1,0:T(8,128)(2,1)}, bf16[96,2048]{1,0:T(8,128)(2,1)}, u32[]{:S(2)}, u32[]{:S(2)}) collective-permute-start(bf16[96,2048]{1,0:T(8,128)(2,1)} %slice.27), channel_id=1, source_target_pairs={{0,3},{1,0},{2,1},{3,2},{4,7},{5,4},{6,5},{7,6},{8,11},{9,8},{10,9... | collective-permute-start | bytes 1179656 | tf_op jit(solution)/shard_map/ppermute | solution.py:420
  81.8 7.8 %copy-start.8 = (bf16[192,2048]{1,0:T(8,128)(2,1)}, bf16[192,2048]{1,0:T(8,128)(2,1)S(1)}, u32[]{:S(2)}) copy-start(bf16[192,2048]{1,0:T(8,128)(2,1)S(1)} %collective-permute-done.8.refs_11_) | copy-start | bytes 2359300
  81.8 24.4 %collective-permute-start.10 = (bf16[96,2048]{1,0:T(8,128)(2,1)}, bf16[96,2048]{1,0:T(8,128)(2,1)}, u32[]{:S(2)}, u32[]{:S(2)}) collective-permute-start(bf16[96,2048]{1,0:T(8,128)(2,1)} %slice.28), channel_id=1, source_target_pairs={{0,1},{1,2},{2,3},{3,0},{4,5},{5,6},{6,7},{7,4},{8,9},{9,10},{10,1... | collective-permute-start | bytes 1179656 | tf_op jit(solution)/shard_map/ppermute | solution.py:420
  86.8 2.8 %copy-start.9 = (bf16[96,2048]{1,0:T(8,128)(2,1)}, bf16[96,2048]{1,0:T(8,128)(2,1)S(1)}, u32[]{:S(2)}) copy-start(bf16[96,2048]{1,0:T(8,128)(2,1)S(1)} %collective-permute-done.2.refs_3_) | copy-start | bytes 1179652
  86.8 19.4 %collective-permute-start.11 = (bf16[96,2048]{1,0:T(8,128)(2,1)}, bf16[96,2048]{1,0:T(8,128)(2,1)}, u32[]{:S(2)}, u32[]{:S(2)}) collective-permute-start(bf16[96,2048]{1,0:T(8,128)(2,1)} %slice.29), channel_id=1, source_target_pairs={{0,3},{1,0},{2,1},{3,2},{4,7},{5,4},{6,5},{7,6},{8,11},{9,8},{10,9... | collective-permute-start | bytes 1179656 | tf_op jit(solution)/shard_map/ppermute | solution.py:420
  89.8 16.4 %copy-start = (bf16[3,16,768]{2,1,0:T(8,128)(2,1)}, bf16[3,16,768]{2,1,0:T(8,128)(2,1)S(1)}, u32[]{:S(2)}) copy-start(bf16[3,16,768]{2,1,0:T(8,128)(2,1)S(1)} %fusion.2.refs_15_.refs_3_.right_ref) | copy-start | bytes 221188
  113.6 56.3 %all-to-all-start.1 = ((bf16[128,48,128]{2,1,0:T(8,128)(2,1)}), bf16[128,48,128]{2,1,0:T(8,128)(2,1)S(1)}, u32[]{:S(2)}, u32[]{:S(2)}) async-start(bf16[128,48,128]{2,1,0:T(8,128)(2,1)} %get-tuple-element.34), calls=%async_computation.1 | async-start | bytes 3145728 | tf_op jit(solution)/shard_map/all_to_all | solution.py:487
  131.8 8.8 %collective-permute-start.12 = (f32[3,16,768]{2,1,0:T(8,128)}, f32[3,16,768]{2,1,0:T(8,128)S(1)}, u32[]{:S(2)}, u32[]{:S(2)}) collective-permute-start(f32[3,16,768]{2,1,0:T(8,128)} %get-tuple-element.40), channel_id=1, source_target_pairs={{0,1},{1,2},{2,3},{3,0},{4,5},{5,6},{6,7},{7,4},{8,9},{9,10},{10,1... | collective-permute-start | bytes 442376 | tf_op jit(solution)/shard_map/ppermute | solution.py:504
  134.0 9.2 %collective-permute-start.13 = (f32[3,16,768]{2,1,0:T(8,128)}, f32[3,16,768]{2,1,0:T(8,128)S(1)}, u32[]{:S(2)}, u32[]{:S(2)}) collective-permute-start(f32[3,16,768]{2,1,0:T(8,128)} %get-tuple-element.41), channel_id=1, source_target_pairs={{0,2},{1,3},{2,0},{3,1},{4,6},{5,7},{6,4},{7,5},{8,10},{9,11},{10,... | collective-permute-start | bytes 442376 | tf_op jit(solution)/shard_map/ppermute | solution.py:504
  138.1 8.6 %collective-permute-start.14 = (f32[3,16,768]{2,1,0:T(8,128)}, f32[3,16,768]{2,1,0:T(8,128)S(1)}, u32[]{:S(2)}, u32[]{:S(2)}) collective-permute-start(f32[3,16,768]{2,1,0:T(8,128)} %get-tuple-element.42), channel_id=1, source_target_pairs={{0,3},{1,0},{2,1},{3,2},{4,7},{5,4},{6,5},{7,6},{8,11},{9,8},{10,9... | collective-permute-start | bytes 442376 | tf_op jit(solution)/shard_map/ppermute | solution.py:504
  146.7 0.9 copy-start.1
